TPU v7x, 128 devices: a whole 4x4x4 slice. The times are simulated.
128 devices in a mesh: row: 16 (over y, x), col: 8 (over z, core).
Axes of the slice: x: 4, y: 4, z: 4, core: 2. Of those that a mesh axis runs over, the one named last changes fastest.
Arguments:
- white_noise: float32 [8192, 8192], P('row', 'col'), may hold values from -6 to 6
- amplitude: float32 [8192, 8192], P(('row', 'col')), may hold values from 0.3 to 3
- state_prev: float32 [8192, 8192], P('row', 'col'), may hold values from -6 to 6
- catch_id: int32 [64, 64], P('row', 'col'), may hold values from 0 to 2047
- owner_map: int32 [2048, 1], replicated, may hold values from 0 to 127; in each aligned block of 2048 rows (0 to 2047, 2048 to 4095, ...) at most 32 rows name the same one
- unit_graph: float32 [288, 4096], P(None, ('row', 'col')), may hold values from 0.05 to 0.5
- queue_prev: float32 [288, 4096], P(None, ('row', 'col')), may hold values from -6 to 6
Outputs:
- state_new: float32 [8192, 8192], P('row', 'col')
- flow_queue: float32 [288, 4096], P(None, ('row', 'col'))
Inputs may be any that keep to these rules, and one draw needn't show every extreme that they name: `owner_map`: each device owns at most 32 catchments, and some device owns exactly 32.
All inputs are finite; a program needn't handle non-finite values.
Results may differ from a plain program's by a relative error of at most 0.000088.
Values sent between devices are 32-bit elements; how exact they have to be, the bound alone decides.
No kernel may reach another device: no remote copies, remote signals or barrier semaphores. Data moves between devices by JAX's collectives and lax.ppermute only.
A program may use at most 128 MiB of HBM per device.

v0:
```python
from functools import partial

import jax
import jax.numpy as jnp
import ml_dtypes
import numpy as np
from jax import lax
from jax.experimental import pallas as pl
from jax.experimental.pallas import tpu as pltpu
from jax.sharding import PartitionSpec as P

TILE = 128
CAP = 32
N = 8192
DEV = 128
HALF = 32
BOTH = ("row", "col")

bump_height = 64.0
persist = 0.8
innovate = 0.6
log_mean = -0.3
log_scale = 0.6

BF = jnp.bfloat16
F32 = jnp.float32


def hi_lo(table):
    table = np.asarray(table, np.float64)
    hi = table.astype(ml_dtypes.bfloat16)
    lo = (table - hi.astype(np.float64)).astype(ml_dtypes.bfloat16)
    return np.concatenate([hi, lo], axis=1)


def angle(left, right, length):
    return 2.0 * np.pi / length * (np.outer(left, right) % length)


def real_forward():
    turn = angle(np.arange(64), np.arange(64), 64)
    table = np.concatenate([np.cos(turn[:33]), -np.sin(turn[1:32])], axis=0)
    return hi_lo(np.kron(table, np.eye(8)))


def real_inverse():
    turn = angle(np.arange(64), np.arange(64), 64)
    real = 2.0 * np.cos(turn[:, :33])
    real[:, 0] = 1.0
    table = np.concatenate([real, -2.0 * np.sin(turn[:, 1:32])], axis=1)
    return hi_lo(np.kron(table, np.eye(8)))


def row_twiddle():
    turn = angle(np.arange(33), np.arange(128), N)
    return np.concatenate([np.cos(turn), np.sin(turn)], axis=1).astype(np.float32)


def row_forward():
    turn = angle(np.arange(128), np.arange(128), 128)
    cos, sin = np.cos(turn), np.sin(turn)
    whole = np.block([[cos, sin], [-sin, cos]])
    low = (np.arange(128) < 64).astype(np.float64)[:, None]
    first = np.block([[cos * low, sin * low], [-sin * low, cos * low]])
    imag = -sin * (1 - low)
    imag[64] = 1.0
    last = np.concatenate([cos * (1 - low), imag], axis=0)
    return hi_lo(whole), hi_lo(np.concatenate([whole, first, last], axis=1))


def row_inverse():
    turn = angle(np.arange(128), np.arange(128), 128)
    cos, sin = np.cos(turn), np.sin(turn)
    whole = np.block([[cos, sin], [-sin, cos]])
    low = (np.arange(128) < 64).astype(np.float64)[:, None]
    first = np.block([[cos * low, sin * low], [-sin * low, cos * low]])
    top, bottom = 2.0 * cos * (1 - low), -2.0 * sin * (1 - low)
    top[64] = cos[64]
    bottom[64] = 1.0
    last = np.concatenate([top, bottom], axis=0)
    both = np.concatenate([first, last], axis=1)
    return hi_lo(whole), hi_lo(both)


def col_tables(sign):
    turn = angle(np.arange(128), np.arange(128), 128)
    cos, sin = np.cos(turn), sign * np.sin(turn)
    long = np.block([[cos, -sin], [sin, cos]])
    turn = angle(np.arange(64), np.arange(64), 64)
    cos, sin = np.kron(np.eye(2), np.cos(turn)), np.kron(np.eye(2), sign * np.sin(turn))
    short = np.block([[cos, sin], [-sin, cos]])
    return hi_lo(long), hi_lo(short)


def col_twiddle():
    turn = angle(np.arange(128), np.arange(128) % 64, N)
    return np.concatenate([np.cos(turn), np.sin(turn)], axis=1).astype(np.float32)


def split(value):
    hi = value.astype(BF)
    return hi, (value - hi.astype(F32)).astype(BF)


def dot(left, right, dims=((1,), (0,))):
    return lax.dot_general(left, right, (dims, ((), ())), preferred_element_type=F32)


def times_table(value, table, depth):
    hi, lo = split(value)
    t_hi, t_lo = table[:depth, :], table[depth:, :]
    return dot(hi, t_hi) + dot(lo, t_hi) + dot(hi, t_lo)


def table_times(table, value, dims=((1,), (0,))):
    depth = table.shape[1] // 2
    hi, lo = split(value)
    t_hi, t_lo = table[:, :depth], table[:, depth:]
    return dot(t_hi, hi, dims) + dot(t_hi, lo, dims) + dot(t_lo, hi, dims)


def call(body, out, scratch=(), limit=24, flops=2_000_000_000, bytes_accessed=6_000_000):
    return pl.pallas_call(
        body,
        out_shape=out,
        scratch_shapes=list(scratch),
        compiler_params=pltpu.CompilerParams(vmem_limit_bytes=limit << 20),
        cost_estimate=pl.CostEstimate(flops=flops, bytes_accessed=bytes_accessed, transcendentals=0),
    )


def forward_rows(x_ref, wide_ref, tw_ref, whole_ref, tail_ref, out_ref, mid):
    def groups(step, carry):
        base = pl.multiple_of(step * 16, 16)
        left = [x_ref[c, pl.ds(base, 8), h * 128 : h * 128 + 128] for c in range(8) for h in range(8)]
        right = [x_ref[c, pl.ds(base + 8, 8), h * 128 : h * 128 + 128] for c in range(8) for h in range(8)]
        block = jnp.concatenate([jnp.concatenate(left, axis=0), jnp.concatenate(right, axis=0)], axis=1)
        spec = table_times(wide_ref, block)
        for p in range(33):
            cos, sin = tw_ref[p : p + 1, :128], tw_ref[p : p + 1, 128:]
            for g in range(2):
                lanes = slice(g * 128, g * 128 + 128)
                rows = pl.ds(p * 64 + base + g * 8, 8)
                real = spec[p * 8 : p * 8 + 8, lanes]
                if p == 0:
                    mid[rows, :128] = real
                    continue
                if p == 32:
                    mid[rows, :128] = real * cos
                    mid[rows, 128:] = -(real * sin)
                    continue
                imag = spec[(32 + p) * 8 : (32 + p) * 8 + 8, lanes]
                mid[rows, :128] = real * cos + imag * sin
                mid[rows, 128:] = imag * cos - real * sin
        return carry

    lax.fori_loop(0, 4, groups, 0)

    def store(t, value):
        for u in range(2):
            lanes = slice(u * 128, u * 128 + 128)
            out_ref[pl.ds(2 * t + u, 128, stride=32), :] = value[:128, lanes]
            out_ref[pl.ds(16 + 2 * t + u, 128, stride=32), :] = value[128:, lanes]

    for t in range(7):
        rows = mid[(4 * t + 1) * 64 : (4 * t + 5) * 64, :]
        store(t, table_times(whole_ref, rows, ((1,), (1,))))
    plain = jnp.concatenate(
        [mid[29 * 64 : 32 * 64, :], jnp.zeros((192, 384), F32)], axis=1
    )
    mixed = jnp.concatenate(
        [jnp.zeros((64, 256), F32), mid[32 * 64 : 33 * 64, :], mid[0:64, :128]], axis=1
    )
    store(7, table_times(tail_ref, jnp.concatenate([plain, mixed], axis=0), ((1,), (1,))))


def columns(x_ref, w_ref, tw_ref, long_ref, short_ref, ilong_ref, ishort_ref, out_ref):
    cos, sin = tw_ref[:, :128], tw_ref[:, 128:]

    def back(real, imag):
        joint = jnp.concatenate([real, imag], axis=1)
        mixed = times_table(joint, ishort_ref, 256)
        real, imag = mixed[:, :128], mixed[:, 128:]
        return real * cos - imag * sin, imag * cos + real * sin

    def last(real, imag):
        return table_times(ilong_ref, jnp.concatenate([real, imag], axis=0))

    def pair(t, extra):
        blocks = [2 * t, 2 * t + 1]
        real = jnp.concatenate([x_ref[pl.ds(b, 128, stride=32), :] for b in blocks], axis=1)
        imag = jnp.concatenate([x_ref[pl.ds(16 + b, 128, stride=32), :] for b in blocks], axis=1)
        mid = table_times(long_ref, jnp.concatenate([real, imag], axis=0))
        reals, imags = [], []
        tail = None
        for u, b in enumerate(blocks):
            lanes = slice(u * 128, u * 128 + 128)
            real, imag = mid[:128, lanes], mid[128:, lanes]
            joint = jnp.concatenate([real * cos + imag * sin, imag * cos - real * sin], axis=1)
            spec = times_table(joint, short_ref, 256)
            if extra and u == 1:
                weight = w_ref[16]
                tail = back(spec[:, :128] * weight, spec[:, 128:] * weight)
            weight = w_ref[b]
            real, imag = back(spec[:, :128] * weight, spec[:, 128:] * weight)
            reals.append(real)
            imags.append(imag)
        done = last(jnp.concatenate(reals, axis=1), jnp.concatenate(imags, axis=1))
        for u, b in enumerate(blocks):
            lanes = slice(u * 128, u * 128 + 128)
            out_ref[pl.ds(b, 128, stride=32), :] = done[:128, lanes]
            out_ref[pl.ds(16 + b, 128, stride=32), :] = done[128:, lanes]
        if extra:
            done = last(*tail)
            out_ref[pl.ds(31, 128, stride=32), :] = done[128:, :]

    def step(t, carry):
        pair(t, False)
        return carry

    lax.fori_loop(0, 7, step, 0)
    pair(7, True)


def inverse_rows(x_ref, wide_ref, tw_ref, whole_ref, tail_ref, out_ref, mid):
    def product(blocks, tables):
        real = jnp.concatenate([x_ref[pl.ds(b, 128, stride=32), :] for b in blocks], axis=1)
        imag = jnp.concatenate([x_ref[pl.ds(16 + b, 128, stride=32), :] for b in blocks], axis=1)
        joint = jnp.concatenate([real, imag], axis=0).T
        return [table_right(joint, table) for table in tables]

    def table_right(joint, table):
        half = table.shape[1] // 2
        hi, lo = split(joint)
        t_hi, t_lo = table[:, :half], table[:, half:]
        return dot(hi, t_hi) + dot(lo, t_hi) + dot(hi, t_lo)

    def place(p, value):
        cos, sin = tw_ref[p : p + 1, :128], tw_ref[p : p + 1, 128:]
        real, imag = value[:, :128], value[:, 128:256]
        mid[p * 64 : p * 64 + 64, :] = real * cos - imag * sin
        if p < 32:
            mid[(32 + p) * 64 : (33 + p) * 64, :] = imag * cos + real * sin

    for t in range(8):
        tables = [whole_ref] if t < 7 else [whole_ref, tail_ref]
        results = product([2 * t, 2 * t + 1], tables)
        for k in range(4):
            slot = 4 * t + k
            if slot < 31:
                place(slot + 1, results[0][k * 64 : k * 64 + 64, :])
            else:
                value = results[1][k * 64 : k * 64 + 64, :]
                place(32, value)
                mid[0:64, :] = value[:, 256:]

    def groups(step, carry):
        base = pl.multiple_of(step * 16, 16)
        left = [mid[pl.ds(pp * 64 + base, 8), :] for pp in range(64)]
        right = [mid[pl.ds(pp * 64 + base + 8, 8), :] for pp in range(64)]
        block = jnp.concatenate([jnp.concatenate(left, axis=0), jnp.concatenate(right, axis=0)], axis=1)
        field = table_times(wide_ref, block)
        for c in range(8):
            for h in range(8):
                row = (c * 8 + h) * 8
                for g in range(2):
                    out_ref[c, pl.ds(base + g * 8, 8), h * 128 : h * 128 + 128] = field[
                        row : row + 8, g * 128 : g * 128 + 128
                    ]
        return carry

    lax.fori_loop(0, 4, groups, 0)


def reversal():
    flip = np.zeros((128, 128), np.float32)
    for k in range(1, 128):
        flip[k, 128 - k] = 1.0
    first = np.zeros((128, 128), np.float32)
    first[0, 0] = 1.0
    return np.concatenate([flip, first], axis=1).astype(ml_dtypes.bfloat16)


def weights(d_ref, amp_ref, mir_ref, row_ref, flip_ref, out_ref, own, rev, zero):
    d = d_ref[0]
    low = d < 64
    middle = d == 64

    def fill(kb):
        lanes = slice(kb * 128, kb * 128 + 128)
        return amp_ref[:, lanes], mir_ref[:, lanes], row_ref[0:1, lanes]

    for kb in range(64):
        amp, mir, row = fill(kb)
        own_tail = jnp.where(low, amp[32:33], amp[0:1])
        mir_tail = jnp.where(low, mir[0:1], jnp.where(middle, amp[0:1], row))
        flipped = [mir[31 - s : 32 - s] for s in range(31)]
        own_rows = jnp.concatenate(
            [amp[1:32], own_tail, jnp.where(middle, row, own_tail)], axis=0
        )
        mir_rows = jnp.concatenate(flipped + [mir_tail, jnp.where(middle, row, mir_tail)], axis=0)
        own[pl.ds(kb, 33, stride=64), :] = own_rows
        rev[pl.ds(63 - kb, 33, stride=64), :] = mir_rows
        zero[pl.ds((64 - kb) % 64, 33, stride=64), :] = mir_rows

    ka = lax.broadcasted_iota(jnp.int32, (128, 128), 0)
    lane = lax.broadcasted_iota(jnp.int32, (128, 128), 1)
    k0 = ka + 128 * (lane % 64)
    f0 = jnp.where(k0 < N // 2, k0, k0 - N).astype(F32)
    flip, first = flip_ref[:, :128], flip_ref[:, 128:]

    def exact(table, rows):
        a = rows.astype(BF)
        rest = rows - a.astype(F32)
        b = rest.astype(BF)
        c = (rest - b.astype(F32)).astype(BF)
        dims = ((1,), (1,))
        return dot(table, a, dims) + dot(table, b, dims) + dot(table, c, dims)

    def weight(own_rows, rev_rows, zero_rows, p):
        k1 = d * 64 + p
        f1 = jnp.where(k1 < N // 2, k1, k1 - N).astype(F32)
        width_sq = float((N // 128) * (N // 128))
        envelope = 1.0 + bump_height / (1.0 + (f0 * f0 + f1 * f1) / width_sq)
        both = own_rows.T + exact(flip, rev_rows) + exact(first, zero_rows)
        return both * (envelope * (0.5 / (N * N)))

    def step(b, carry):
        rows = pl.ds(pl.multiple_of(b * 128, 128), 128)
        slot = 2 * b + lane // 64
        p = jnp.where(slot < 31, slot + 1, jnp.where(low, 32, 0))
        out_ref[b] = weight(own[rows, :], rev[rows, :], zero[rows, :], p)
        return carry

    lax.fori_loop(0, 16, step, 0)
    upper = slice(31 * 64, 33 * 64)
    p = jnp.where(low, 32, jnp.where(middle, -64 * 64, 0))
    p = jnp.where(lane < 64, jnp.where(low, 32, 0), p)
    value = weight(own[upper, :], rev[upper, :], zero[upper, :], p)
    out_ref[16] = jnp.where(lane < 64, out_ref[15], value)


def catchment_rows(catch_id, owner_map, devices):
    owners = owner_map[:, 0]
    hits = (owners[:, None] == jnp.arange(devices, dtype=jnp.int32)[None, :]).astype(jnp.int32)
    ranks = jnp.sum(hits * (jnp.cumsum(hits, axis=0) - 1), axis=1)
    slot = owners * CAP + ranks
    matches = catch_id.reshape(-1)[:, None] == jnp.arange(owners.shape[0], dtype=jnp.int32)[None, :]
    return jnp.sum(jnp.where(matches, slot[None, :], 0), axis=1)


def shards(white_noise, amplitude, state_prev, catch_id, owner_map, unit_graph, queue_prev):
    d = lax.axis_index(BOTH)
    flat = jax.ShapeDtypeStruct((DEV * 32, 128), F32)
    slab = lax.all_to_all(white_noise.reshape(8, 64, 1024), "col", 0, 0, tiled=True)
    mirrored = lax.ppermute(amplitude[32:64], BOTH, [(i, DEV - 1 - i) for i in range(DEV)])
    partner = lax.ppermute(
        amplitude[0:1], BOTH, [(0, 64)] + [(i, DEV - i) for i in range(1, 64)]
    )
    weight = pl.pallas_call(
        weights,
        out_shape=jax.ShapeDtypeStruct((17, 128, 128), F32),
        in_specs=[pl.BlockSpec(memory_space=pltpu.SMEM)] + [pl.BlockSpec(memory_space=pltpu.VMEM)] * 4,
        scratch_shapes=[pltpu.VMEM((33 * 64, 128), F32)] * 3,
        compiler_params=pltpu.CompilerParams(vmem_limit_bytes=24 << 20),
        cost_estimate=pl.CostEstimate(flops=200_000_000, bytes_accessed=6_000_000, transcendentals=0),
    )(d.astype(jnp.int32).reshape(1), amplitude, mirrored, partner, reversal())

    tw_row = row_twiddle()
    whole, tail = row_forward()
    spec = call(forward_rows, flat, [pltpu.VMEM((33 * 64, 256), F32)])(
        slab, real_forward(), tw_row, whole, tail
    )
    spec = lax.all_to_all(spec.reshape(DEV, 32, 128), BOTH, 0, 0, tiled=True)
    long, short = col_tables(-1.0)
    ilong, ishort = col_tables(1.0)
    stack = lambda table: np.concatenate([table[:, :256], table[:, 256:]], axis=0)
    shaped = call(columns, flat)(
        spec.reshape(DEV * 32, 128), weight, col_twiddle(), long, stack(short), ilong, stack(ishort)
    )
    shaped = lax.all_to_all(shaped.reshape(DEV, 32, 128), BOTH, 0, 0, tiled=True)
    whole, tail = row_inverse()
    field = call(
        inverse_rows, jax.ShapeDtypeStruct((8, 64, 1024), F32), [pltpu.VMEM((64 * 64, 128), F32)]
    )(shaped.reshape(DEV * 32, 128), real_inverse(), tw_row, whole, tail)
    filtered = lax.all_to_all(field, "col", 0, 0, tiled=True).reshape(512, 1024)

    state_new = persist * state_prev + innovate * filtered
    rain = jnp.exp(log_mean + log_scale * state_new)
    tile_rain = rain.reshape(4, TILE, 8, TILE).mean(axis=(1, 3)).reshape(-1)
    tile_slot = catchment_rows(catch_id, owner_map, DEV)
    slot_hits = tile_slot[:, None] == jnp.arange(DEV * CAP, dtype=jnp.int32)[None, :]
    partial_sums = jnp.sum(jnp.where(slot_hits, tile_rain[:, None], 0.0), axis=0)
    received = lax.all_to_all(partial_sums.reshape(DEV, 1, CAP), BOTH, 0, 0, tiled=True)
    slot_rain = received.sum(axis=(0, 1))
    shifted = jnp.concatenate(
        [queue_prev[1:], jnp.zeros((1, queue_prev.shape[1]), jnp.float32)], axis=0
    )
    flow_queue = shifted + unit_graph * slot_rain[None, :]
    return (state_new, flow_queue)


def solution(mesh):
    return jax.shard_map(
        shards,
        mesh=mesh,
        in_specs=(
            P("row", "col"),
            P(BOTH, None),
            P("row", "col"),
            P("row", "col"),
            P(),
            P(None, BOTH),
            P(None, BOTH),
        ),
        out_specs=(P("row", "col"), P(None, BOTH)),
        check_vma=False,
    )
```

profile of v0, /device:TPU:1, one launch (start us, length us, event | category | flops | bytes accessed | tf_op | source)
XLA Modules:
  0.0 218.7 jit_solution(5319198599443210288)
XLA Ops:
  0.6 0.0 copy-start.6
  0.7 0.0 copy-start.9
  0.7 0.0 copy-start.16
  0.7 33.4 %all_to_all.25.x_ref = f32[8,64,1024]{2,1,0:T(8,128)S(1)} all-to-all(f32[8,64,1024]{2,1,0:T(8,128)} %bitcast.30), channel_id=1, replica_groups=mesh['row'=16,'col'=8] {'col'}, dimensions={0} | all-to-all | bytes 4194304 | tf_op jit(solution)/shard_map/all_to_all | solution.py:355
  34.1 4.5 %shard_map.203 = f32[4096,128]{1,0:T(8,128)S(1)} custom-call(f32[8,64,1024]{2,1,0:T(8,128)S(1)} %all_to_all.25.x_ref, bf16[512,1024]{1,0:T(8,128)(2,1)S(1)} %copy-done.6, f32[33,256]{1,0:T(8,128)S(1)} %copy-done.16, bf16[256,512]{1,0:T(8,128)(2,1)S(1)} %copy-done.9, bf16[256,1280]{1,0:T(8,128)(2,1)S(1)} %copy-done.7), custom_call_target="tpu_custom_call" | custom-call | flops 2000000000 | bytes 6000000 | tf_op jit(solution)/shard_map/pallas_call | solution.py:371
  38.6 1.3 copy-done.1
  40.0 8.6 %all-to-all-start.1 = ((f32[128,32,128]{2,1,0:T(8,128)}), f32[128,32,128]{2,1,0:T(8,128)}, u32[]{:S(2)}, u32[]{:S(2)}) async-start(f32[128,32,128]{2,1,0:T(8,128)} %bitcast.26), calls=%async_computation.1 | async-start | bytes 4194304 | tf_op jit(solution)/shard_map/all_to_all | solution.py:374
  48.5 0.0 copy-start.4
  48.6 1.1 slice.15
  49.6 8.0 %collective-permute-start = (f32[32,8192]{1,0:T(8,128)}, f32[32,8192]{1,0:T(8,128)S(1)}, u32[]{:S(2)}, u32[]{:S(2)}) collective-permute-start(f32[32,8192]{1,0:T(8,128)} %slice.15), channel_id=1, source_target_pairs={{0,127},{1,126},{2,125},{3,124},{4,123},{5,122},{6,121},{7,120},{8... | collective-permute-start | bytes 3145736 | tf_op jit(solution)/shard_map/ppermute | solution.py:356
  57.6 1.9 collective-permute-start.1
  59.5 34.1 %collective-permute-done.1.row_ref = f32[1,8192]{1,0:T(1,128)S(1)} collective-permute-done((f32[1,8192]{1,0:T(1,128)S(1)}, f32[1,8192]{1,0:T(1,128)S(1)}, u32[]{:S(2)}, u32[]{:S(2)}) %collective-permute-start.1) | collective-permute-done | bytes 32800 | tf_op jit(solution)/shard_map/ppermute | solution.py:357
  93.6 7.7 %collective-permute-done.mir_ref = f32[32,8192]{1,0:T(8,128)S(1)} collective-permute-done((f32[32,8192]{1,0:T(8,128)}, f32[32,8192]{1,0:T(8,128)S(1)}, u32[]{:S(2)}, u32[]{:S(2)}) %collective-permute-start) | collective-permute-done | bytes 1048608 | tf_op jit(solution)/shard_map/ppermute | solution.py:356
  101.2 1.0 copy-done.2
  102.2 1.2 copy-done.3
  103.5 7.2 %shard_map.204.w_ref = f32[17,128,128]{2,1,0:T(8,128)S(1)} custom-call(s32[1]{0:T(128)} %bitcast.3.d_ref, f32[64,8192]{1,0:T(8,128)S(1)} %copy-done, f32[32,8192]{1,0:T(8,128)S(1)} %copy-done.3, f32[1,8192]{1,0:T(1,128)S(1)} %collective-permute-done.1.row_ref, bf16[128,256]{1,0:T(8,128)(2,1)S(1)} %copy-done.4), custom_call_target="tpu_custom_call" | custom-call | flops 200000000 | bytes 6000000 | tf_op jit(solution)/shard_map/pallas_call | solution.py:360
  110.7 0.0 copy-start.10
  110.7 0.9 copy-done.10
  111.7 0.9 copy-done.12
  112.6 0.9 copy-done.13
  113.6 0.9 copy-done.14
  114.5 12.6 %shard_map.205 = f32[4096,128]{1,0:T(8,128)S(1)} custom-call(f32[4096,128]{1,0:T(8,128)} %bitcast.2.x_ref, f32[17,128,128]{2,1,0:T(8,128)S(1)} %shard_map.204.w_ref, f32[128,256]{1,0:T(8,128)S(1)} %copy-done.15, bf16[256,512]{1,0:T(8,128)(2,1)S(1)} %copy-done.10, bf16[512,256]{1,0:T(8,128)(2,1)S(1)} %copy-done.12, bf16[256,512]{1,0:T(8,128)(2,1)S(1)} %copy-done.13, ...), custom_call_target="tpu_custom_call" | custom-call | flops 2000000000 | bytes 6000000 | tf_op jit(solution)/shard_map/pallas_call | solution.py:378
  127.2 0.0 copy-start.5
  127.2 34.5 %all_to_all.26 = f32[128,32,128]{2,1,0:T(8,128)S(1)} all-to-all(f32[128,32,128]{2,1,0:T(8,128)S(1)} %bitcast.27), channel_id=1, replica_groups=mesh['row'=16,'col'=8] {'row','col'}, dimensions={0} | all-to-all | bytes 4194304 | tf_op jit(solution)/shard_map/all_to_all | solution.py:381
  161.7 5.7 %shard_map.206 = f32[8,64,1024]{2,1,0:T(8,128)} custom-call(f32[4096,128]{1,0:T(8,128)S(1)} %bitcast.28, bf16[512,1024]{1,0:T(8,128)(2,1)S(1)} %copy-done.5, f32[33,256]{1,0:T(8,128)S(1)} %copy-done.16, bf16[256,512]{1,0:T(8,128)(2,1)S(1)} %copy-done.11, bf16[256,768]{1,0:T(8,128)(2,1)S(1)} %copy-done.8), custom_call_target="tpu_custom_call" | custom-call | flops 2000000000 | bytes 6000000 | tf_op jit(solution)/shard_map/pallas_call | solution.py:383
  167.4 4.9 %all-to-all-start.3 = ((f32[8,64,1024]{2,1,0:T(8,128)}), f32[8,64,1024]{2,1,0:T(8,128)S(1)}, u32[]{:S(2)}, u32[]{:S(2)}) async-start(f32[8,64,1024]{2,1,0:T(8,128)} %shard_map.206), calls=%async_computation.3 | async-start | bytes 4194304 | tf_op jit(solution)/shard_map/all_to_all | solution.py:386
  172.3 0.1 copy.28
  172.4 0.3 fusion.1
  172.8 0.1 add_add_fusion
  172.9 0.3 copy.29
  173.2 0.2 copy-done.21
  173.5 0.1 eq.51
  173.6 0.6 fusion
  174.2 0.2 select_reduce_fusion.1
  174.4 24.2 %all-to-all-done.3 = f32[8,64,1024]{2,1,0:T(8,128)S(1)} async-done(((f32[8,64,1024]{2,1,0:T(8,128)}), f32[8,64,1024]{2,1,0:T(8,128)S(1)}, u32[]{:S(2)}, u32[]{:S(2)}) %all-to-all-start.3) | async-done | bytes 2097184 | tf_op jit(solution)/shard_map/all_to_all | solution.py:386
  198.7 0.4 broadcast_multiply_fusion
  199.1 1.2 copy-done.17
  200.3 2.1 exponential_bitcast_fusion
  202.4 0.5 copy.31
  202.9 0.3 bitcast_reduce_fusion
  203.2 0.1 div.10
  203.2 0.1 select_reduce_fusion
  203.4 0.7 reshape.75
  204.1 4.2 %all-to-all-start.4 = ((f32[128,1,32]{2,1,0:T(1,128)}), f32[128,1,32]{2,1,0:T(1,128)S(1)}, u32[]{:S(2)}, u32[]{:S(2)}) async-start(f32[128,1,32]{2,1,0:T(1,128)} %bitcast.12), calls=%async_computation.4 | async-start | bytes 131072 | tf_op jit(solution)/shard_map/all_to_all | solution.py:394
  208.3 0.1 slice.17
  208.4 9.5 %all-to-all-done.4 = f32[128,1,32]{2,1,0:T(1,128)S(1)} async-done(((f32[128,1,32]{2,1,0:T(1,128)}), f32[128,1,32]{2,1,0:T(1,128)S(1)}, u32[]{:S(2)}, u32[]{:S(2)}) %all-to-all-start.4) | async-done | bytes 16416 | tf_op jit(solution)/shard_map/all_to_all | solution.py:394
  217.9 0.2 reduce_sum.49
  218.0 0.7 multiply_add_fusion
  (36 shorter events, 0.1 us)
Async XLA Ops:
  0.6 33.5 %copy-start.6 = (bf16[512,1024]{1,0:T(8,128)(2,1)S(1)}, bf16[512,1024]{1,0:T(8,128)(2,1)}, u32[]{:S(2)}) copy-start(bf16[512,1024]{1,0:T(8,128)(2,1)} %constant.57.clone.wide_ref) | copy-start | bytes 3145732
  0.6 33.5 %copy-start.7 = (bf16[256,1280]{1,0:T(8,128)(2,1)S(1)}, bf16[256,1280]{1,0:T(8,128)(2,1)}, u32[]{:S(2)}) copy-start(bf16[256,1280]{1,0:T(8,128)(2,1)} %constant.60.clone.tail_ref) | copy-start | bytes 1966084
  0.7 33.5 %copy-start.9 = (bf16[256,512]{1,0:T(8,128)(2,1)S(1)}, bf16[256,512]{1,0:T(8,128)(2,1)}, u32[]{:S(2)}) copy-start(bf16[256,512]{1,0:T(8,128)(2,1)} %constant.59.clone.whole_ref.long_ref) | copy-start | bytes 786436
  0.7 33.5 %copy-start.16 = (f32[33,256]{1,0:T(8,128)S(1)}, f32[33,256]{1,0:T(8,128)}, u32[]{:S(2)}) copy-start(f32[33,256]{1,0:T(8,128)} %constant.58.clone.tw_ref) | copy-start | bytes 101380
  38.6 1.3 copy-start.1
  40.0 8.6 %copy-start = (f32[64,8192]{1,0:T(8,128)S(1)}, f32[64,8192]{1,0:T(8,128)}, u32[]{:S(2)}) copy-start(f32[64,8192]{1,0:T(8,128)} %amp_ref.1) | copy-start | bytes 6291460
  40.0 70.7 %all-to-all-start.1 = ((f32[128,32,128]{2,1,0:T(8,128)}), f32[128,32,128]{2,1,0:T(8,128)}, u32[]{:S(2)}, u32[]{:S(2)}) async-start(f32[128,32,128]{2,1,0:T(8,128)} %bitcast.26), calls=%async_computation.1 | async-start | bytes 4194304 | tf_op jit(solution)/shard_map/all_to_all | solution.py:374
  48.5 53.7 %copy-start.4 = (bf16[128,256]{1,0:T(8,128)(2,1)S(1)}, bf16[128,256]{1,0:T(8,128)(2,1)}, u32[]{:S(2)}) copy-start(bf16[128,256]{1,0:T(8,128)(2,1)} %constant.56.clone.flip_ref) | copy-start | bytes 196612
  49.6 51.6 %collective-permute-start = (f32[32,8192]{1,0:T(8,128)}, f32[32,8192]{1,0:T(8,128)S(1)}, u32[]{:S(2)}, u32[]{:S(2)}) collective-permute-start(f32[32,8192]{1,0:T(8,128)} %slice.15), channel_id=1, source_target_pairs={{0,127},{1,126},{2,125},{3,124},{4,123},{5,122},{6,121},{7,120},{8... | collective-permute-start | bytes 3145736 | tf_op jit(solution)/shard_map/ppermute | solution.py:356
  57.6 36.0 %collective-permute-start.1 = (f32[1,8192]{1,0:T(1,128)S(1)}, f32[1,8192]{1,0:T(1,128)S(1)}, u32[]{:S(2)}, u32[]{:S(2)}) collective-permute-start(f32[1,8192]{1,0:T(1,128)S(1)} %slice.16), channel_id=1, source_target_pairs={{0,64},{1,127},{2,126},{3,125},{4,124},{5,123},{6,122},{7,121},{8,... | collective-permute-start | bytes 98312 | tf_op jit(solution)/shard_map/ppermute | solution.py:357
  101.2 1.0 copy-start.2
  102.2 1.2 copy-start.3
  103.5 7.3 %copy-start.15 = (f32[128,256]{1,0:T(8,128)S(1)}, f32[128,256]{1,0:T(8,128)}, u32[]{:S(2)}) copy-start(f32[128,256]{1,0:T(8,128)} %constant.61.clone.tw_ref) | copy-start | bytes 393220
  110.7 1.0 copy-start.10
  111.7 0.9 copy-start.12
  112.6 0.9 copy-start.13
  113.6 0.9 copy-start.14
  127.2 34.5 %copy-start.5 = (bf16[512,1024]{1,0:T(8,128)(2,1)S(1)}, bf16[512,1024]{1,0:T(8,128)(2,1)}, u32[]{:S(2)}) copy-start(bf16[512,1024]{1,0:T(8,128)(2,1)} %constant.65.clone.wide_ref) | copy-start | bytes 3145732
  127.2 34.5 %copy-start.8 = (bf16[256,768]{1,0:T(8,128)(2,1)S(1)}, bf16[256,768]{1,0:T(8,128)(2,1)}, u32[]{:S(2)}) copy-start(bf16[256,768]{1,0:T(8,128)(2,1)} %constant.66.clone.tail_ref) | copy-start | bytes 1179652
  127.2 34.5 %copy-start.11 = (bf16[256,512]{1,0:T(8,128)(2,1)S(1)}, bf16[256,512]{1,0:T(8,128)(2,1)}, u32[]{:S(2)}) copy-start(bf16[256,512]{1,0:T(8,128)(2,1)} %constant.59.clone.whole_ref.long_ref) | copy-start | bytes 786436
  167.4 4.9 %copy-start.18 = (s32[2048,1]{0,1:T(1,128)S(1)}, s32[2048,1]{0,1:T(1,128)}, u32[]{:S(2)}) copy-start(s32[2048,1]{0,1:T(1,128)} %param.24) | copy-start | bytes 24580
  167.4 31.3 %all-to-all-start.3 = ((f32[8,64,1024]{2,1,0:T(8,128)}), f32[8,64,1024]{2,1,0:T(8,128)S(1)}, u32[]{:S(2)}, u32[]{:S(2)}) async-start(f32[8,64,1024]{2,1,0:T(8,128)} %shard_map.206), calls=%async_computation.3 | async-start | bytes 4194304 | tf_op jit(solution)/shard_map/all_to_all | solution.py:386
  172.8 0.7 copy-start.21
  198.7 1.6 copy-start.17
  202.9 5.5 %copy-start.19 = (f32[288,32]{0,1:T(8,128)S(1)}, f32[288,32]{0,1:T(8,128)}, u32[]{:S(2)}) copy-start(f32[288,32]{0,1:T(8,128)} %param.26) | copy-start | bytes 110596
  202.9 15.2 %copy-start.20 = (f32[288,32]{0,1:T(8,128)S(1)}, f32[288,32]{0,1:T(8,128)}, u32[]{:S(2)}) copy-start(f32[288,32]{0,1:T(8,128)} %param.25) | copy-start | bytes 110596
  204.1 13.8 %all-to-all-start.4 = ((f32[128,1,32]{2,1,0:T(1,128)}), f32[128,1,32]{2,1,0:T(1,128)S(1)}, u32[]{:S(2)}, u32[]{:S(2)}) async-start(f32[128,1,32]{2,1,0:T(1,128)} %bitcast.12), calls=%async_computation.4 | async-start | bytes 131072 | tf_op jit(solution)/shard_map/all_to_all | solution.py:394
where the time goes:
time: 219 us
  waiting for transfers between devices  75.4 us (34%)
  blocking collectives  67.9 us (31%)
  Pallas kernels  30.1 us (14%)
  starting transfers between devices  27.5 us (13%)
  local copies, waits for them, and re-layouts  11.8 us (5%)
  other arithmetic  5.05 us (2%)
    all_to_all x1, blocking collectives, shards(): lax.all_to_all(shaped.reshape(DEV, 32, 128), BOTH, 0, 0, tiled=True)  34.5 us
    ppermute x1, waiting for transfers between devices, shards(): lax.ppermute(amplitude[0:1], BOTH, [(0, 64)] + [(i, DEV - i) for i in ran...  34.1 us
    all_to_all x1, blocking collectives, shards(): lax.all_to_all(white_noise.reshape(8, 64, 1024), 'col', 0, 0, tiled=True)  33.4 us
    all_to_all x1, waiting for transfers between devices, shards(): filtered = lax.all_to_all(field, 'col', 0, 0, tiled=True).reshape(512, 1024)  24.2 us
    pallas_call x1, Pallas kernels, shards(): call(columns, flat)  12.6 us
    all_to_all x1, waiting for transfers between devices, shards(): lax.all_to_all(partial_sums.reshape(DEV, 1, CAP), BOTH, 0, 0, tiled=True)  9.46 us
    unnamed x45, local copies, waits for them, and re-layouts  9.32 us
    all_to_all x1, starting transfers between devices, shards(): spec = lax.all_to_all(spec.reshape(DEV, 32, 128), BOTH, 0, 0, tiled=True)  8.57 us
  transfers between devices with their start and end apart: 5, of which 4 were waited for; matrix products, arithmetic and copies ran while one was open for 1% of the time, Pallas kernels for 3%

commit v1 on v0

v1 whole, which is shorter than its diff:
```python
from functools import partial

import jax
import jax.numpy as jnp
import ml_dtypes
import numpy as np
from jax import lax
from jax.experimental import pallas as pl
from jax.experimental.pallas import tpu as pltpu
from jax.sharding import PartitionSpec as P

TILE = 128
CAP = 32
N = 8192
DEV = 128
HALF = 32
BOTH = ("row", "col")

bump_height = 64.0
persist = 0.8
innovate = 0.6
log_mean = -0.3
log_scale = 0.6

BF = jnp.bfloat16
F32 = jnp.float32


def hi_lo(table):
    table = np.asarray(table, np.float64)
    hi = table.astype(ml_dtypes.bfloat16)
    lo = (table - hi.astype(np.float64)).astype(ml_dtypes.bfloat16)
    return np.concatenate([hi, lo], axis=1)


def stacked(table):
    half = table.shape[1] // 2
    return np.concatenate([table[:, :half], table[:, half:]], axis=0)


def angle(left, right, length):
    return 2.0 * np.pi / length * (np.outer(left, right) % length)


def real_forward():
    turn = angle(np.arange(64), np.arange(64), 64)
    table = np.concatenate([np.cos(turn[:33]), -np.sin(turn[1:32])], axis=0)
    return hi_lo(table)


def real_inverse():
    turn = angle(np.arange(64), np.arange(64), 64)
    real = 2.0 * np.cos(turn[:, :33])
    real[:, 0] = 1.0
    table = np.concatenate([real, -2.0 * np.sin(turn[:, 1:32])], axis=1)
    return hi_lo(table)


def widen(small_ref, fwd_ref, inv_ref):
    tall = (
        lax.broadcasted_iota(jnp.int32, (512, 64), 0) // 8 == lax.broadcasted_iota(jnp.int32, (512, 64), 1)
    ).astype(BF)
    row = lax.broadcasted_iota(jnp.int32, (512, 512), 0)
    col = lax.broadcasted_iota(jnp.int32, (512, 512), 1)
    same = row % 8 == col % 8
    for k, ref in enumerate([fwd_ref, inv_ref]):
        for half in range(2):
            small = small_ref[k, :, half * 64 : half * 64 + 64]
            grown = dot(dot(tall, small).astype(BF), tall, ((1,), (1,)))
            ref[half * 512 : half * 512 + 512, :] = jnp.where(same, grown, 0.0).astype(BF)


def row_twiddle():
    turn = angle(np.arange(33), np.arange(128), N)
    return np.concatenate([np.cos(turn), np.sin(turn)], axis=1).astype(np.float32)


def row_tables():
    turn = angle(np.arange(128), np.arange(128), 128)
    cos, sin = np.cos(turn), np.sin(turn)
    high = (np.arange(128) >= 64).astype(np.float64)[:, None]
    imag = -sin * high
    imag[64] = 1.0
    forward = np.concatenate([cos * high, imag], axis=0)
    top, bottom = 2.0 * cos * high, -2.0 * sin * high
    top[64] = cos[64]
    bottom[64] = 1.0
    inverse = np.concatenate([top, bottom], axis=0)
    return hi_lo(np.block([[cos, sin], [-sin, cos]])), hi_lo(forward), hi_lo(inverse)


def col_tables(sign):
    turn = angle(np.arange(128), np.arange(128), 128)
    cos, sin = np.cos(turn), sign * np.sin(turn)
    long = np.block([[cos, -sin], [sin, cos]])
    turn = angle(np.arange(64), np.arange(64), 64)
    cos, sin = np.kron(np.eye(2), np.cos(turn)), np.kron(np.eye(2), sign * np.sin(turn))
    short = np.block([[cos, sin], [-sin, cos]])
    return hi_lo(long), hi_lo(short)


def col_twiddle():
    turn = angle(np.arange(128), np.arange(128) % 64, N)
    return np.concatenate([np.cos(turn), np.sin(turn)], axis=1).astype(np.float32)


def split(value):
    hi = value.astype(BF)
    return hi, (value - hi.astype(F32)).astype(BF)


def dot(left, right, dims=((1,), (0,))):
    return lax.dot_general(left, right, (dims, ((), ())), preferred_element_type=F32)


def times_table(value, table):
    rows, half = value.shape[0], table.shape[1] // 2
    hi, lo = split(value)
    first = dot(jnp.concatenate([hi, lo], axis=0), table[:, :half])
    return first[:rows] + first[rows:] + dot(hi, table[:, half:])


def table_times(table, value, dims=((1,), (0,))):
    rows = table.shape[0] // 2
    hi, lo = split(value)
    first = dot(table[...], hi, dims)
    return first[:rows] + first[rows:] + dot(table[:rows, :], lo, dims)


def take(ref, group):
    return jnp.swapaxes(ref[:, group * 8 : group * 8 + 8, :], 0, 1)


def put(ref, group, blocks):
    ref[:, group * 8 : group * 8 + 8, :] = jnp.swapaxes(jnp.stack(blocks), 0, 1)


def call(body, out, scratch=(), limit=24, flops=2_000_000_000, bytes_accessed=6_000_000):
    return pl.pallas_call(
        body,
        out_shape=out,
        scratch_shapes=list(scratch),
        compiler_params=pltpu.CompilerParams(vmem_limit_bytes=limit << 20),
        cost_estimate=pl.CostEstimate(flops=flops, bytes_accessed=bytes_accessed, transcendentals=0),
    )


def forward_rows(x_ref, wide_ref, tw_ref, whole_ref, last_ref, out_ref, mid):
    def groups(step, carry):
        base = pl.multiple_of(step * 16, 16)
        left = [x_ref[c, pl.ds(base, 8), h * 128 : h * 128 + 128] for c in range(8) for h in range(8)]
        right = [x_ref[c, pl.ds(base + 8, 8), h * 128 : h * 128 + 128] for c in range(8) for h in range(8)]
        block = jnp.concatenate([jnp.concatenate(left, axis=0), jnp.concatenate(right, axis=0)], axis=1)
        spec = table_times(wide_ref, block)
        for p in range(33):
            cos, sin = tw_ref[p : p + 1, :128], tw_ref[p : p + 1, 128:]
            for g in range(2):
                lanes = slice(g * 128, g * 128 + 128)
                rows = pl.ds(p * 64 + base + g * 8, 8)
                real = spec[p * 8 : p * 8 + 8, lanes]
                if p == 0:
                    mid[rows, :128] = real
                    continue
                if p == 32:
                    mid[rows, :128] = real * cos
                    mid[rows, 128:] = -(real * sin)
                    continue
                imag = spec[(32 + p) * 8 : (32 + p) * 8 + 8, lanes]
                mid[rows, :128] = real * cos + imag * sin
                mid[rows, 128:] = imag * cos - real * sin
        return carry

    lax.fori_loop(0, 4, groups, 0)

    reals, imags = [], []
    for t in range(8):
        rows = mid[(4 * t + 1) * 64 : (4 * t + 5) * 64, :]
        value = table_times(whole_ref, rows, ((1,), (1,)))
        if t == 7:
            rows = jnp.concatenate([jnp.zeros((192, 128), F32), mid[0:64, :128]], axis=0)
            other = table_times(last_ref, rows, ((1,), (1,)))
            q = lax.broadcasted_iota(jnp.int32, (256, 256), 0) % 128
            lane = lax.broadcasted_iota(jnp.int32, (256, 256), 1)
            value = jnp.where((q >= 64) & (lane >= 192), other, value)
        for u in range(2):
            reals.append(value[:128, u * 128 : u * 128 + 128])
            imags.append(value[128:, u * 128 : u * 128 + 128])
        if t % 4 == 3:
            put(out_ref, t // 4, reals)
            put(out_ref, 2 + t // 4, imags)
            reals, imags = [], []


def columns(x_ref, w_ref, tw_ref, table_ref, out_ref):
    long_ref, ilong_ref = table_ref.at[0:512, :], table_ref.at[512:1024, :]
    short_ref, ishort_ref = [
        jnp.concatenate([table_ref[k : k + 256, :], table_ref[k + 256 : k + 512, :]], axis=1)
        for k in (1024, 1536)
    ]
    cos, sin = tw_ref[:, :128], tw_ref[:, 128:]

    def some(blocks, extra):
        group = blocks[0] // 8
        real = jnp.concatenate(list(take(x_ref, group)), axis=1)
        imag = jnp.concatenate(list(take(x_ref, 2 + group)), axis=1)
        mid = table_times(long_ref, jnp.concatenate([real, imag], axis=0))
        joints = []
        for u in range(len(blocks)):
            real, imag = mid[:128, u * 128 : u * 128 + 128], mid[128:, u * 128 : u * 128 + 128]
            joints.append(jnp.concatenate([real * cos + imag * sin, imag * cos - real * sin], axis=1))
        spec = times_table(jnp.concatenate(joints, axis=0), short_ref)
        joints = []
        for u, b in enumerate(blocks):
            weight = w_ref[b]
            joints.append(spec[u * 128 : u * 128 + 128] * jnp.concatenate([weight, weight], axis=1))
        if extra:
            weight = w_ref[16]
            u = len(blocks) - 1
            joints.append(spec[u * 128 : u * 128 + 128] * jnp.concatenate([weight, weight], axis=1))
        mixed = times_table(jnp.concatenate(joints, axis=0), ishort_ref)
        reals, imags = [], []
        for u in range(len(joints)):
            real, imag = mixed[u * 128 : u * 128 + 128, :128], mixed[u * 128 : u * 128 + 128, 128:]
            reals.append(real * cos - imag * sin)
            imags.append(imag * cos + real * sin)
        done = table_times(
            ilong_ref,
            jnp.concatenate([jnp.concatenate(reals, axis=1), jnp.concatenate(imags, axis=1)], axis=0),
        )
        last = len(joints) - 1
        put(out_ref, group, [done[:128, u * 128 : u * 128 + 128] for u in range(8)])
        put(out_ref, 2 + group, [done[128:, u * 128 : u * 128 + 128] for u in [*range(7), last]])

    some(range(8), False)
    some(range(8, 16), True)


def inverse_rows(x_ref, wide_ref, tw_ref, whole_ref, last_ref, out_ref, mid):

    def place(p, value):
        cos, sin = tw_ref[p : p + 1, :128], tw_ref[p : p + 1, 128:]
        real, imag = value[:, :128], value[:, 128:]
        mid[p * 64 : p * 64 + 64, :] = real * cos - imag * sin
        if p < 32:
            mid[(32 + p) * 64 : (33 + p) * 64, :] = imag * cos + real * sin

    for t in range(8):
        if t % 4 == 0:
            reals, imags = take(x_ref, t // 4), take(x_ref, 2 + t // 4)
        u = t % 4 * 2
        real = jnp.concatenate([reals[u], reals[u + 1]], axis=1)
        imag = jnp.concatenate([imags[u], imags[u + 1]], axis=1)
        joint = jnp.concatenate([real, imag], axis=0).T
        if t == 7:
            slot = lax.broadcasted_iota(jnp.int32, (256, 256), 0)
            q = lax.broadcasted_iota(jnp.int32, (256, 256), 1) % 128
            mid[0:64, :] = times_table(joint[192:, :], last_ref)
            joint = jnp.where((slot >= 192) & (q >= 64), 0.0, joint)
        result = times_table(joint, whole_ref)
        for k in range(4):
            place(4 * t + k + 1, result[k * 64 : k * 64 + 64, :])

    def groups(step, carry):
        base = pl.multiple_of(step * 16, 16)
        left = [mid[pl.ds(pp * 64 + base, 8), :] for pp in range(64)]
        right = [mid[pl.ds(pp * 64 + base + 8, 8), :] for pp in range(64)]
        block = jnp.concatenate([jnp.concatenate(left, axis=0), jnp.concatenate(right, axis=0)], axis=1)
        field = table_times(wide_ref, block)
        for c in range(8):
            for h in range(8):
                row = (c * 8 + h) * 8
                for g in range(2):
                    out_ref[c, pl.ds(base + g * 8, 8), h * 128 : h * 128 + 128] = field[
                        row : row + 8, g * 128 : g * 128 + 128
                    ]
        return carry

    lax.fori_loop(0, 4, groups, 0)


def finish(slot_ref, field_ref, prev_ref, state_ref, sums_ref, cells):
    for block in range(8):
        for h in range(8):
            lanes = slice(h * 128, h * 128 + 128)
            state = persist * prev_ref[block, :, lanes] + innovate * field_ref[block, :, lanes]
            state_ref[block, :, lanes] = state
            rain = jnp.exp(log_mean + log_scale * state)
            cells[h, block : block + 1, :] = jnp.sum(rain, axis=0, keepdims=True)
    dest = lax.broadcasted_iota(jnp.int32, (DEV, 128), 0) * CAP
    lane = lax.broadcasted_iota(jnp.int32, (DEV, 128), 1)
    place = jnp.where(lane < CAP, dest + lane, -1)
    total = jnp.zeros((DEV, 128), F32)
    for h in range(8):
        half = jnp.sum(cells[h], axis=1, keepdims=True)
        for a in range(4):
            tile = (half[2 * a : 2 * a + 1] + half[2 * a + 1 : 2 * a + 2]) * (1.0 / (TILE * TILE))
            total = total + jnp.where(place == slot_ref[a * 8 + h], tile, 0.0)
    sums_ref[...] = total


def reversal():
    flip = np.zeros((128, 128), np.float32)
    for k in range(1, 128):
        flip[k, 128 - k] = 1.0
    first = np.zeros((128, 128), np.float32)
    first[0, 0] = 1.0
    return np.concatenate([flip, first], axis=1).astype(ml_dtypes.bfloat16)


def weights(d_ref, amp_ref, near_ref, far_ref, row_ref, flip_ref, out_ref, own, rev, zero):
    d = d_ref[0]
    low = d < 64
    middle = d == 64

    def fill(kb):
        lanes = slice(kb * 128, kb * 128 + 128)
        return amp_ref[:, lanes], jnp.concatenate([near_ref[:, lanes], far_ref[:, lanes]], axis=0), row_ref[0:1, lanes]

    for kb in range(64):
        amp, mir, row = fill(kb)
        own_tail = jnp.where(low, amp[32:33], amp[0:1])
        mir_tail = jnp.where(low, mir[0:1], jnp.where(middle, amp[0:1], row))
        flipped = [mir[31 - s : 32 - s] for s in range(31)]
        own_rows = jnp.concatenate(
            [amp[1:32], own_tail, jnp.where(middle, row, own_tail)], axis=0
        )
        mir_rows = jnp.concatenate(flipped + [mir_tail, jnp.where(middle, row, mir_tail)], axis=0)
        own[pl.ds(kb, 33, stride=64), :] = own_rows
        rev[pl.ds(63 - kb, 33, stride=64), :] = mir_rows
        zero[pl.ds((64 - kb) % 64, 33, stride=64), :] = mir_rows

    ka = lax.broadcasted_iota(jnp.int32, (128, 128), 0)
    lane = lax.broadcasted_iota(jnp.int32, (128, 128), 1)
    k0 = ka + 128 * (lane % 64)
    f0 = jnp.where(k0 < N // 2, k0, k0 - N).astype(F32)
    flip, first = flip_ref[:, :128], flip_ref[:, 128:]

    def exact(table, rows):
        a = rows.astype(BF)
        rest = rows - a.astype(F32)
        b = rest.astype(BF)
        c = (rest - b.astype(F32)).astype(BF)
        dims = ((1,), (1,))
        return dot(table, a, dims) + dot(table, b, dims) + dot(table, c, dims)

    def weight(own_rows, rev_rows, zero_rows, p):
        k1 = d * 64 + p
        f1 = jnp.where(k1 < N // 2, k1, k1 - N).astype(F32)
        width_sq = float((N // 128) * (N // 128))
        envelope = 1.0 + bump_height / (1.0 + (f0 * f0 + f1 * f1) / width_sq)
        both = own_rows.T + exact(flip, rev_rows) + exact(first, zero_rows)
        return both * (envelope * (0.5 / (N * N)))

    def step(b, carry):
        rows = pl.ds(pl.multiple_of(b * 128, 128), 128)
        slot = 2 * b + lane // 64
        p = jnp.where(slot < 31, slot + 1, jnp.where(low, 32, 0))
        out_ref[b] = weight(own[rows, :], rev[rows, :], zero[rows, :], p)
        return carry

    lax.fori_loop(0, 16, step, 0)
    upper = slice(31 * 64, 33 * 64)
    p = jnp.where(low, 32, jnp.where(middle, -64 * 64, 0))
    p = jnp.where(lane < 64, jnp.where(low, 32, 0), p)
    value = weight(own[upper, :], rev[upper, :], zero[upper, :], p)
    out_ref[16] = jnp.where(lane < 64, out_ref[15], value)


def catchment_rows(catch_id, owner_map, devices):
    owners = owner_map[:, 0]
    hits = (owners[:, None] == jnp.arange(devices, dtype=jnp.int32)[None, :]).astype(jnp.int32)
    ranks = jnp.sum(hits * (jnp.cumsum(hits, axis=0) - 1), axis=1)
    slot = owners * CAP + ranks
    matches = catch_id.reshape(-1)[:, None] == jnp.arange(owners.shape[0], dtype=jnp.int32)[None, :]
    return jnp.sum(jnp.where(matches, slot[None, :], 0), axis=1)


def shards(white_noise, amplitude, state_prev, catch_id, owner_map, unit_graph, queue_prev):
    d = lax.axis_index(BOTH)
    flat = jax.ShapeDtypeStruct((DEV, 32, 128), F32)
    slab = lax.all_to_all(white_noise.reshape(8, 64, 1024), "col", 0, 0, tiled=True)
    forward_wide, inverse_wide = call(
        widen, [jax.ShapeDtypeStruct((1024, 512), BF)] * 2, flops=100_000_000, bytes_accessed=2_000_000
    )(np.stack([real_forward(), real_inverse()]))
    near = lax.ppermute(amplitude[32:48], BOTH, [(i, DEV - 1 - i) for i in range(DEV)])
    far = lax.ppermute(amplitude[48:64], "row", [(i, 15 - i) for i in range(16)])
    partner = lax.ppermute(
        amplitude[0:1], BOTH, [(0, 64)] + [(i, DEV - i) for i in range(1, 64)]
    )
    slab, near, far, partner = lax.optimization_barrier((slab, near, far, partner))
    far = lax.ppermute(far, "col", [(i, 7 - i) for i in range(8)])
    weight = pl.pallas_call(
        weights,
        out_shape=jax.ShapeDtypeStruct((17, 128, 128), F32),
        in_specs=[pl.BlockSpec(memory_space=pltpu.SMEM)] + [pl.BlockSpec(memory_space=pltpu.VMEM)] * 5,
        scratch_shapes=[pltpu.VMEM((33 * 64, 128), F32)] * 3,
        compiler_params=pltpu.CompilerParams(vmem_limit_bytes=24 << 20),
        cost_estimate=pl.CostEstimate(flops=200_000_000, bytes_accessed=6_000_000, transcendentals=0),
    )(d.astype(jnp.int32).reshape(1), amplitude, near, far, partner, reversal())

    tw_row = row_twiddle()
    whole, forward_last, inverse_last = row_tables()
    spec = call(forward_rows, flat, [pltpu.VMEM((33 * 64, 256), F32)])(
        slab, forward_wide, tw_row, stacked(whole), stacked(forward_last)
    )
    spec, far = lax.optimization_barrier((spec, far))
    spec = lax.all_to_all(spec, BOTH, 0, 0, tiled=True)
    long, short = col_tables(-1.0)
    ilong, ishort = col_tables(1.0)
    tables = np.concatenate([stacked(table) for table in (long, ilong, short, ishort)], axis=0)
    shaped = call(columns, flat)(spec, weight, col_twiddle(), tables)
    shaped = lax.all_to_all(shaped, BOTH, 0, 0, tiled=True)
    slab_type = jax.ShapeDtypeStruct((8, 64, 1024), F32)
    field = call(inverse_rows, slab_type, [pltpu.VMEM((64 * 64, 128), F32)])(
        shaped, inverse_wide, tw_row, whole, inverse_last
    )
    filtered = lax.all_to_all(field, "col", 0, 0, tiled=True)
    tile_slot = catchment_rows(catch_id, owner_map, DEV)
    state_new, sums = pl.pallas_call(
        finish,
        out_shape=[slab_type, jax.ShapeDtypeStruct((DEV, 128), F32)],
        in_specs=[pl.BlockSpec(memory_space=pltpu.SMEM)] + [pl.BlockSpec(memory_space=pltpu.VMEM)] * 2,
        scratch_shapes=[pltpu.VMEM((8, 8, 128), F32)],
        compiler_params=pltpu.CompilerParams(vmem_limit_bytes=24 << 20),
        cost_estimate=pl.CostEstimate(flops=5_000_000, bytes_accessed=6_000_000, transcendentals=500_000),
    )(tile_slot.astype(jnp.int32), filtered, state_prev.reshape(8, 64, 1024))
    received = lax.all_to_all(sums.reshape(DEV, 1, 128), BOTH, 0, 0, tiled=True)
    slot_rain = received.sum(axis=(0, 1))[:CAP]
    shifted = jnp.concatenate(
        [queue_prev[1:], jnp.zeros((1, queue_prev.shape[1]), jnp.float32)], axis=0
    )
    flow_queue = shifted + unit_graph * slot_rain[None, :]
    return (state_new.reshape(512, 1024), flow_queue)


def solution(mesh):
    return jax.shard_map(
        shards,
        mesh=mesh,
        in_specs=(
            P("row", "col"),
            P(BOTH, None),
            P("row", "col"),
            P("row", "col"),
            P(),
            P(None, BOTH),
            P(None, BOTH),
        ),
        out_specs=(P("row", "col"), P(None, BOTH)),
        check_vma=False,
    )
```

time: 219 us -> 198 us (0.904)
  blocking collectives: 67.9 us -> 34.7 us
  starting transfers between devices: 27.5 us -> 45 us
  other arithmetic: 5.05 us -> 2.13 us
  Pallas kernels: 30.1 us -> 27.2 us
    all_to_all x2 -> x1, blocking collectives: 67.9 us -> 34.7 us  [shards(): shaped = lax.all_to_all(shaped, BOTH, 0, 0, tiled=True)]
    all_to_all x3 -> x4, waiting for transfers between devices: 33.7 us -> 55.1 us  [the longest x1 24.2 us: shards(): filtered = lax.all_to_all(field, 'col', 0, 0, tiled=True)]
    ppermute x1, waiting for transfers between devices: 34.1 us -> 18.8 us  [shards(): lax.ppermute(amplitude[0:1], BOTH, [(0, 64)] + [(i, DEV - i) for i in ran...]
    all_to_all x3 -> x4, starting transfers between devices: 17.7 us -> 27.4 us  [the longest x1 11.3 us: shards(): spec = lax.all_to_all(spec, BOTH, 0, 0, tiled=True)]
    ppermute x1 -> x3, waiting for transfers between devices: 7.66 us -> 2.66 us  [the longest x1 2.65 us: shards(): far = lax.ppermute(far, 'col', [(i, 7 - i) for i in range(8)])]
    ppermute x1, starting transfers between devices: 1.85 us -> 6.15 us  [shards(): lax.ppermute(amplitude[0:1], BOTH, [(0, 64)] + [(i, DEV - i) for i in ran...]
    pallas_call x2 -> x4, Pallas kernels: 18.3 us -> 14.6 us  [the longest x1 7.16 us: shards(): shaped = call(columns, flat)(spec, weight, col_twiddle(), tables)]
    ppermute x1 -> x3, starting transfers between devices: 7.97 us -> 11.4 us  [the longest x1 7.57 us: shards(): lax.ppermute(amplitude[32:48], BOTH, [(i, DEV - 1 - i) for i in range(DEV)])]
  transfers between devices with their start and end apart: 5 -> 8, of which waited for: 4 -> 6; matrix products, arithmetic and copies ran while one was open for 1% -> 1% of each run, Pallas kernels for 3% -> 7%
where the time goes in v1:
time: 198 us
  waiting for transfers between devices  76.6 us (39%)
  starting transfers between devices  45 us (23%)
  blocking collectives  34.7 us (18%)
  Pallas kernels  27.2 us (14%)
  local copies, waits for them, and re-layouts  11.1 us (6%)
  other arithmetic  2.13 us (1%)
    all_to_all x1, blocking collectives, shards(): shaped = lax.all_to_all(shaped, BOTH, 0, 0, tiled=True)  34.7 us
    all_to_all x1, waiting for transfers between devices, shards(): filtered = lax.all_to_all(field, 'col', 0, 0, tiled=True)  24.2 us
    all_to_all x1, waiting for transfers between devices, shards(): spec = lax.all_to_all(spec, BOTH, 0, 0, tiled=True)  20.5 us
    ppermute x1, waiting for transfers between devices, shards(): lax.ppermute(amplitude[0:1], BOTH, [(0, 64)] + [(i, DEV - i) for i in ran...  18.8 us
    all_to_all x1, starting transfers between devices, shards(): spec = lax.all_to_all(spec, BOTH, 0, 0, tiled=True)  11.3 us
    unnamed x46, local copies, waits for them, and re-layouts  10.4 us
    all_to_all x1, waiting for transfers between devices, shards(): received = lax.all_to_all(sums.reshape(DEV, 1, 128), BOTH, 0, 0, tiled=True)  9.46 us
    ppermute x1, starting transfers between devices, shards(): lax.ppermute(amplitude[32:48], BOTH, [(i, DEV - 1 - i) for i in range(DEV)])  7.57 us
  transfers between devices with their start and end apart: 8, of which 6 were waited for; matrix products, arithmetic and copies ran while one was open for 1% of the time, Pallas kernels for 7%

profile of v1, /device:TPU:1, one launch (start us, length us, event | category | flops | bytes accessed | tf_op | source)
XLA Modules:
  0.0 197.6 jit_solution(2391575124404569044)
XLA Ops:
  0.6 7.0 %all-to-all-start = ((f32[8,64,1024]{2,1,0:T(8,128)}), f32[8,64,1024]{2,1,0:T(8,128)}, u32[]{:S(2)}, u32[]{:S(2)}) async-start(f32[8,64,1024]{2,1,0:T(8,128)} %bitcast.19), calls=%async_computation | async-start | bytes 4194304 | tf_op jit(solution)/shard_map/all_to_all | solution.py:381
  7.6 0.0 copy-start.14
  7.6 0.0 copy-start.15
  7.6 0.1 fusion.4
  7.7 7.6 %collective-permute-start = (f32[16,8192]{1,0:T(8,128)S(1)}, f32[16,8192]{1,0:T(8,128)S(1)}, u32[]{:S(2)}, u32[]{:S(2)}) collective-permute-start(f32[16,8192]{1,0:T(8,128)S(1)} %get-tuple-element.21), channel_id=1, source_target_pairs={{0,127},{1,126},{2,125},{3,124},{4,123},{5,122},{6,121},{7,120},{8... | collective-permute-start | bytes 1572872 | tf_op jit(solution)/shard_map/ppermute | solution.py:385
  15.3 6.1 %collective-permute-start.2 = (f32[1,8192]{1,0:T(1,128)S(1)}, f32[1,8192]{1,0:T(1,128)S(1)}, u32[]{:S(2)}, u32[]{:S(2)}) collective-permute-start(f32[1,8192]{1,0:T(1,128)S(1)} %slice.25), channel_id=1, source_target_pairs={{0,64},{1,127},{2,126},{3,125},{4,124},{5,123},{6,122},{7,121},{8,... | collective-permute-start | bytes 98312 | tf_op jit(solution)/shard_map/ppermute | solution.py:387
  21.5 18.8 %collective-permute-done.2.row_ref = f32[1,8192]{1,0:T(1,128)S(1)} collective-permute-done((f32[1,8192]{1,0:T(1,128)S(1)}, f32[1,8192]{1,0:T(1,128)S(1)}, u32[]{:S(2)}, u32[]{:S(2)}) %collective-permute-start.2) | collective-permute-done | bytes 32800 | tf_op jit(solution)/shard_map/ppermute | solution.py:387
  40.3 0.0 collective-permute-done.near_ref
  40.3 0.8 copy-done.4
  41.0 0.9 all-to-all-done.x_ref
  41.9 3.9 %collective-permute-start.3 = (f32[16,8192]{1,0:T(8,128)S(1)}, f32[16,8192]{1,0:T(8,128)S(1)}, u32[]{:S(2)}, u32[]{:S(2)}) collective-permute-start(f32[16,8192]{1,0:T(8,128)S(1)} %collective-permute-done.1), channel_id=1, source_target_pairs={{0,7},{1,6},{2,5},{3,4},{4,3},{5,2},{6,1},{7,0},{8,15},{9,14},{10,... | collective-permute-start | bytes 1572872 | tf_op jit(solution)/shard_map/ppermute | solution.py:391
  45.8 1.2 shard_map.167
  47.1 1.0 copy-done.17
  48.0 5.3 %shard_map.168 = f32[128,32,128]{2,1,0:T(8,128)S(1)} custom-call(f32[8,64,1024]{2,1,0:T(8,128)} %all-to-all-done.x_ref, bf16[1024,512]{1,0:T(8,128)(2,1)S(1)} %get-tuple-element.12.wide_ref, f32[33,256]{1,0:T(8,128)S(1)} %copy-done.15, bf16[512,256]{1,0:T(8,128)(2,1)S(1)} %copy-done.11, bf16[512,128]{1,0:T(8,128)(2,1)S(1)} %copy-done.14), custom_call_target="tpu_custom_call" | custom-call | flops 2000000000 | bytes 6000000 | tf_op jit(solution)/shard_map/pallas_call | solution.py:403
  53.4 0.0 copy-start.2
  53.4 1.3 copy-done.2
  54.7 2.7 %collective-permute-done.3.far_ref = f32[16,8192]{1,0:T(8,128)S(1)} collective-permute-done((f32[16,8192]{1,0:T(8,128)S(1)}, f32[16,8192]{1,0:T(8,128)S(1)}, u32[]{:S(2)}, u32[]{:S(2)}) %collective-permute-start.3) | collective-permute-done | bytes 524320 | tf_op jit(solution)/shard_map/ppermute | solution.py:391
  57.3 0.8 copy-done.6
  58.1 11.3 %all-to-all-start.1 = ((f32[128,32,128]{2,1,0:T(8,128)}), f32[128,32,128]{2,1,0:T(8,128)}, u32[]{:S(2)}, u32[]{:S(2)}) async-start(f32[128,32,128]{2,1,0:T(8,128)} %copy-done.2), calls=%async_computation.1 | async-start | bytes 4194304 | tf_op jit(solution)/shard_map/all_to_all | solution.py:407
  69.5 1.0 copy-done.5
  70.5 1.0 copy-done.7
  71.5 7.2 %shard_map.169.w_ref = f32[17,128,128]{2,1,0:T(8,128)S(1)} custom-call(s32[1]{0:T(128)} %bitcast.6.d_ref, f32[64,8192]{1,0:T(8,128)S(1)} %copy-done, f32[16,8192]{1,0:T(8,128)S(1)} %copy-done.5, f32[16,8192]{1,0:T(8,128)S(1)} %copy-done.7, f32[1,8192]{1,0:T(1,128)S(1)} %collective-permute-done.2.row_ref, bf16[128,256]{1,0:T(8,128)(2,1)S(1)} %copy-done.8), custom_call_target="tpu_custom_call" | custom-call | flops 200000000 | bytes 6000000 | tf_op jit(solution)/shard_map/pallas_call | solution.py:392
  78.8 20.5 %all-to-all-done.1.x_ref = f32[128,32,128]{2,1,0:T(8,128)} async-done(((f32[128,32,128]{2,1,0:T(8,128)}), f32[128,32,128]{2,1,0:T(8,128)}, u32[]{:S(2)}, u32[]{:S(2)}) %all-to-all-start.1) | async-done | bytes 2097184 | tf_op jit(solution)/shard_map/all_to_all | solution.py:407
  99.3 1.2 copy-done.9
  100.5 7.2 %shard_map.170 = f32[128,32,128]{2,1,0:T(8,128)S(1)} custom-call(f32[128,32,128]{2,1,0:T(8,128)} %all-to-all-done.1.x_ref, f32[17,128,128]{2,1,0:T(8,128)S(1)} %shard_map.169.w_ref, f32[128,256]{1,0:T(8,128)S(1)} %copy-done.13, bf16[2048,256]{1,0:T(8,128)(2,1)S(1)} %copy-done.9), custom_call_target="tpu_custom_call" | custom-call | flops 2000000000 | bytes 6000000 | tf_op jit(solution)/shard_map/pallas_call | solution.py:411
  107.7 0.0 copy-start.10
  107.7 0.0 copy-start.12
  107.8 34.7 %all_to_all.25.x_ref = f32[128,32,128]{2,1,0:T(8,128)S(1)} all-to-all(f32[128,32,128]{2,1,0:T(8,128)S(1)} %shard_map.170), channel_id=1, replica_groups=mesh['row'=16,'col'=8] {'row','col'}, dimensions={0} | all-to-all | bytes 4194304 | tf_op jit(solution)/shard_map/all_to_all | solution.py:412
  142.5 3.7 %shard_map.171 = f32[8,64,1024]{2,1,0:T(8,128)S(1)} custom-call(f32[128,32,128]{2,1,0:T(8,128)S(1)} %all_to_all.25.x_ref, bf16[1024,512]{1,0:T(8,128)(2,1)S(1)} %copy-done.18, f32[33,256]{1,0:T(8,128)S(1)} %copy-done.15, bf16[256,512]{1,0:T(8,128)(2,1)S(1)} %copy-done.10, bf16[256,256]{1,0:T(8,128)(2,1)S(1)} %copy-done.12), custom_call_target="tpu_custom_call" | custom-call | flops 2000000000 | bytes 6000000 | tf_op jit(solution)/shard_map/pallas_call | solution.py:414
  146.2 0.0 copy-start.3
  146.2 1.3 copy-done.3
  147.5 4.9 %all-to-all-start.3 = ((f32[8,64,1024]{2,1,0:T(8,128)}), f32[8,64,1024]{2,1,0:T(8,128)S(1)}, u32[]{:S(2)}, u32[]{:S(2)}) async-start(f32[8,64,1024]{2,1,0:T(8,128)} %copy-done.3), calls=%async_computation.3 | async-start | bytes 4194304 | tf_op jit(solution)/shard_map/all_to_all | solution.py:417
  152.4 0.1 copy.24
  152.5 0.3 fusion.1
  152.9 0.1 add_add_fusion
  153.0 0.3 copy.25
  153.3 0.2 copy-done.22
  153.6 0.1 eq.38
  153.7 0.6 fusion
  154.3 0.2 select_reduce_fusion.slot_ref
  154.5 24.2 %all-to-all-done.3.field_ref = f32[8,64,1024]{2,1,0:T(8,128)S(1)} async-done(((f32[8,64,1024]{2,1,0:T(8,128)}), f32[8,64,1024]{2,1,0:T(8,128)S(1)}, u32[]{:S(2)}, u32[]{:S(2)}) %all-to-all-start.3) | async-done | bytes 2097184 | tf_op jit(solution)/shard_map/all_to_all | solution.py:417
  178.8 1.6 copy-done.1
  180.4 2.6 %shard_map.172 = (f32[8,64,1024]{2,1,0:T(8,128)}, f32[128,128]{1,0:T(8,128)}) custom-call(s32[32]{0:T(128)S(1)} %select_reduce_fusion.slot_ref, f32[8,64,1024]{2,1,0:T(8,128)S(1)} %all-to-all-done.3.field_ref, f32[8,64,1024]{2,1,0:T(8,128)S(1)} %bitcast.18), custom_call_target="tpu_custom_call" | custom-call | flops 5000000 | bytes 6000000 | tf_op jit(solution)/shard_map/pallas_call | solution.py:419
  182.9 4.3 %all-to-all-start.4 = ((f32[128,1,128]{2,1,0:T(1,128)}), f32[128,1,128]{2,1,0:T(1,128)S(1)}, u32[]{:S(2)}, u32[]{:S(2)}) async-start(f32[128,1,128]{2,1,0:T(1,128)} %bitcast.10), calls=%async_computation.4 | async-start | bytes 131072 | tf_op jit(solution)/shard_map/all_to_all | solution.py:427
  187.2 0.1 slice.26
  187.3 9.5 %all-to-all-done.4 = f32[128,1,128]{2,1,0:T(1,128)S(1)} async-done(((f32[128,1,128]{2,1,0:T(1,128)}), f32[128,1,128]{2,1,0:T(1,128)S(1)}, u32[]{:S(2)}, u32[]{:S(2)}) %all-to-all-start.4) | async-done | bytes 65568 | tf_op jit(solution)/shard_map/all_to_all | solution.py:427
  196.8 0.2 reduce_sum.29
  196.9 0.7 multiply_add_fusion
  (37 shorter events, 0.1 us)
Async XLA Ops:
  0.6 7.0 %copy-start = (f32[64,8192]{1,0:T(8,128)S(1)}, f32[64,8192]{1,0:T(8,128)}, u32[]{:S(2)}) copy-start(f32[64,8192]{1,0:T(8,128)} %amp_ref.1) | copy-start | bytes 6291460
  0.6 41.3 %all-to-all-start = ((f32[8,64,1024]{2,1,0:T(8,128)}), f32[8,64,1024]{2,1,0:T(8,128)}, u32[]{:S(2)}, u32[]{:S(2)}) async-start(f32[8,64,1024]{2,1,0:T(8,128)} %bitcast.19), calls=%async_computation | async-start | bytes 4194304 | tf_op jit(solution)/shard_map/all_to_all | solution.py:381
  7.6 38.2 %copy-start.16 = (bf16[2,64,128]{2,1,0:T(8,128)(2,1)S(1)}, bf16[2,64,128]{2,1,0:T(8,128)(2,1)}, u32[]{:S(2)}) copy-start(bf16[2,64,128]{2,1,0:T(8,128)(2,1)} %constant.43.clone.small_ref) | copy-start | bytes 98308
  7.6 40.4 %copy-start.11 = (bf16[512,256]{1,0:T(8,128)(2,1)S(1)}, bf16[512,256]{1,0:T(8,128)(2,1)}, u32[]{:S(2)}) copy-start(bf16[512,256]{1,0:T(8,128)(2,1)} %constant.46.clone.whole_ref) | copy-start | bytes 786436
  7.6 40.4 %copy-start.14 = (bf16[512,128]{1,0:T(8,128)(2,1)S(1)}, bf16[512,128]{1,0:T(8,128)(2,1)}, u32[]{:S(2)}) copy-start(bf16[512,128]{1,0:T(8,128)(2,1)} %constant.47.clone.last_ref) | copy-start | bytes 393220
  7.6 40.4 %copy-start.15 = (f32[33,256]{1,0:T(8,128)S(1)}, f32[33,256]{1,0:T(8,128)}, u32[]{:S(2)}) copy-start(f32[33,256]{1,0:T(8,128)} %constant.45.clone.tw_ref) | copy-start | bytes 101380
  7.7 32.5 %collective-permute-start = (f32[16,8192]{1,0:T(8,128)S(1)}, f32[16,8192]{1,0:T(8,128)S(1)}, u32[]{:S(2)}, u32[]{:S(2)}) collective-permute-start(f32[16,8192]{1,0:T(8,128)S(1)} %get-tuple-element.21), channel_id=1, source_target_pairs={{0,127},{1,126},{2,125},{3,124},{4,123},{5,122},{6,121},{7,120},{8... | collective-permute-start | bytes 1572872 | tf_op jit(solution)/shard_map/ppermute | solution.py:385
  15.3 25.8 %collective-permute-start.1 = (f32[16,8192]{1,0:T(8,128)S(1)}, f32[16,8192]{1,0:T(8,128)S(1)}, u32[]{:S(2)}, u32[]{:S(2)}) collective-permute-start(f32[16,8192]{1,0:T(8,128)S(1)} %get-tuple-element.20), channel_id=1, source_target_pairs={{0,120},{8,112},{16,104},{24,96},{32,88},{40,80},{48,72},{56,64},{... | collective-permute-start | bytes 1572872 | tf_op jit(solution)/shard_map/ppermute | solution.py:386
  15.3 24.9 %collective-permute-start.2 = (f32[1,8192]{1,0:T(1,128)S(1)}, f32[1,8192]{1,0:T(1,128)S(1)}, u32[]{:S(2)}, u32[]{:S(2)}) collective-permute-start(f32[1,8192]{1,0:T(1,128)S(1)} %slice.25), channel_id=1, source_target_pairs={{0,64},{1,127},{2,126},{3,125},{4,124},{5,123},{6,122},{7,121},{8,... | collective-permute-start | bytes 98312 | tf_op jit(solution)/shard_map/ppermute | solution.py:387
  40.3 0.8 copy-start.4
  41.9 15.4 %collective-permute-start.3 = (f32[16,8192]{1,0:T(8,128)S(1)}, f32[16,8192]{1,0:T(8,128)S(1)}, u32[]{:S(2)}, u32[]{:S(2)}) collective-permute-start(f32[16,8192]{1,0:T(8,128)S(1)} %collective-permute-done.1), channel_id=1, source_target_pairs={{0,7},{1,6},{2,5},{3,4},{4,3},{5,2},{6,1},{7,0},{8,15},{9,14},{10,... | collective-permute-start | bytes 1572872 | tf_op jit(solution)/shard_map/ppermute | solution.py:391
  47.0 1.0 copy-start.17
  53.4 1.3 copy-start.2
  54.7 14.8 %copy-start.8 = (bf16[128,256]{1,0:T(8,128)(2,1)S(1)}, bf16[128,256]{1,0:T(8,128)(2,1)}, u32[]{:S(2)}) copy-start(bf16[128,256]{1,0:T(8,128)(2,1)} %constant.44.clone.flip_ref) | copy-start | bytes 196612
  57.3 0.8 copy-start.6
  58.1 41.2 %all-to-all-start.1 = ((f32[128,32,128]{2,1,0:T(8,128)}), f32[128,32,128]{2,1,0:T(8,128)}, u32[]{:S(2)}, u32[]{:S(2)}) async-start(f32[128,32,128]{2,1,0:T(8,128)} %copy-done.2), calls=%async_computation.1 | async-start | bytes 4194304 | tf_op jit(solution)/shard_map/all_to_all | solution.py:407
  69.4 1.0 copy-start.5
  70.5 1.0 copy-start.7
  71.5 27.8 %copy-start.13 = (f32[128,256]{1,0:T(8,128)S(1)}, f32[128,256]{1,0:T(8,128)}, u32[]{:S(2)}) copy-start(f32[128,256]{1,0:T(8,128)} %constant.48.clone.tw_ref) | copy-start | bytes 393220
  99.3 1.2 copy-start.9
  107.7 34.8 %copy-start.10 = (bf16[256,512]{1,0:T(8,128)(2,1)S(1)}, bf16[256,512]{1,0:T(8,128)(2,1)}, u32[]{:S(2)}) copy-start(bf16[256,512]{1,0:T(8,128)(2,1)} %constant.50.clone.whole_ref) | copy-start | bytes 786436
  107.7 34.8 %copy-start.12 = (bf16[256,256]{1,0:T(8,128)(2,1)S(1)}, bf16[256,256]{1,0:T(8,128)(2,1)}, u32[]{:S(2)}) copy-start(bf16[256,256]{1,0:T(8,128)(2,1)} %constant.51.clone.last_ref) | copy-start | bytes 393220
  107.7 34.8 %copy-start.18 = (bf16[1024,512]{1,0:T(8,128)(2,1)S(1)}, bf16[1024,512]{1,0:T(8,128)(2,1)}, u32[]{:S(2)}) copy-start(bf16[1024,512]{1,0:T(8,128)(2,1)} %copy-done.17) | copy-start | bytes 3145732
  146.2 1.3 copy-start.3
  147.5 4.9 %copy-start.19 = (s32[2048,1]{0,1:T(1,128)S(1)}, s32[2048,1]{0,1:T(1,128)}, u32[]{:S(2)}) copy-start(s32[2048,1]{0,1:T(1,128)} %param.20) | copy-start | bytes 24580
  147.5 31.3 %all-to-all-start.3 = ((f32[8,64,1024]{2,1,0:T(8,128)}), f32[8,64,1024]{2,1,0:T(8,128)S(1)}, u32[]{:S(2)}, u32[]{:S(2)}) async-start(f32[8,64,1024]{2,1,0:T(8,128)} %copy-done.3), calls=%async_computation.3 | async-start | bytes 4194304 | tf_op jit(solution)/shard_map/all_to_all | solution.py:417
  152.9 0.7 copy-start.22
  178.8 1.6 copy-start.1
  180.4 6.9 %copy-start.20 = (f32[288,32]{0,1:T(8,128)S(1)}, f32[288,32]{0,1:T(8,128)}, u32[]{:S(2)}) copy-start(f32[288,32]{0,1:T(8,128)} %param.22) | copy-start | bytes 110596
  180.4 16.6 %copy-start.21 = (f32[288,32]{0,1:T(8,128)S(1)}, f32[288,32]{0,1:T(8,128)}, u32[]{:S(2)}) copy-start(f32[288,32]{0,1:T(8,128)} %param.21) | copy-start | bytes 110596
  182.9 13.8 %all-to-all-start.4 = ((f32[128,1,128]{2,1,0:T(1,128)}), f32[128,1,128]{2,1,0:T(1,128)S(1)}, u32[]{:S(2)}, u32[]{:S(2)}) async-start(f32[128,1,128]{2,1,0:T(1,128)} %bitcast.10), calls=%async_computation.4 | async-start | bytes 131072 | tf_op jit(solution)/shard_map/all_to_all | solution.py:427

commit v2 on v1

--- a/solution.py
+++ b/solution.py
@@ -7,14 +7,20 @@
 from jax import lax
 from jax.experimental import pallas as pl
 from jax.experimental.pallas import tpu as pltpu
+from jax.sharding import Mesh
 from jax.sharding import PartitionSpec as P
 
 TILE = 128
 CAP = 32
 N = 8192
 DEV = 128
-HALF = 32
-BOTH = ("row", "col")
+FAR = 8
+ROW = ("y", "x")
+COL = ("z", "core")
+BOTH = ROW + COL
+CORES = ("core", "y", "x", "z")
+ORDER = [2 * (e % 64) + e // 64 for e in range(DEV)]
+PAIRS = ORDER + [DEV + e for e in ORDER]
 
 bump_height = 64.0
 persist = 0.8
@@ -86,13 +92,15 @@
     top[64] = cos[64]
     bottom[64] = 1.0
     inverse = np.concatenate([top, bottom], axis=0)
-    return hi_lo(np.block([[cos, sin], [-sin, cos]])), hi_lo(forward), hi_lo(inverse)
+    whole = np.block([[cos, sin], [-sin, cos]])
+    return [hi_lo(table[PAIRS]) for table in (whole, forward, inverse)]
 
 
 def col_tables(sign):
     turn = angle(np.arange(128), np.arange(128), 128)
     cos, sin = np.cos(turn), sign * np.sin(turn)
     long = np.block([[cos, -sin], [sin, cos]])
+    long = long[:, PAIRS] if sign < 0 else long[PAIRS]
     turn = angle(np.arange(64), np.arange(64), 64)
     cos, sin = np.kron(np.eye(2), np.cos(turn)), np.kron(np.eye(2), sign * np.sin(turn))
     short = np.block([[cos, sin], [-sin, cos]])
@@ -179,9 +187,9 @@
         if t == 7:
             rows = jnp.concatenate([jnp.zeros((192, 128), F32), mid[0:64, :128]], axis=0)
             other = table_times(last_ref, rows, ((1,), (1,)))
-            q = lax.broadcasted_iota(jnp.int32, (256, 256), 0) % 128
+            order = lax.broadcasted_iota(jnp.int32, (256, 256), 0) % 64
             lane = lax.broadcasted_iota(jnp.int32, (256, 256), 1)
-            value = jnp.where((q >= 64) & (lane >= 192), other, value)
+            value = jnp.where((order >= 32) & (lane >= 192), other, value)
         for u in range(2):
             reals.append(value[:128, u * 128 : u * 128 + 128])
             imags.append(value[128:, u * 128 : u * 128 + 128])
@@ -191,7 +199,7 @@
             reals, imags = [], []
 
 
-def columns(x_ref, w_ref, tw_ref, table_ref, out_ref):
+def columns(x_ref, far_ref, near_ref, tw_ref, table_ref, out_ref):
     long_ref, ilong_ref = table_ref.at[0:512, :], table_ref.at[512:1024, :]
     short_ref, ishort_ref = [
         jnp.concatenate([table_ref[k : k + 256, :], table_ref[k + 256 : k + 512, :]], axis=1)
@@ -211,10 +219,10 @@
         spec = times_table(jnp.concatenate(joints, axis=0), short_ref)
         joints = []
         for u, b in enumerate(blocks):
-            weight = w_ref[b]
+            weight = far_ref[b] if b < FAR // 2 else near_ref[b - FAR // 2]
             joints.append(spec[u * 128 : u * 128 + 128] * jnp.concatenate([weight, weight], axis=1))
         if extra:
-            weight = w_ref[16]
+            weight = near_ref[16 - FAR // 2]
             u = len(blocks) - 1
             joints.append(spec[u * 128 : u * 128 + 128] * jnp.concatenate([weight, weight], axis=1))
         mixed = times_table(jnp.concatenate(joints, axis=0), ishort_ref)
@@ -253,9 +261,9 @@
         joint = jnp.concatenate([real, imag], axis=0).T
         if t == 7:
             slot = lax.broadcasted_iota(jnp.int32, (256, 256), 0)
-            q = lax.broadcasted_iota(jnp.int32, (256, 256), 1) % 128
+            order = lax.broadcasted_iota(jnp.int32, (256, 256), 1) % 64
             mid[0:64, :] = times_table(joint[192:, :], last_ref)
-            joint = jnp.where((slot >= 192) & (q >= 64), 0.0, joint)
+            joint = jnp.where((slot >= 192) & (order >= 32), 0.0, joint)
         result = times_table(joint, whole_ref)
         for k in range(4):
             place(4 * t + k + 1, result[k * 64 : k * 64 + 64, :])
@@ -278,12 +286,11 @@
     lax.fori_loop(0, 4, groups, 0)
 
 
-def finish(slot_ref, field_ref, prev_ref, state_ref, sums_ref, cells):
+def tile_sums(slot_ref, field_ref, prev_ref, sums_ref, cells):
     for block in range(8):
         for h in range(8):
             lanes = slice(h * 128, h * 128 + 128)
             state = persist * prev_ref[block, :, lanes] + innovate * field_ref[block, :, lanes]
-            state_ref[block, :, lanes] = state
             rain = jnp.exp(log_mean + log_scale * state)
             cells[h, block : block + 1, :] = jnp.sum(rain, axis=0, keepdims=True)
     dest = lax.broadcasted_iota(jnp.int32, (DEV, 128), 0) * CAP
@@ -298,72 +305,95 @@
     sums_ref[...] = total
 
 
+def next_state(field_ref, prev_ref, state_ref):
+    state_ref[...] = persist * prev_ref[...] + innovate * field_ref[...]
+
+
 def reversal():
     flip = np.zeros((128, 128), np.float32)
     for k in range(1, 128):
         flip[k, 128 - k] = 1.0
     first = np.zeros((128, 128), np.float32)
     first[0, 0] = 1.0
-    return np.concatenate([flip, first], axis=1).astype(ml_dtypes.bfloat16)
-
-
-def weights(d_ref, amp_ref, near_ref, far_ref, row_ref, flip_ref, out_ref, own, rev, zero):
+    return np.concatenate([np.eye(128, dtype=np.float32), flip, first], axis=1).astype(ml_dtypes.bfloat16)
+
+
+def exact_parts(rows):
+    a = rows.astype(BF)
+    rest = rows - a.astype(F32)
+    b = rest.astype(BF)
+    return a, b, (rest - b.astype(F32)).astype(BF)
+
+
+def unfold(ref, group, backward):
+    order = range(63, -1, -1) if backward else range(64)
+    rows = slice(group * 8, group * 8 + 8)
+    return jnp.swapaxes(jnp.stack([ref[rows, k * 128 : k * 128 + 128] for k in order]), 0, 1)
+
+
+def weight_block(own, rev, flip_ref, d, p):
+    rows = [
+        jnp.concatenate([a, b, pltpu.roll(b, 1, 0)], axis=1) for a, b in zip(own, rev, strict=True)
+    ]
+    joint = jnp.concatenate(rows, axis=0)
+    dims = ((1,), (1,))
+    both = sum(dot(flip_ref[...], part, dims) for part in exact_parts(joint))
+    shape = (128, len(own) * 64)
+    ka = lax.broadcasted_iota(jnp.int32, shape, 0)
+    lane = lax.broadcasted_iota(jnp.int32, shape, 1)
+    k0 = ka + 128 * (lane % 64)
+    f0 = jnp.where(k0 < N // 2, k0, k0 - N).astype(F32)
+    k1 = d * 64 + p(lane // 64)
+    f1 = jnp.where(k1 < N // 2, k1, k1 - N).astype(F32)
+    width_sq = float((N // 128) * (N // 128))
+    envelope = 1.0 + bump_height / (1.0 + (f0 * f0 + f1 * f1) / width_sq)
+    return both * (envelope * (0.5 / (N * N)))
+
+
+def put_weight(out_ref, first, value):
+    for b in range(value.shape[1] // 128):
+        out_ref[first + b] = value[:, b * 128 : b * 128 + 128]
+
+
+def far_weights(d_ref, amp_ref, far_ref, flip_ref, out_ref):
+    d = d_ref[0]
+    own = [row for g in range(FAR // 8 + 1) for row in unfold(amp_ref, g, False)]
+    rev = [row for g in range(FAR // 8) for row in unfold(far_ref, g, True)]
+    for s in range(0, FAR, 8):
+        mirrored = [rev[FAR - 1 - k] for k in range(s, s + 8)]
+        value = weight_block(own[s + 1 : s + 9], mirrored, flip_ref, d, lambda k, s=s: k + (s + 1))
+        put_weight(out_ref, s // 2, value)
+
+
+def near_weights(d_ref, amp_ref, near_ref, row_ref, flip_ref, out_ref):
     d = d_ref[0]
     low = d < 64
     middle = d == 64
-
-    def fill(kb):
-        lanes = slice(kb * 128, kb * 128 + 128)
-        return amp_ref[:, lanes], jnp.concatenate([near_ref[:, lanes], far_ref[:, lanes]], axis=0), row_ref[0:1, lanes]
-
-    for kb in range(64):
-        amp, mir, row = fill(kb)
-        own_tail = jnp.where(low, amp[32:33], amp[0:1])
-        mir_tail = jnp.where(low, mir[0:1], jnp.where(middle, amp[0:1], row))
-        flipped = [mir[31 - s : 32 - s] for s in range(31)]
-        own_rows = jnp.concatenate(
-            [amp[1:32], own_tail, jnp.where(middle, row, own_tail)], axis=0
-        )
-        mir_rows = jnp.concatenate(flipped + [mir_tail, jnp.where(middle, row, mir_tail)], axis=0)
-        own[pl.ds(kb, 33, stride=64), :] = own_rows
-        rev[pl.ds(63 - kb, 33, stride=64), :] = mir_rows
-        zero[pl.ds((64 - kb) % 64, 33, stride=64), :] = mir_rows
-
-    ka = lax.broadcasted_iota(jnp.int32, (128, 128), 0)
-    lane = lax.broadcasted_iota(jnp.int32, (128, 128), 1)
-    k0 = ka + 128 * (lane % 64)
-    f0 = jnp.where(k0 < N // 2, k0, k0 - N).astype(F32)
-    flip, first = flip_ref[:, :128], flip_ref[:, 128:]
-
-    def exact(table, rows):
-        a = rows.astype(BF)
-        rest = rows - a.astype(F32)
-        b = rest.astype(BF)
-        c = (rest - b.astype(F32)).astype(BF)
-        dims = ((1,), (1,))
-        return dot(table, a, dims) + dot(table, b, dims) + dot(table, c, dims)
-
-    def weight(own_rows, rev_rows, zero_rows, p):
-        k1 = d * 64 + p
-        f1 = jnp.where(k1 < N // 2, k1, k1 - N).astype(F32)
-        width_sq = float((N // 128) * (N // 128))
-        envelope = 1.0 + bump_height / (1.0 + (f0 * f0 + f1 * f1) / width_sq)
-        both = own_rows.T + exact(flip, rev_rows) + exact(first, zero_rows)
-        return both * (envelope * (0.5 / (N * N)))
-
-    def step(b, carry):
-        rows = pl.ds(pl.multiple_of(b * 128, 128), 128)
-        slot = 2 * b + lane // 64
-        p = jnp.where(slot < 31, slot + 1, jnp.where(low, 32, 0))
-        out_ref[b] = weight(own[rows, :], rev[rows, :], zero[rows, :], p)
-        return carry
-
-    lax.fori_loop(0, 16, step, 0)
-    upper = slice(31 * 64, 33 * 64)
-    p = jnp.where(low, 32, jnp.where(middle, -64 * 64, 0))
-    p = jnp.where(lane < 64, jnp.where(low, 32, 0), p)
-    value = weight(own[upper, :], rev[upper, :], zero[upper, :], p)
-    out_ref[16] = jnp.where(lane < 64, out_ref[15], value)
+    own = [row for g in range(5) for row in unfold(amp_ref, g, False)]
+    rev = [row for g in range(4 - FAR // 8) for row in unfold(near_ref, g, True)]
+    row = row_ref[...]
+    turn = lax.broadcasted_iota(jnp.int32, (64, 64), 0) + lax.broadcasted_iota(jnp.int32, (64, 64), 1) == 63
+    turned = sum(dot(turn.astype(BF), part) for part in exact_parts(row))
+    back = unfold(amp_ref, 0, True)[0]
+    own_tail = jnp.where(low, own[32], own[0])
+    rev_tail = jnp.where(low, rev[0], jnp.where(middle, back, turned))
+    own_all = own[1:32] + [own_tail]
+    rev_all = [None] * FAR + [rev[31 - k] for k in range(FAR, 31)] + [rev_tail]
+
+    def plain(k, s):
+        return jnp.where(k + s < 31, k + (s + 1), jnp.where(low, 32, 0))
+
+    for s in range(FAR, 32, 8):
+        value = weight_block(own_all[s : s + 8], rev_all[s : s + 8], flip_ref, d, lambda k, s=s: plain(k, s))
+        put_weight(out_ref, (s - FAR) // 2, value)
+    value = weight_block(
+        [own[31], jnp.where(middle, row, own_tail)],
+        [rev[1], jnp.where(middle, turned, rev_tail)],
+        flip_ref,
+        d,
+        lambda k: jnp.where(k == 0, 31, jnp.where(low, 32, jnp.where(middle, -64 * 64, 0))),
+    )
+    put_weight(out_ref, 16 - FAR // 2, value)
 
 
 def catchment_rows(catch_id, owner_map, devices):
@@ -378,52 +408,64 @@
 def shards(white_noise, amplitude, state_prev, catch_id, owner_map, unit_graph, queue_prev):
     d = lax.axis_index(BOTH)
     flat = jax.ShapeDtypeStruct((DEV, 32, 128), F32)
-    slab = lax.all_to_all(white_noise.reshape(8, 64, 1024), "col", 0, 0, tiled=True)
+    slab = lax.all_to_all(white_noise.reshape(8, 64, 1024), COL, 0, 0, tiled=True)
+    small = np.stack([real_forward(), real_inverse()])
+    near = lax.ppermute(amplitude[32 : 64 - FAR], BOTH, [(i, DEV - 1 - i) for i in range(DEV)])
+    far = lax.ppermute(amplitude[64 - FAR : 64], ROW, [(i, 15 - i) for i in range(16)])
+    partner = lax.ppermute(
+        amplitude[0:1], BOTH, [(0, 64)] + [(i, DEV - i) for i in range(1, 64)]
+    )
+    slab, near, far, partner = lax.optimization_barrier((slab, near, far, partner))
+    far = lax.ppermute(far, COL, [(i, 7 - i) for i in range(8)])
     forward_wide, inverse_wide = call(
         widen, [jax.ShapeDtypeStruct((1024, 512), BF)] * 2, flops=100_000_000, bytes_accessed=2_000_000
-    )(np.stack([real_forward(), real_inverse()]))
-    near = lax.ppermute(amplitude[32:48], BOTH, [(i, DEV - 1 - i) for i in range(DEV)])
-    far = lax.ppermute(amplitude[48:64], "row", [(i, 15 - i) for i in range(16)])
-    partner = lax.ppermute(
-        amplitude[0:1], BOTH, [(0, 64)] + [(i, DEV - i) for i in range(1, 64)]
-    )
-    slab, near, far, partner = lax.optimization_barrier((slab, near, far, partner))
-    far = lax.ppermute(far, "col", [(i, 7 - i) for i in range(8)])
-    weight = pl.pallas_call(
-        weights,
-        out_shape=jax.ShapeDtypeStruct((17, 128, 128), F32),
-        in_specs=[pl.BlockSpec(memory_space=pltpu.SMEM)] + [pl.BlockSpec(memory_space=pltpu.VMEM)] * 5,
-        scratch_shapes=[pltpu.VMEM((33 * 64, 128), F32)] * 3,
-        compiler_params=pltpu.CompilerParams(vmem_limit_bytes=24 << 20),
-        cost_estimate=pl.CostEstimate(flops=200_000_000, bytes_accessed=6_000_000, transcendentals=0),
-    )(d.astype(jnp.int32).reshape(1), amplitude, near, far, partner, reversal())
+    )(small)
+    tile_slot = catchment_rows(catch_id, owner_map, DEV).astype(jnp.int32)
+    device = d.astype(jnp.int32).reshape(1)
+    scalar, vector = pl.BlockSpec(memory_space=pltpu.SMEM), pl.BlockSpec(memory_space=pltpu.VMEM)
+
+    def weigh(body, blocks, *args):
+        return pl.pallas_call(
+            body,
+            out_shape=jax.ShapeDtypeStruct((blocks, 128, 128), F32),
+            in_specs=[scalar] + [vector] * len(args),
+            compiler_params=pltpu.CompilerParams(vmem_limit_bytes=24 << 20),
+            cost_estimate=pl.CostEstimate(flops=300_000_000, bytes_accessed=3_000_000, transcendentals=0),
+        )(device, *args)
+
+    flip = reversal()
+    near_weight = weigh(near_weights, 17 - FAR // 2, amplitude, near, partner.reshape(64, 128), flip)
+    far_weight = weigh(far_weights, FAR // 2, amplitude, far, flip)
 
     tw_row = row_twiddle()
     whole, forward_last, inverse_last = row_tables()
     spec = call(forward_rows, flat, [pltpu.VMEM((33 * 64, 256), F32)])(
         slab, forward_wide, tw_row, stacked(whole), stacked(forward_last)
     )
-    spec, far = lax.optimization_barrier((spec, far))
-    spec = lax.all_to_all(spec, BOTH, 0, 0, tiled=True)
+    spec, near_weight, far_weight, tile_slot, inverse_wide = lax.optimization_barrier(
+        (spec, near_weight, far_weight, tile_slot, inverse_wide)
+    )
+    spec = lax.all_to_all(spec, CORES, 0, 0, tiled=True)
     long, short = col_tables(-1.0)
     ilong, ishort = col_tables(1.0)
     tables = np.concatenate([stacked(table) for table in (long, ilong, short, ishort)], axis=0)
-    shaped = call(columns, flat)(spec, weight, col_twiddle(), tables)
-    shaped = lax.all_to_all(shaped, BOTH, 0, 0, tiled=True)
+    shaped = call(columns, flat)(spec, far_weight, near_weight, col_twiddle(), tables)
+    shaped = lax.all_to_all(shaped, CORES, 0, 0, tiled=True)
     slab_type = jax.ShapeDtypeStruct((8, 64, 1024), F32)
     field = call(inverse_rows, slab_type, [pltpu.VMEM((64 * 64, 128), F32)])(
         shaped, inverse_wide, tw_row, whole, inverse_last
     )
-    filtered = lax.all_to_all(field, "col", 0, 0, tiled=True)
-    tile_slot = catchment_rows(catch_id, owner_map, DEV)
-    state_new, sums = pl.pallas_call(
-        finish,
-        out_shape=[slab_type, jax.ShapeDtypeStruct((DEV, 128), F32)],
-        in_specs=[pl.BlockSpec(memory_space=pltpu.SMEM)] + [pl.BlockSpec(memory_space=pltpu.VMEM)] * 2,
+    filtered = lax.all_to_all(field, COL, 0, 0, tiled=True)
+    prev = state_prev.reshape(8, 64, 1024)
+    sums = pl.pallas_call(
+        tile_sums,
+        out_shape=jax.ShapeDtypeStruct((DEV, 128), F32),
+        in_specs=[scalar] + [vector] * 2,
         scratch_shapes=[pltpu.VMEM((8, 8, 128), F32)],
         compiler_params=pltpu.CompilerParams(vmem_limit_bytes=24 << 20),
-        cost_estimate=pl.CostEstimate(flops=5_000_000, bytes_accessed=6_000_000, transcendentals=500_000),
-    )(tile_slot.astype(jnp.int32), filtered, state_prev.reshape(8, 64, 1024))
+        cost_estimate=pl.CostEstimate(flops=5_000_000, bytes_accessed=4_000_000, transcendentals=500_000),
+    )(tile_slot, filtered, prev)
+    state_new = call(next_state, slab_type, flops=2_000_000)(filtered, prev)
     received = lax.all_to_all(sums.reshape(DEV, 1, 128), BOTH, 0, 0, tiled=True)
     slot_rain = received.sum(axis=(0, 1))[:CAP]
     shifted = jnp.concatenate(
@@ -434,18 +476,11 @@
 
 
 def solution(mesh):
+    chips = Mesh(mesh.devices.reshape(4, 4, 4, 2), BOTH)
     return jax.shard_map(
         shards,
-        mesh=mesh,
-        in_specs=(
-            P("row", "col"),
-            P(BOTH, None),
-            P("row", "col"),
-            P("row", "col"),
-            P(),
-            P(None, BOTH),
-            P(None, BOTH),
-        ),
-        out_specs=(P("row", "col"), P(None, BOTH)),
+        mesh=chips,
+        in_specs=(P(ROW, COL), P(BOTH, None), P(ROW, COL), P(ROW, COL), P(), P(None, BOTH), P(None, BOTH)),
+        out_specs=(P(ROW, COL), P(None, BOTH)),
         check_vma=False,
     )

time: 198 us -> 192 us (0.970)
  blocking collectives: 34.7 us -> 104 us
  waiting for transfers between devices: 76.6 us -> 27.4 us
  starting transfers between devices: 45 us -> 30.3 us
  local copies, waits for them, and re-layouts: 11.1 us -> 4.23 us
  Pallas kernels: 27.2 us -> 21.8 us
    all_to_all x1 -> x3, blocking collectives: 34.7 us -> 104 us  [the longest x1 37.9 us: shards(): spec = lax.all_to_all(spec, CORES, 0, 0, tiled=True)]
    all_to_all x3 -> x1, waiting for transfers between devices: 45.7 us -> 2.76 us  [shards(): lax.all_to_all(white_noise.reshape(8, 64, 1024), COL, 0, 0, tiled=True)]
    all_to_all x3 -> x1, starting transfers between devices: 23.2 us -> 6.96 us  [shards(): lax.all_to_all(white_noise.reshape(8, 64, 1024), COL, 0, 0, tiled=True)]
    unnamed x46 -> x34, local copies, waits for them, and re-layouts: 10.4 us -> 2.65 us
    pallas_call x3 -> x5, Pallas kernels: 17 us -> 11.5 us  [the longest x1 5.71 us: shards(): call(columns, flat)(spec, far_weight, near_weight, col_twiddle(), tables)]
    all_to_all x1, waiting for transfers between devices: 9.46 us -> 6.08 us  [shards(): received = lax.all_to_all(sums.reshape(DEV, 1, 128), BOTH, 0, 0, tiled=True)]
    ppermute x3, waiting for transfers between devices: 2.66 us -> 0.01 us  [the longest x1 0.01 us: shards(): lax.ppermute(amplitude[64 - FAR:64], ROW, [(i, 15 - i) for i in range(16)])]
  transfers between devices with their start and end apart: 8 -> 6, of which waited for: 6 -> 3; matrix products, arithmetic and copies ran while one was open for 1% -> 2% of each run, Pallas kernels for 7% -> 5%
where the time goes in v2:
time: 192 us
  blocking collectives  104 us (54%)
  starting transfers between devices  30.3 us (16%)
  waiting for transfers between devices  27.4 us (14%)
  Pallas kernels  21.8 us (11%)
  local copies, waits for them, and re-layouts  4.23 us (2%)
  other arithmetic  3.35 us (2%)
    all_to_all x1, blocking collectives, shards(): spec = lax.all_to_all(spec, CORES, 0, 0, tiled=True)  37.9 us
    all_to_all x1, blocking collectives, shards(): shaped = lax.all_to_all(shaped, CORES, 0, 0, tiled=True)  34.9 us
    all_to_all x1, blocking collectives, shards(): filtered = lax.all_to_all(field, COL, 0, 0, tiled=True)  31.2 us
    ppermute x1, waiting for transfers between devices, shards(): lax.ppermute(amplitude[0:1], BOTH, [(0, 64)] + [(i, DEV - i) for i in ran...  18.6 us
    ppermute x1, starting transfers between devices, shards(): lax.ppermute(amplitude[32:64 - FAR], BOTH, [(i, DEV - 1 - i) for i in ran...  7.49 us
    all_to_all x1, starting transfers between devices, shards(): lax.all_to_all(white_noise.reshape(8, 64, 1024), COL, 0, 0, tiled=True)  6.96 us
    ppermute x1, starting transfers between devices, shards(): lax.ppermute(amplitude[0:1], BOTH, [(0, 64)] + [(i, DEV - i) for i in ran...  6.12 us
    all_to_all x1, waiting for transfers between devices, shards(): received = lax.all_to_all(sums.reshape(DEV, 1, 128), BOTH, 0, 0, tiled=True)  6.08 us
  transfers between devices with their start and end apart: 6, of which 3 were waited for; matrix products, arithmetic and copies ran while one was open for 2% of the time, Pallas kernels for 5%

profile of v2, /device:TPU:1, one launch (start us, length us, event | category | flops | bytes accessed | tf_op | source)
XLA Modules:
  0.0 192.0 jit_solution(13565349451553398031)
XLA Ops:
  0.6 7.0 %all-to-all-start = ((f32[8,64,1024]{2,1,0:T(8,128)}), f32[8,64,1024]{2,1,0:T(8,128)}, u32[]{:S(2)}, u32[]{:S(2)}) async-start(f32[8,64,1024]{2,1,0:T(8,128)} %bitcast.23), calls=%async_computation | async-start | bytes 4194304 | tf_op jit(solution)/shard_map/all_to_all | solution.py:411
  7.6 0.9 slice.21
  8.5 7.5 %collective-permute-start = (f32[24,8192]{1,0:T(8,128)}, f32[24,8192]{1,0:T(8,128)S(1)}, u32[]{:S(2)}, u32[]{:S(2)}) collective-permute-start(f32[24,8192]{1,0:T(8,128)} %slice.21), channel_id=1, source_target_pairs={{0,127},{1,126},{2,125},{3,124},{4,123},{5,122},{6,121},{7,120},{8... | collective-permute-start | bytes 2359304 | tf_op jit(solution)/shard_map/ppermute | solution.py:413
  16.0 0.1 collective-permute-start.1
  16.2 6.1 %collective-permute-start.2 = (f32[1,8192]{1,0:T(1,128)S(1)}, f32[1,8192]{1,0:T(1,128)S(1)}, u32[]{:S(2)}, u32[]{:S(2)}) collective-permute-start(f32[1,8192]{1,0:T(1,128)S(1)} %slice.23), channel_id=1, source_target_pairs={{0,64},{1,127},{2,126},{3,125},{4,124},{5,123},{6,122},{7,121},{8,... | collective-permute-start | bytes 98312 | tf_op jit(solution)/shard_map/ppermute | solution.py:415
  22.3 0.1 copy.24
  22.4 0.3 fusion.1
  22.8 0.0 copy-start.12
  22.8 1.0 copy-done.12
  23.8 1.3 add_add_fusion
  25.1 0.0 copy-start.16
  25.1 0.0 copy-start.11
  25.1 0.0 copy-start.3
  25.1 0.3 copy.25
  25.5 0.6 fusion
  26.1 0.1 eq.38
  26.2 18.6 %collective-permute-done.2 = f32[1,8192]{1,0:T(1,128)S(1)} collective-permute-done((f32[1,8192]{1,0:T(1,128)S(1)}, f32[1,8192]{1,0:T(1,128)S(1)}, u32[]{:S(2)}, u32[]{:S(2)}) %collective-permute-start.2) | collective-permute-done | bytes 32800 | tf_op jit(solution)/shard_map/ppermute | solution.py:415
  44.8 0.0 collective-permute-done.1
  44.8 0.0 collective-permute-done.near_ref
  44.8 2.8 %all-to-all-done.x_ref = f32[8,64,1024]{2,1,0:T(8,128)} async-done(((f32[8,64,1024]{2,1,0:T(8,128)}), f32[8,64,1024]{2,1,0:T(8,128)}, u32[]{:S(2)}, u32[]{:S(2)}) %all-to-all-start) | async-done | bytes 2097184 | tf_op jit(solution)/shard_map/all_to_all | solution.py:411
  47.6 3.9 %collective-permute-start.3 = (f32[8,8192]{1,0:T(8,128)}, f32[8,8192]{1,0:T(8,128)S(1)}, u32[]{:S(2)}, u32[]{:S(2)}) collective-permute-start(f32[8,8192]{1,0:T(8,128)} %collective-permute-done.1), channel_id=1, source_target_pairs={{0,7},{1,6},{2,5},{3,4},{4,3},{5,2},{6,1},{7,0},{8,15},{9,14},{10,... | collective-permute-start | bytes 786440 | tf_op jit(solution)/shard_map/ppermute | solution.py:419
  51.4 0.2 select_reduce_fusion.slot_ref
  51.7 0.0 copy-start.6
  51.7 0.0 copy-start.9
  51.7 0.0 copy-start.10
  51.7 1.2 shard_map.167
  52.9 1.4 shard_map.169.near_ref
  54.4 5.3 %shard_map.168 = f32[128,32,128]{2,1,0:T(8,128)S(1)} custom-call(f32[8,64,1024]{2,1,0:T(8,128)} %all-to-all-done.x_ref, bf16[1024,512]{1,0:T(8,128)(2,1)S(1)} %get-tuple-element.14.wide_ref, f32[33,256]{1,0:T(8,128)S(1)} %copy-done.10, bf16[512,256]{1,0:T(8,128)(2,1)S(1)} %copy-done.6, bf16[512,128]{1,0:T(8,128)(2,1)S(1)} %copy-done.9), custom_call_target="tpu_custom_call" | custom-call | flops 2000000000 | bytes 6000000 | tf_op jit(solution)/shard_map/pallas_call | solution.py:442
  59.7 0.0 collective-permute-done.3.far_ref
  59.7 0.6 shard_map.170.far_ref
  60.4 0.0 copy-start.4
  60.4 0.0 copy-start.8
  60.4 37.9 %all_to_all.25.x_ref = f32[128,32,128]{2,1,0:T(8,128)S(1)} all-to-all(f32[128,32,128]{2,1,0:T(8,128)S(1)} %shard_map.168), channel_id=1, replica_groups=mesh['y'=4,'x'=4,'z'=4,'core'=2] {'core','y','x','z'}, dimensions={0} | all-to-all | bytes 4194304 | tf_op jit(solution)/shard_map/all_to_all | solution.py:448
  98.3 5.7 %shard_map.171 = f32[128,32,128]{2,1,0:T(8,128)S(1)} custom-call(f32[128,32,128]{2,1,0:T(8,128)S(1)} %all_to_all.25.x_ref, f32[4,128,128]{2,1,0:T(8,128)S(1)} %shard_map.170.far_ref, f32[13,128,128]{2,1,0:T(8,128)S(1)} %shard_map.169.near_ref, f32[128,256]{1,0:T(8,128)S(1)} %copy-done.8, bf16[2048,256]{1,0:T(8,128)(2,1)S(1)} %copy-done.4), custom_call_target="tpu_custom_call" | custom-call | flops 2000000000 | bytes 6000000 | tf_op jit(solution)/shard_map/pallas_call | solution.py:452
  104.0 0.0 copy-start.5
  104.0 0.0 copy-start.7
  104.0 34.9 %all_to_all.26.x_ref = f32[128,32,128]{2,1,0:T(8,128)S(1)} all-to-all(f32[128,32,128]{2,1,0:T(8,128)S(1)} %shard_map.171), channel_id=1, replica_groups=mesh['y'=4,'x'=4,'z'=4,'core'=2] {'core','y','x','z'}, dimensions={0} | all-to-all | bytes 4194304 | tf_op jit(solution)/shard_map/all_to_all | solution.py:453
  139.0 3.7 %shard_map.172 = f32[8,64,1024]{2,1,0:T(8,128)S(1)} custom-call(f32[128,32,128]{2,1,0:T(8,128)S(1)} %all_to_all.26.x_ref, bf16[1024,512]{1,0:T(8,128)(2,1)S(1)} %get-tuple-element.22.wide_ref, f32[33,256]{1,0:T(8,128)S(1)} %copy-done.10, bf16[256,512]{1,0:T(8,128)(2,1)S(1)} %copy-done.5, bf16[256,256]{1,0:T(8,128)(2,1)S(1)} %copy-done.7), custom_call_target="tpu_custom_call" | custom-call | flops 2000000000 | bytes 6000000 | tf_op jit(solution)/shard_map/pallas_call | solution.py:455
  142.7 0.0 copy-start.1
  142.7 31.2 %all_to_all.27.field_ref = f32[8,64,1024]{2,1,0:T(8,128)S(1)} all-to-all(f32[8,64,1024]{2,1,0:T(8,128)S(1)} %shard_map.172), channel_id=1, replica_groups=mesh['y'=4,'x'=4,'z'=4,'core'=2] {'z','core'}, dimensions={0} | all-to-all | bytes 4194304 | tf_op jit(solution)/shard_map/all_to_all | solution.py:458
  173.9 2.1 %shard_map.174 = f32[128,128]{1,0:T(8,128)} custom-call(s32[32]{0:T(128)S(1)} %select_reduce_fusion.slot_ref, f32[8,64,1024]{2,1,0:T(8,128)S(1)} %all_to_all.27.field_ref, f32[8,64,1024]{2,1,0:T(8,128)S(1)} %bitcast.19), custom_call_target="tpu_custom_call" | custom-call | flops 5000000 | bytes 4000000 | tf_op jit(solution)/shard_map/pallas_call | solution.py:460
  176.0 5.8 %all-to-all-start.4 = ((f32[128,1,128]{2,1,0:T(1,128)}), f32[128,1,128]{2,1,0:T(1,128)S(1)}, u32[]{:S(2)}, u32[]{:S(2)}) async-start(f32[128,1,128]{2,1,0:T(1,128)} %bitcast.11), calls=%async_computation.4 | async-start | bytes 131072 | tf_op jit(solution)/shard_map/all_to_all | solution.py:469
  181.8 0.1 slice.26
  181.8 1.6 copy-done.2
  183.4 1.6 shard_map.173
  185.1 6.1 %all-to-all-done.4 = f32[128,1,128]{2,1,0:T(1,128)S(1)} async-done(((f32[128,1,128]{2,1,0:T(1,128)}), f32[128,1,128]{2,1,0:T(1,128)S(1)}, u32[]{:S(2)}, u32[]{:S(2)}) %all-to-all-start.4) | async-done | bytes 65568 | tf_op jit(solution)/shard_map/all_to_all | solution.py:469
  191.2 0.2 reduce_sum.29
  191.3 0.7 multiply_add_fusion
  (26 shorter events, 0.1 us)
Async XLA Ops:
  0.6 7.0 %copy-start = (f32[64,8192]{1,0:T(8,128)S(1)}, f32[64,8192]{1,0:T(8,128)}, u32[]{:S(2)}) copy-start(f32[64,8192]{1,0:T(8,128)} %amp_ref.3) | copy-start | bytes 6291460
  0.6 46.9 %all-to-all-start = ((f32[8,64,1024]{2,1,0:T(8,128)}), f32[8,64,1024]{2,1,0:T(8,128)}, u32[]{:S(2)}, u32[]{:S(2)}) async-start(f32[8,64,1024]{2,1,0:T(8,128)} %bitcast.23), calls=%async_computation | async-start | bytes 4194304 | tf_op jit(solution)/shard_map/all_to_all | solution.py:411
  7.6 14.7 %copy-start.13 = (s32[2048,1]{0,1:T(1,128)S(1)}, s32[2048,1]{0,1:T(1,128)}, u32[]{:S(2)}) copy-start(s32[2048,1]{0,1:T(1,128)} %param.20) | copy-start | bytes 24580
  8.5 36.3 %collective-permute-start = (f32[24,8192]{1,0:T(8,128)}, f32[24,8192]{1,0:T(8,128)S(1)}, u32[]{:S(2)}, u32[]{:S(2)}) collective-permute-start(f32[24,8192]{1,0:T(8,128)} %slice.21), channel_id=1, source_target_pairs={{0,127},{1,126},{2,125},{3,124},{4,123},{5,122},{6,121},{7,120},{8... | collective-permute-start | bytes 2359304 | tf_op jit(solution)/shard_map/ppermute | solution.py:413
  16.0 28.7 %collective-permute-start.1 = (f32[8,8192]{1,0:T(8,128)S(1)}, f32[8,8192]{1,0:T(8,128)}, u32[]{:S(2)}, u32[]{:S(2)}) collective-permute-start(f32[8,8192]{1,0:T(8,128)S(1)} %slice.22), channel_id=1, source_target_pairs={{0,120},{8,112},{16,104},{24,96},{32,88},{40,80},{48,72},{56,64},{... | collective-permute-start | bytes 786440 | tf_op jit(solution)/shard_map/ppermute | solution.py:414
  16.2 28.6 %collective-permute-start.2 = (f32[1,8192]{1,0:T(1,128)S(1)}, f32[1,8192]{1,0:T(1,128)S(1)}, u32[]{:S(2)}, u32[]{:S(2)}) collective-permute-start(f32[1,8192]{1,0:T(1,128)S(1)} %slice.23), channel_id=1, source_target_pairs={{0,64},{1,127},{2,126},{3,125},{4,124},{5,123},{6,122},{7,121},{8,... | collective-permute-start | bytes 98312 | tf_op jit(solution)/shard_map/ppermute | solution.py:415
  22.8 1.0 copy-start.12
  25.1 1.0 copy-start.16
  25.1 26.6 %copy-start.11 = (bf16[2,64,128]{2,1,0:T(8,128)(2,1)S(1)}, bf16[2,64,128]{2,1,0:T(8,128)(2,1)}, u32[]{:S(2)}) copy-start(bf16[2,64,128]{2,1,0:T(8,128)(2,1)} %constant.52.clone.small_ref) | copy-start | bytes 98308
  25.1 27.8 %copy-start.3 = (bf16[128,384]{1,0:T(8,128)(2,1)S(1)}, bf16[128,384]{1,0:T(8,128)(2,1)}, u32[]{:S(2)}) copy-start(bf16[128,384]{1,0:T(8,128)(2,1)} %constant.53.clone.flip_ref) | copy-start | bytes 294916
  47.6 12.2 %collective-permute-start.3 = (f32[8,8192]{1,0:T(8,128)}, f32[8,8192]{1,0:T(8,128)S(1)}, u32[]{:S(2)}, u32[]{:S(2)}) collective-permute-start(f32[8,8192]{1,0:T(8,128)} %collective-permute-done.1), channel_id=1, source_target_pairs={{0,7},{1,6},{2,5},{3,4},{4,3},{5,2},{6,1},{7,0},{8,15},{9,14},{10,... | collective-permute-start | bytes 786440 | tf_op jit(solution)/shard_map/ppermute | solution.py:419
  51.7 2.7 %copy-start.6 = (bf16[512,256]{1,0:T(8,128)(2,1)S(1)}, bf16[512,256]{1,0:T(8,128)(2,1)}, u32[]{:S(2)}) copy-start(bf16[512,256]{1,0:T(8,128)(2,1)} %constant.55.clone.whole_ref) | copy-start | bytes 786436
  51.7 2.7 %copy-start.9 = (bf16[512,128]{1,0:T(8,128)(2,1)S(1)}, bf16[512,128]{1,0:T(8,128)(2,1)}, u32[]{:S(2)}) copy-start(bf16[512,128]{1,0:T(8,128)(2,1)} %constant.56.clone.last_ref) | copy-start | bytes 393220
  51.7 2.7 %copy-start.10 = (f32[33,256]{1,0:T(8,128)S(1)}, f32[33,256]{1,0:T(8,128)}, u32[]{:S(2)}) copy-start(f32[33,256]{1,0:T(8,128)} %constant.54.clone.tw_ref) | copy-start | bytes 101380
  60.4 37.9 %copy-start.4 = (bf16[2048,256]{1,0:T(8,128)(2,1)S(1)}, bf16[2048,256]{1,0:T(8,128)(2,1)}, u32[]{:S(2)}) copy-start(bf16[2048,256]{1,0:T(8,128)(2,1)} %constant.58.clone.table_ref) | copy-start | bytes 3145732
  60.4 37.9 %copy-start.8 = (f32[128,256]{1,0:T(8,128)S(1)}, f32[128,256]{1,0:T(8,128)}, u32[]{:S(2)}) copy-start(f32[128,256]{1,0:T(8,128)} %constant.57.clone.tw_ref) | copy-start | bytes 393220
  104.0 35.0 %copy-start.5 = (bf16[256,512]{1,0:T(8,128)(2,1)S(1)}, bf16[256,512]{1,0:T(8,128)(2,1)}, u32[]{:S(2)}) copy-start(bf16[256,512]{1,0:T(8,128)(2,1)} %constant.59.clone.whole_ref) | copy-start | bytes 786436
  104.0 35.0 %copy-start.7 = (bf16[256,256]{1,0:T(8,128)(2,1)S(1)}, bf16[256,256]{1,0:T(8,128)(2,1)}, u32[]{:S(2)}) copy-start(bf16[256,256]{1,0:T(8,128)(2,1)} %constant.60.clone.last_ref) | copy-start | bytes 393220
  142.7 31.2 %copy-start.1 = (f32[512,1024]{1,0:T(8,128)S(1)}, f32[512,1024]{1,0:T(8,128)}, u32[]{:S(2)}) copy-start(f32[512,1024]{1,0:T(8,128)} %param.18) | copy-start | bytes 6291460
  173.9 7.9 %copy-start.14 = (f32[288,32]{0,1:T(8,128)S(1)}, f32[288,32]{0,1:T(8,128)}, u32[]{:S(2)}) copy-start(f32[288,32]{0,1:T(8,128)} %param.22) | copy-start | bytes 110596
  176.0 15.2 %all-to-all-start.4 = ((f32[128,1,128]{2,1,0:T(1,128)}), f32[128,1,128]{2,1,0:T(1,128)S(1)}, u32[]{:S(2)}, u32[]{:S(2)}) async-start(f32[128,1,128]{2,1,0:T(1,128)} %bitcast.11), calls=%async_computation.4 | async-start | bytes 131072 | tf_op jit(solution)/shard_map/all_to_all | solution.py:469
  181.8 1.6 copy-start.2
  183.4 7.9 %copy-start.15 = (f32[288,32]{0,1:T(8,128)S(1)}, f32[288,32]{0,1:T(8,128)}, u32[]{:S(2)}) copy-start(f32[288,32]{0,1:T(8,128)} %param.21) | copy-start | bytes 110596

commit v3 on v2

--- a/solution.py
+++ b/solution.py
@@ -7,7 +7,6 @@
 from jax import lax
 from jax.experimental import pallas as pl
 from jax.experimental.pallas import tpu as pltpu
-from jax.sharding import Mesh
 from jax.sharding import PartitionSpec as P
 
 TILE = 128
@@ -15,12 +14,7 @@
 N = 8192
 DEV = 128
 FAR = 8
-ROW = ("y", "x")
-COL = ("z", "core")
-BOTH = ROW + COL
-CORES = ("core", "y", "x", "z")
-ORDER = [2 * (e % 64) + e // 64 for e in range(DEV)]
-PAIRS = ORDER + [DEV + e for e in ORDER]
+BOTH = ("row", "col")
 
 bump_height = 64.0
 persist = 0.8
@@ -92,15 +86,13 @@
     top[64] = cos[64]
     bottom[64] = 1.0
     inverse = np.concatenate([top, bottom], axis=0)
-    whole = np.block([[cos, sin], [-sin, cos]])
-    return [hi_lo(table[PAIRS]) for table in (whole, forward, inverse)]
+    return hi_lo(np.block([[cos, sin], [-sin, cos]])), hi_lo(forward), hi_lo(inverse)
 
 
 def col_tables(sign):
     turn = angle(np.arange(128), np.arange(128), 128)
     cos, sin = np.cos(turn), sign * np.sin(turn)
     long = np.block([[cos, -sin], [sin, cos]])
-    long = long[:, PAIRS] if sign < 0 else long[PAIRS]
     turn = angle(np.arange(64), np.arange(64), 64)
     cos, sin = np.kron(np.eye(2), np.cos(turn)), np.kron(np.eye(2), sign * np.sin(turn))
     short = np.block([[cos, sin], [-sin, cos]])
@@ -153,9 +145,20 @@
     )
 
 
-def forward_rows(x_ref, wide_ref, tw_ref, whole_ref, last_ref, out_ref, mid):
+def forward_rows(x_hbm, wide_hbm, tw_ref, whole_ref, last_ref, out_ref, mid, x_ref, wide_ref, sems):
+    def fetch(step):
+        rows = pl.ds(pl.multiple_of(step * 16, 16), 16)
+        return pltpu.make_async_copy(x_hbm.at[:, rows, :], x_ref.at[:, rows, :], sems.at[step])
+
+    table = pltpu.make_async_copy(wide_hbm, wide_ref, sems.at[4])
+    table.start()
+    for step in range(4):
+        fetch(step).start()
+    table.wait()
+
     def groups(step, carry):
         base = pl.multiple_of(step * 16, 16)
+        fetch(step).wait()
         left = [x_ref[c, pl.ds(base, 8), h * 128 : h * 128 + 128] for c in range(8) for h in range(8)]
         right = [x_ref[c, pl.ds(base + 8, 8), h * 128 : h * 128 + 128] for c in range(8) for h in range(8)]
         block = jnp.concatenate([jnp.concatenate(left, axis=0), jnp.concatenate(right, axis=0)], axis=1)
@@ -187,9 +190,9 @@
         if t == 7:
             rows = jnp.concatenate([jnp.zeros((192, 128), F32), mid[0:64, :128]], axis=0)
             other = table_times(last_ref, rows, ((1,), (1,)))
-            order = lax.broadcasted_iota(jnp.int32, (256, 256), 0) % 64
+            q = lax.broadcasted_iota(jnp.int32, (256, 256), 0) % 128
             lane = lax.broadcasted_iota(jnp.int32, (256, 256), 1)
-            value = jnp.where((order >= 32) & (lane >= 192), other, value)
+            value = jnp.where((q >= 64) & (lane >= 192), other, value)
         for u in range(2):
             reals.append(value[:128, u * 128 : u * 128 + 128])
             imags.append(value[128:, u * 128 : u * 128 + 128])
@@ -261,9 +264,9 @@
         joint = jnp.concatenate([real, imag], axis=0).T
         if t == 7:
             slot = lax.broadcasted_iota(jnp.int32, (256, 256), 0)
-            order = lax.broadcasted_iota(jnp.int32, (256, 256), 1) % 64
+            q = lax.broadcasted_iota(jnp.int32, (256, 256), 1) % 128
             mid[0:64, :] = times_table(joint[192:, :], last_ref)
-            joint = jnp.where((slot >= 192) & (order >= 32), 0.0, joint)
+            joint = jnp.where((slot >= 192) & (q >= 64), 0.0, joint)
         result = times_table(joint, whole_ref)
         for k in range(4):
             place(4 * t + k + 1, result[k * 64 : k * 64 + 64, :])
@@ -408,15 +411,13 @@
 def shards(white_noise, amplitude, state_prev, catch_id, owner_map, unit_graph, queue_prev):
     d = lax.axis_index(BOTH)
     flat = jax.ShapeDtypeStruct((DEV, 32, 128), F32)
-    slab = lax.all_to_all(white_noise.reshape(8, 64, 1024), COL, 0, 0, tiled=True)
+    slab = lax.all_to_all(white_noise.reshape(8, 64, 1024), "col", 0, 0, tiled=True)
     small = np.stack([real_forward(), real_inverse()])
     near = lax.ppermute(amplitude[32 : 64 - FAR], BOTH, [(i, DEV - 1 - i) for i in range(DEV)])
-    far = lax.ppermute(amplitude[64 - FAR : 64], ROW, [(i, 15 - i) for i in range(16)])
+    far = lax.ppermute(amplitude[64 - FAR : 64], "row", [(i, 15 - i) for i in range(16)])
     partner = lax.ppermute(
         amplitude[0:1], BOTH, [(0, 64)] + [(i, DEV - i) for i in range(1, 64)]
     )
-    slab, near, far, partner = lax.optimization_barrier((slab, near, far, partner))
-    far = lax.ppermute(far, COL, [(i, 7 - i) for i in range(8)])
     forward_wide, inverse_wide = call(
         widen, [jax.ShapeDtypeStruct((1024, 512), BF)] * 2, flops=100_000_000, bytes_accessed=2_000_000
     )(small)
@@ -435,27 +436,39 @@
 
     flip = reversal()
     near_weight = weigh(near_weights, 17 - FAR // 2, amplitude, near, partner.reshape(64, 128), flip)
+    slab, near_weight, far, tile_slot, forward_wide, inverse_wide = lax.optimization_barrier(
+        (slab, near_weight, far, tile_slot, forward_wide, inverse_wide)
+    )
+    far = lax.ppermute(far, "col", [(i, 7 - i) for i in range(8)])
     far_weight = weigh(far_weights, FAR // 2, amplitude, far, flip)
 
     tw_row = row_twiddle()
     whole, forward_last, inverse_last = row_tables()
-    spec = call(forward_rows, flat, [pltpu.VMEM((33 * 64, 256), F32)])(
-        slab, forward_wide, tw_row, stacked(whole), stacked(forward_last)
-    )
-    spec, near_weight, far_weight, tile_slot, inverse_wide = lax.optimization_barrier(
-        (spec, near_weight, far_weight, tile_slot, inverse_wide)
-    )
-    spec = lax.all_to_all(spec, CORES, 0, 0, tiled=True)
+    spec = pl.pallas_call(
+        forward_rows,
+        out_shape=flat,
+        in_specs=[pl.BlockSpec(memory_space=pl.ANY)] * 2 + [vector] * 3,
+        scratch_shapes=[
+            pltpu.VMEM((33 * 64, 256), F32),
+            pltpu.VMEM((8, 64, 1024), F32),
+            pltpu.VMEM((1024, 512), BF),
+            pltpu.SemaphoreType.DMA((5,)),
+        ],
+        compiler_params=pltpu.CompilerParams(vmem_limit_bytes=24 << 20),
+        cost_estimate=pl.CostEstimate(flops=2_000_000_000, bytes_accessed=6_000_000, transcendentals=0),
+    )(slab, forward_wide, tw_row, stacked(whole), stacked(forward_last))
+    spec, far_weight = lax.optimization_barrier((spec, far_weight))
+    spec = lax.all_to_all(spec, BOTH, 0, 0, tiled=True)
     long, short = col_tables(-1.0)
     ilong, ishort = col_tables(1.0)
     tables = np.concatenate([stacked(table) for table in (long, ilong, short, ishort)], axis=0)
     shaped = call(columns, flat)(spec, far_weight, near_weight, col_twiddle(), tables)
-    shaped = lax.all_to_all(shaped, CORES, 0, 0, tiled=True)
+    shaped = lax.all_to_all(shaped, BOTH, 0, 0, tiled=True)
     slab_type = jax.ShapeDtypeStruct((8, 64, 1024), F32)
     field = call(inverse_rows, slab_type, [pltpu.VMEM((64 * 64, 128), F32)])(
         shaped, inverse_wide, tw_row, whole, inverse_last
     )
-    filtered = lax.all_to_all(field, COL, 0, 0, tiled=True)
+    filtered = lax.all_to_all(field, "col", 0, 0, tiled=True)
     prev = state_prev.reshape(8, 64, 1024)
     sums = pl.pallas_call(
         tile_sums,
@@ -476,11 +489,18 @@
 
 
 def solution(mesh):
-    chips = Mesh(mesh.devices.reshape(4, 4, 4, 2), BOTH)
     return jax.shard_map(
         shards,
-        mesh=chips,
-        in_specs=(P(ROW, COL), P(BOTH, None), P(ROW, COL), P(ROW, COL), P(), P(None, BOTH), P(None, BOTH)),
-        out_specs=(P(ROW, COL), P(None, BOTH)),
+        mesh=mesh,
+        in_specs=(
+            P("row", "col"),
+            P(BOTH, None),
+            P("row", "col"),
+            P("row", "col"),
+            P(),
+            P(None, BOTH),
+            P(None, BOTH),
+        ),
+        out_specs=(P("row", "col"), P(None, BOTH)),
         check_vma=False,
     )

time: 192 us -> 191 us (level)
  starting transfers between devices: 30.3 us -> 24.4 us
  local copies, waits for them, and re-layouts: 4.23 us -> 9.86 us
  waiting for transfers between devices: 27.4 us -> 23.9 us
  blocking collectives: 104 us -> 106 us
    ppermute x1, waiting for transfers between devices: 18.6 us -> 12.4 us  [shards(): lax.ppermute(amplitude[0:1], BOTH, [(0, 64)] + [(i, DEV - i) for i in ran...]
    ppermute x1, starting transfers between devices: 6.12 us -> 1.66 us  [shards(): lax.ppermute(amplitude[0:1], BOTH, [(0, 64)] + [(i, DEV - i) for i in ran...]
    unnamed x34 -> x44, local copies, waits for them, and re-layouts: 2.65 us -> 6.87 us
    ppermute x2, waiting for transfers between devices: 0.01 us -> 2.67 us  [the longest x1 2.58 us: shards(): lax.ppermute(amplitude[64 - FAR:64], 'row', [(i, 15 - i) for i in range(1...]
  transfers between devices with their start and end apart: 6 -> 6, of which waited for: 3 -> 6; matrix products, arithmetic and copies ran while one was open for 2% -> 3% of each run, Pallas kernels for 5% -> 5%
where the time goes in v3:
time: 191 us; the launch traced here: 190 us
  blocking collectives  106 us (55%)
  starting transfers between devices  24.4 us (13%)
  waiting for transfers between devices  23.9 us (13%)
  Pallas kernels  21.2 us (11%)
  local copies, waits for them, and re-layouts  9.86 us (5%)
  other arithmetic  4.33 us (2%)
    all_to_all x1, blocking collectives, shards(): spec = lax.all_to_all(spec, BOTH, 0, 0, tiled=True)  40.8 us
    all_to_all x1, blocking collectives, shards(): shaped = lax.all_to_all(shaped, BOTH, 0, 0, tiled=True)  34.6 us
    all_to_all x1, blocking collectives, shards(): filtered = lax.all_to_all(field, 'col', 0, 0, tiled=True)  30.3 us
    ppermute x1, waiting for transfers between devices, shards(): lax.ppermute(amplitude[0:1], BOTH, [(0, 64)] + [(i, DEV - i) for i in ran...  12.4 us
    ppermute x1, starting transfers between devices, shards(): lax.ppermute(amplitude[32:64 - FAR], BOTH, [(i, DEV - 1 - i) for i in ran...  7.49 us
    all_to_all x1, starting transfers between devices, shards(): lax.all_to_all(white_noise.reshape(8, 64, 1024), 'col', 0, 0, tiled=True)  6.96 us
    unnamed x44, local copies, waits for them, and re-layouts  6.87 us
    all_to_all x1, waiting for transfers between devices, shards(): received = lax.all_to_all(sums.reshape(DEV, 1, 128), BOTH, 0, 0, tiled=True)  6.18 us
  transfers between devices with their start and end apart: 6, of which 6 were waited for; matrix products, arithmetic and copies ran while one was open for 3% of the time, Pallas kernels for 5%

profile of v3, /device:TPU:1, one launch (start us, length us, event | category | flops | bytes accessed | tf_op | source)
XLA Modules:
  0.0 190.2 jit_solution(7680114369922092526)
XLA Ops:
  0.6 7.0 %all-to-all-start = ((f32[8,64,1024]{2,1,0:T(8,128)}), f32[8,64,1024]{2,1,0:T(8,128)}, u32[]{:S(2)}, u32[]{:S(2)}) async-start(f32[8,64,1024]{2,1,0:T(8,128)} %bitcast.23), calls=%async_computation | async-start | bytes 4194304 | tf_op jit(solution)/shard_map/all_to_all | solution.py:414
  7.6 1.0 slice.21
  8.6 7.5 %collective-permute-start = (f32[24,8192]{1,0:T(8,128)}, f32[24,8192]{1,0:T(8,128)S(1)}, u32[]{:S(2)}, u32[]{:S(2)}) collective-permute-start(f32[24,8192]{1,0:T(8,128)} %slice.21), channel_id=1, source_target_pairs={{0,127},{1,126},{2,125},{3,124},{4,123},{5,122},{6,121},{7,120},{8... | collective-permute-start | bytes 2359304 | tf_op jit(solution)/shard_map/ppermute | solution.py:416
  16.1 1.7 collective-permute-start.1
  17.7 0.7 slice.23
  18.5 0.1 copy.24
  18.6 1.3 fusion.1
  19.9 0.7 slice_bitcast_fusion
  20.6 1.3 add_add_fusion
  21.9 0.0 copy-start.13
  21.9 0.0 copy-start.5
  21.9 0.3 copy.25
  22.3 0.6 fusion
  23.0 0.1 eq.38
  23.0 0.2 select_reduce_fusion.slot_ref
  23.3 0.0 copy-start.8
  23.3 0.0 copy-start.12
  23.3 1.2 shard_map.168
  24.5 1.0 copy-done.14
  25.5 1.0 copy-done.16
  26.4 12.4 %collective-permute-done.1 = f32[1,8192]{1,0:T(1,128)S(1)} collective-permute-done((f32[1,8192]{1,0:T(1,128)S(1)}, f32[1,8192]{1,0:T(1,128)S(1)}, u32[]{:S(2)}, u32[]{:S(2)}) %collective-permute-start.1) | collective-permute-done | bytes 32800 | tf_op jit(solution)/shard_map/ppermute | solution.py:418
  38.8 0.8 collective-permute-done.near_ref
  39.6 0.9 copy-done.3
  40.5 1.1 copy-done.4
  41.7 1.5 shard_map.167.near_ref
  43.1 2.6 %collective-permute-done.2 = f32[8,8192]{1,0:T(8,128)} collective-permute-done((f32[8,8192]{1,0:T(8,128)}, f32[8,8192]{1,0:T(8,128)}, u32[]{:S(2)}, u32[]{:S(2)}) %collective-permute-start.2) | collective-permute-done | bytes 262176 | tf_op jit(solution)/shard_map/ppermute | solution.py:417
  45.7 1.8 all-to-all-done.x_hbm
  47.6 3.9 %collective-permute-start.3 = (f32[8,8192]{1,0:T(8,128)}, f32[8,8192]{1,0:T(8,128)S(1)}, u32[]{:S(2)}, u32[]{:S(2)}) collective-permute-start(f32[8,8192]{1,0:T(8,128)} %collective-permute-done.2), channel_id=1, source_target_pairs={{0,7},{1,6},{2,5},{3,4},{4,3},{5,2},{6,1},{7,0},{8,15},{9,14},{10,... | collective-permute-start | bytes 786440 | tf_op jit(solution)/shard_map/ppermute | solution.py:442
  51.4 1.2 copy-done.17
  52.7 4.9 %shard_map.169 = f32[128,32,128]{2,1,0:T(8,128)S(1)} custom-call(f32[8,64,1024]{2,1,0:T(8,128)} %all-to-all-done.x_hbm, bf16[1024,512]{1,0:T(8,128)(2,1)S(1)} %copy-done.17, f32[33,256]{1,0:T(8,128)S(1)} %copy-done.12, bf16[512,256]{1,0:T(8,128)(2,1)S(1)} %copy-done.8, bf16[512,128]{1,0:T(8,128)(2,1)S(1)} %copy-done.11), custom_call_target="tpu_custom_call" | custom-call | flops 2000000000 | bytes 6000000 | tf_op jit(solution)/shard_map/pallas_call | solution.py:447
  57.6 0.1 collective-permute-done.3.far_ref
  57.7 0.6 shard_map.170.far_ref
  58.3 0.0 copy-start.6
  58.3 0.0 copy-start.10
  58.3 40.8 %all_to_all.25.x_ref = f32[128,32,128]{2,1,0:T(8,128)S(1)} all-to-all(f32[128,32,128]{2,1,0:T(8,128)S(1)} %shard_map.169), channel_id=1, replica_groups=mesh['row'=16,'col'=8] {'row','col'}, dimensions={0} | all-to-all | bytes 4194304 | tf_op jit(solution)/shard_map/all_to_all | solution.py:461
  99.1 5.6 %shard_map.171 = f32[128,32,128]{2,1,0:T(8,128)S(1)} custom-call(f32[128,32,128]{2,1,0:T(8,128)S(1)} %all_to_all.25.x_ref, f32[4,128,128]{2,1,0:T(8,128)S(1)} %shard_map.170.far_ref, f32[13,128,128]{2,1,0:T(8,128)S(1)} %shard_map.167.near_ref, f32[128,256]{1,0:T(8,128)S(1)} %copy-done.10, bf16[2048,256]{1,0:T(8,128)(2,1)S(1)} %copy-done.6), custom_call_target="tpu_custom_call" | custom-call | flops 2000000000 | bytes 6000000 | tf_op jit(solution)/shard_map/pallas_call | solution.py:465
  104.7 0.0 copy-start.9
  104.7 34.6 %all_to_all.26.x_ref = f32[128,32,128]{2,1,0:T(8,128)S(1)} all-to-all(f32[128,32,128]{2,1,0:T(8,128)S(1)} %shard_map.171), channel_id=1, replica_groups=mesh['row'=16,'col'=8] {'row','col'}, dimensions={0} | all-to-all | bytes 4194304 | tf_op jit(solution)/shard_map/all_to_all | solution.py:466
  139.3 3.7 %shard_map.172 = f32[8,64,1024]{2,1,0:T(8,128)S(1)} custom-call(f32[128,32,128]{2,1,0:T(8,128)S(1)} %all_to_all.26.x_ref, bf16[1024,512]{1,0:T(8,128)(2,1)S(1)} %copy-done.15, f32[33,256]{1,0:T(8,128)S(1)} %copy-done.12, bf16[256,512]{1,0:T(8,128)(2,1)S(1)} %copy-done.7, bf16[256,256]{1,0:T(8,128)(2,1)S(1)} %copy-done.9), custom_call_target="tpu_custom_call" | custom-call | flops 2000000000 | bytes 6000000 | tf_op jit(solution)/shard_map/pallas_call | solution.py:468
  143.0 30.3 %all_to_all.27.field_ref = f32[8,64,1024]{2,1,0:T(8,128)S(1)} all-to-all(f32[8,64,1024]{2,1,0:T(8,128)S(1)} %shard_map.172), channel_id=1, replica_groups=mesh['row'=16,'col'=8] {'col'}, dimensions={0} | all-to-all | bytes 4194304 | tf_op jit(solution)/shard_map/all_to_all | solution.py:471
  173.3 2.1 %shard_map.174 = f32[128,128]{1,0:T(8,128)} custom-call(s32[32]{0:T(128)S(1)} %select_reduce_fusion.slot_ref, f32[8,64,1024]{2,1,0:T(8,128)S(1)} %all_to_all.27.field_ref, f32[8,64,1024]{2,1,0:T(8,128)S(1)} %bitcast.19), custom_call_target="tpu_custom_call" | custom-call | flops 5000000 | bytes 4000000 | tf_op jit(solution)/shard_map/pallas_call | solution.py:473
  175.4 4.4 %all-to-all-start.4 = ((f32[128,1,128]{2,1,0:T(1,128)}), f32[128,1,128]{2,1,0:T(1,128)S(1)}, u32[]{:S(2)}, u32[]{:S(2)}) async-start(f32[128,1,128]{2,1,0:T(1,128)} %bitcast.11), calls=%async_computation.4 | async-start | bytes 131072 | tf_op jit(solution)/shard_map/all_to_all | solution.py:482
  179.8 0.1 slice.26
  179.9 1.6 copy-done.2
  181.5 1.6 shard_map.173
  183.2 6.2 %all-to-all-done.4 = f32[128,1,128]{2,1,0:T(1,128)S(1)} async-done(((f32[128,1,128]{2,1,0:T(1,128)}), f32[128,1,128]{2,1,0:T(1,128)S(1)}, u32[]{:S(2)}, u32[]{:S(2)}) %all-to-all-start.4) | async-done | bytes 65568 | tf_op jit(solution)/shard_map/all_to_all | solution.py:482
  189.3 0.2 reduce_sum.29
  189.5 0.7 multiply_add_fusion
  (36 shorter events, 0.1 us)
Async XLA Ops:
  0.6 7.0 %copy-start = (f32[64,8192]{1,0:T(8,128)S(1)}, f32[64,8192]{1,0:T(8,128)}, u32[]{:S(2)}) copy-start(f32[64,8192]{1,0:T(8,128)} %amp_ref.3) | copy-start | bytes 6291460
  0.6 46.9 %all-to-all-start = ((f32[8,64,1024]{2,1,0:T(8,128)}), f32[8,64,1024]{2,1,0:T(8,128)}, u32[]{:S(2)}, u32[]{:S(2)}) async-start(f32[8,64,1024]{2,1,0:T(8,128)} %bitcast.23), calls=%async_computation | async-start | bytes 4194304 | tf_op jit(solution)/shard_map/all_to_all | solution.py:414
  7.6 10.9 %copy-start.18 = (s32[2048,1]{0,1:T(1,128)S(1)}, s32[2048,1]{0,1:T(1,128)}, u32[]{:S(2)}) copy-start(s32[2048,1]{0,1:T(1,128)} %param.20) | copy-start | bytes 24580
  8.6 31.1 %collective-permute-start = (f32[24,8192]{1,0:T(8,128)}, f32[24,8192]{1,0:T(8,128)S(1)}, u32[]{:S(2)}, u32[]{:S(2)}) collective-permute-start(f32[24,8192]{1,0:T(8,128)} %slice.21), channel_id=1, source_target_pairs={{0,127},{1,126},{2,125},{3,124},{4,123},{5,122},{6,121},{7,120},{8... | collective-permute-start | bytes 2359304 | tf_op jit(solution)/shard_map/ppermute | solution.py:416
  16.1 22.8 %collective-permute-start.1 = (f32[1,8192]{1,0:T(1,128)S(1)}, f32[1,8192]{1,0:T(1,128)S(1)}, u32[]{:S(2)}, u32[]{:S(2)}) collective-permute-start(f32[1,8192]{1,0:T(1,128)S(1)} %slice.22), channel_id=1, source_target_pairs={{0,64},{1,127},{2,126},{3,125},{4,124},{5,123},{6,122},{7,121},{8,... | collective-permute-start | bytes 98312 | tf_op jit(solution)/shard_map/ppermute | solution.py:418
  18.5 27.3 %collective-permute-start.2 = (f32[8,8192]{1,0:T(8,128)}, f32[8,8192]{1,0:T(8,128)}, u32[]{:S(2)}, u32[]{:S(2)}) collective-permute-start(f32[8,8192]{1,0:T(8,128)} %slice.23), channel_id=1, source_target_pairs={{0,120},{8,112},{16,104},{24,96},{32,88},{40,80},{48,72},{56,64},{... | collective-permute-start | bytes 786440 | tf_op jit(solution)/shard_map/ppermute | solution.py:417
  21.9 1.0 copy-start.21
  21.9 1.3 copy-start.13
  21.9 18.6 %copy-start.5 = (bf16[128,384]{1,0:T(8,128)(2,1)S(1)}, bf16[128,384]{1,0:T(8,128)(2,1)}, u32[]{:S(2)}) copy-start(bf16[128,384]{1,0:T(8,128)(2,1)} %constant.44.clone.flip_ref) | copy-start | bytes 294916
  23.3 28.2 %copy-start.8 = (bf16[512,256]{1,0:T(8,128)(2,1)S(1)}, bf16[512,256]{1,0:T(8,128)(2,1)}, u32[]{:S(2)}) copy-start(bf16[512,256]{1,0:T(8,128)(2,1)} %constant.46.clone.whole_ref) | copy-start | bytes 786436
  23.3 28.2 %copy-start.12 = (f32[33,256]{1,0:T(8,128)S(1)}, f32[33,256]{1,0:T(8,128)}, u32[]{:S(2)}) copy-start(f32[33,256]{1,0:T(8,128)} %constant.45.clone.tw_ref) | copy-start | bytes 101380
  24.5 1.0 copy-start.14
  25.5 1.0 copy-start.16
  39.6 0.9 copy-start.3
  40.5 1.1 copy-start.4
  41.7 9.8 %copy-start.11 = (bf16[512,128]{1,0:T(8,128)(2,1)S(1)}, bf16[512,128]{1,0:T(8,128)(2,1)}, u32[]{:S(2)}) copy-start(bf16[512,128]{1,0:T(8,128)(2,1)} %constant.47.clone.last_ref) | copy-start | bytes 393220
  47.6 10.1 %collective-permute-start.3 = (f32[8,8192]{1,0:T(8,128)}, f32[8,8192]{1,0:T(8,128)S(1)}, u32[]{:S(2)}, u32[]{:S(2)}) collective-permute-start(f32[8,8192]{1,0:T(8,128)} %collective-permute-done.2), channel_id=1, source_target_pairs={{0,7},{1,6},{2,5},{3,4},{4,3},{5,2},{6,1},{7,0},{8,15},{9,14},{10,... | collective-permute-start | bytes 786440 | tf_op jit(solution)/shard_map/ppermute | solution.py:442
  51.4 1.2 copy-start.17
  58.3 40.8 %copy-start.6 = (bf16[2048,256]{1,0:T(8,128)(2,1)S(1)}, bf16[2048,256]{1,0:T(8,128)(2,1)}, u32[]{:S(2)}) copy-start(bf16[2048,256]{1,0:T(8,128)(2,1)} %constant.49.clone.table_ref) | copy-start | bytes 3145732
  58.3 40.8 %copy-start.10 = (f32[128,256]{1,0:T(8,128)S(1)}, f32[128,256]{1,0:T(8,128)}, u32[]{:S(2)}) copy-start(f32[128,256]{1,0:T(8,128)} %constant.48.clone.tw_ref) | copy-start | bytes 393220
  104.7 34.6 %copy-start.7 = (bf16[256,512]{1,0:T(8,128)(2,1)S(1)}, bf16[256,512]{1,0:T(8,128)(2,1)}, u32[]{:S(2)}) copy-start(bf16[256,512]{1,0:T(8,128)(2,1)} %constant.50.clone.whole_ref) | copy-start | bytes 786436
  104.7 34.6 %copy-start.9 = (bf16[256,256]{1,0:T(8,128)(2,1)S(1)}, bf16[256,256]{1,0:T(8,128)(2,1)}, u32[]{:S(2)}) copy-start(bf16[256,256]{1,0:T(8,128)(2,1)} %constant.51.clone.last_ref) | copy-start | bytes 393220
  104.7 34.6 %copy-start.15 = (bf16[1024,512]{1,0:T(8,128)(2,1)S(1)}, bf16[1024,512]{1,0:T(8,128)(2,1)}, u32[]{:S(2)}) copy-start(bf16[1024,512]{1,0:T(8,128)(2,1)} %copy-done.14) | copy-start | bytes 3145732
  143.0 30.3 %copy-start.1 = (f32[512,1024]{1,0:T(8,128)S(1)}, f32[512,1024]{1,0:T(8,128)}, u32[]{:S(2)}) copy-start(f32[512,1024]{1,0:T(8,128)} %param.18) | copy-start | bytes 6291460
  173.3 6.5 %copy-start.19 = (f32[288,32]{0,1:T(8,128)S(1)}, f32[288,32]{0,1:T(8,128)}, u32[]{:S(2)}) copy-start(f32[288,32]{0,1:T(8,128)} %param.22) | copy-start | bytes 110596
  175.4 13.9 %all-to-all-start.4 = ((f32[128,1,128]{2,1,0:T(1,128)}), f32[128,1,128]{2,1,0:T(1,128)S(1)}, u32[]{:S(2)}, u32[]{:S(2)}) async-start(f32[128,1,128]{2,1,0:T(1,128)} %bitcast.11), calls=%async_computation.4 | async-start | bytes 131072 | tf_op jit(solution)/shard_map/all_to_all | solution.py:482
  179.9 1.6 copy-start.2
  181.5 8.0 %copy-start.20 = (f32[288,32]{0,1:T(8,128)S(1)}, f32[288,32]{0,1:T(8,128)}, u32[]{:S(2)}) copy-start(f32[288,32]{0,1:T(8,128)} %param.21) | copy-start | bytes 110596

commit v4 on v3

--- a/solution.py
+++ b/solution.py
@@ -425,7 +425,7 @@
     device = d.astype(jnp.int32).reshape(1)
     scalar, vector = pl.BlockSpec(memory_space=pltpu.SMEM), pl.BlockSpec(memory_space=pltpu.VMEM)
 
-    def weigh(body, blocks, *args):
+    def weigh(body, device, blocks, *args):
         return pl.pallas_call(
             body,
             out_shape=jax.ShapeDtypeStruct((blocks, 128, 128), F32),
@@ -435,19 +435,18 @@
         )(device, *args)
 
     flip = reversal()
-    near_weight = weigh(near_weights, 17 - FAR // 2, amplitude, near, partner.reshape(64, 128), flip)
-    slab, near_weight, far, tile_slot, forward_wide, inverse_wide = lax.optimization_barrier(
-        (slab, near_weight, far, tile_slot, forward_wide, inverse_wide)
-    )
+    near, far, partner, tile_slot, forward_wide, inverse_wide = lax.optimization_barrier(
+        (near, far, partner, tile_slot, forward_wide, inverse_wide)
+    )
+    near_weight = weigh(near_weights, device, 17 - FAR // 2, amplitude, near, partner.reshape(64, 128), flip)
     far = lax.ppermute(far, "col", [(i, 7 - i) for i in range(8)])
-    far_weight = weigh(far_weights, FAR // 2, amplitude, far, flip)
-
+    slab, near_weight = lax.optimization_barrier((slab, near_weight))
     tw_row = row_twiddle()
     whole, forward_last, inverse_last = row_tables()
     spec = pl.pallas_call(
         forward_rows,
         out_shape=flat,
-        in_specs=[pl.BlockSpec(memory_space=pl.ANY)] * 2 + [vector] * 3,
+        in_specs=[pl.BlockSpec(memory_space=pltpu.MemorySpace.HBM)] * 2 + [vector] * 3,
         scratch_shapes=[
             pltpu.VMEM((33 * 64, 256), F32),
             pltpu.VMEM((8, 64, 1024), F32),
@@ -457,6 +456,8 @@
         compiler_params=pltpu.CompilerParams(vmem_limit_bytes=24 << 20),
         cost_estimate=pl.CostEstimate(flops=2_000_000_000, bytes_accessed=6_000_000, transcendentals=0),
     )(slab, forward_wide, tw_row, stacked(whole), stacked(forward_last))
+    spec, device = lax.optimization_barrier((spec, device))
+    far_weight = weigh(far_weights, device, FAR // 2, amplitude, far, flip)
     spec, far_weight = lax.optimization_barrier((spec, far_weight))
     spec = lax.all_to_all(spec, BOTH, 0, 0, tiled=True)
     long, short = col_tables(-1.0)

time: 191 us -> 188 us (0.984)
  waiting for transfers between devices: 23.9 us -> 19.4 us
    ppermute x1, starting transfers between devices: 1.66 us -> 6.12 us  [shards(): lax.ppermute(amplitude[0:1], BOTH, [(0, 64)] + [(i, DEV - i) for i in ran...]
    ppermute x1, starting transfers between devices: 3.88 us -> 0.01 us  [shards(): far = lax.ppermute(far, 'col', [(i, 7 - i) for i in range(8)])]
    ppermute x1, waiting for transfers between devices: 2.58 us -> 0.01 us  [shards(): lax.ppermute(amplitude[64 - FAR:64], 'row', [(i, 15 - i) for i in range(1...]
  transfers between devices with their start and end apart: 6 -> 6, of which waited for: 6 -> 3; matrix products, arithmetic and copies ran while one was open for 3% -> 4% of each run, Pallas kernels for 5% -> 5%
where the time goes in v4:
time: 188 us
  blocking collectives  105 us (56%)
  starting transfers between devices  25 us (13%)
  Pallas kernels  21.2 us (11%)
  waiting for transfers between devices  19.4 us (10%)
  local copies, waits for them, and re-layouts  11.1 us (6%)
  other arithmetic  5.56 us (3%)
    all_to_all x1, blocking collectives, shards(): spec = lax.all_to_all(spec, BOTH, 0, 0, tiled=True)  39.7 us
    all_to_all x1, blocking collectives, shards(): shaped = lax.all_to_all(shaped, BOTH, 0, 0, tiled=True)  34.6 us
    all_to_all x1, blocking collectives, shards(): filtered = lax.all_to_all(field, 'col', 0, 0, tiled=True)  30.3 us
    ppermute x1, waiting for transfers between devices, shards(): lax.ppermute(amplitude[0:1], BOTH, [(0, 64)] + [(i, DEV - i) for i in ran...  12.4 us
    unnamed x44, local copies, waits for them, and re-layouts  7.82 us
    ppermute x1, starting transfers between devices, shards(): lax.ppermute(amplitude[32:64 - FAR], BOTH, [(i, DEV - 1 - i) for i in ran...  7.49 us
    all_to_all x1, starting transfers between devices, shards(): lax.all_to_all(white_noise.reshape(8, 64, 1024), 'col', 0, 0, tiled=True)  6.96 us
    all_to_all x1, waiting for transfers between devices, shards(): received = lax.all_to_all(sums.reshape(DEV, 1, 128), BOTH, 0, 0, tiled=True)  6.18 us
  transfers between devices with their start and end apart: 6, of which 3 were waited for; matrix products, arithmetic and copies ran while one was open for 4% of the time, Pallas kernels for 5%

profile of v4, /device:TPU:1, one launch (start us, length us, event | category | flops | bytes accessed | tf_op | source)
XLA Modules:
  0.0 187.7 jit_solution(6829521896552134711)
XLA Ops:
  0.6 7.0 %all-to-all-start = ((f32[8,64,1024]{2,1,0:T(8,128)}), f32[8,64,1024]{2,1,0:T(8,128)}, u32[]{:S(2)}, u32[]{:S(2)}) async-start(f32[8,64,1024]{2,1,0:T(8,128)} %bitcast.23), calls=%async_computation | async-start | bytes 4194304 | tf_op jit(solution)/shard_map/all_to_all | solution.py:414
  7.6 1.0 slice.21
  8.6 7.5 %collective-permute-start = (f32[24,8192]{1,0:T(8,128)}, f32[24,8192]{1,0:T(8,128)S(1)}, u32[]{:S(2)}, u32[]{:S(2)}) collective-permute-start(f32[24,8192]{1,0:T(8,128)} %slice.21), channel_id=1, source_target_pairs={{0,127},{1,126},{2,125},{3,124},{4,123},{5,122},{6,121},{7,120},{8... | collective-permute-start | bytes 2359304 | tf_op jit(solution)/shard_map/ppermute | solution.py:416
  16.1 0.1 collective-permute-start.1
  16.2 6.1 %collective-permute-start.2 = (f32[1,8192]{1,0:T(1,128)S(1)}, f32[1,8192]{1,0:T(1,128)S(1)}, u32[]{:S(2)}, u32[]{:S(2)}) collective-permute-start(f32[1,8192]{1,0:T(1,128)S(1)} %slice.23), channel_id=1, source_target_pairs={{0,64},{1,127},{2,126},{3,125},{4,124},{5,123},{6,122},{7,121},{8,... | collective-permute-start | bytes 98312 | tf_op jit(solution)/shard_map/ppermute | solution.py:418
  22.3 0.1 copy.24
  22.4 1.3 fusion.1
  23.7 0.7 slice_bitcast_fusion
  24.5 1.3 add_add_fusion
  25.8 0.0 copy-start.13
  25.8 0.0 copy-start.5
  25.8 1.3 copy.25
  27.1 0.1 eq.38
  27.2 1.9 fusion
  29.1 0.2 select_reduce_fusion.slot_ref
  29.3 0.0 copy-start.11
  29.3 0.0 copy-start.12
  29.3 1.2 shard_map.167
  30.5 1.0 copy-done.14
  31.5 1.0 copy-done.16
  32.5 12.4 %collective-permute-done.2 = f32[1,8192]{1,0:T(1,128)S(1)} collective-permute-done((f32[1,8192]{1,0:T(1,128)S(1)}, f32[1,8192]{1,0:T(1,128)S(1)}, u32[]{:S(2)}, u32[]{:S(2)}) %collective-permute-start.2) | collective-permute-done | bytes 32800 | tf_op jit(solution)/shard_map/ppermute | solution.py:418
  44.8 0.9 copy-done.3
  45.7 1.1 copy-done.4
  46.9 1.5 shard_map.168.near_ref
  48.4 0.0 copy-start.8
  48.4 0.9 copy-done.8
  49.3 1.2 copy-done.17
  50.6 4.9 %shard_map.169 = f32[128,32,128]{2,1,0:T(8,128)S(1)} custom-call(f32[8,64,1024]{2,1,0:T(8,128)} %all-to-all-done.x_hbm, bf16[1024,512]{1,0:T(8,128)(2,1)S(1)} %copy-done.17, f32[33,256]{1,0:T(8,128)S(1)} %copy-done.12, bf16[512,256]{1,0:T(8,128)(2,1)S(1)} %copy-done.8, bf16[512,128]{1,0:T(8,128)(2,1)S(1)} %copy-done.11), custom_call_target="tpu_custom_call" | custom-call | flops 2000000000 | bytes 6000000 | tf_op jit(solution)/shard_map/pallas_call | solution.py:446
  55.5 0.8 collective-permute-done.3.far_ref
  56.3 0.7 shard_map.170.far_ref
  56.9 0.0 copy-start.6
  57.0 0.0 copy-start.10
  57.0 39.7 %all_to_all.25.x_ref = f32[128,32,128]{2,1,0:T(8,128)S(1)} all-to-all(f32[128,32,128]{2,1,0:T(8,128)S(1)} %shard_map.169), channel_id=1, replica_groups=mesh['row'=16,'col'=8] {'row','col'}, dimensions={0} | all-to-all | bytes 4194304 | tf_op jit(solution)/shard_map/all_to_all | solution.py:462
  96.7 5.6 %shard_map.171 = f32[128,32,128]{2,1,0:T(8,128)S(1)} custom-call(f32[128,32,128]{2,1,0:T(8,128)S(1)} %all_to_all.25.x_ref, f32[4,128,128]{2,1,0:T(8,128)S(1)} %shard_map.170.far_ref, f32[13,128,128]{2,1,0:T(8,128)S(1)} %shard_map.168.near_ref, f32[128,256]{1,0:T(8,128)S(1)} %copy-done.10, bf16[2048,256]{1,0:T(8,128)(2,1)S(1)} %copy-done.6), custom_call_target="tpu_custom_call" | custom-call | flops 2000000000 | bytes 6000000 | tf_op jit(solution)/shard_map/pallas_call | solution.py:466
  102.2 0.0 copy-start.7
  102.3 0.0 copy-start.9
  102.3 34.6 %all_to_all.26.x_ref = f32[128,32,128]{2,1,0:T(8,128)S(1)} all-to-all(f32[128,32,128]{2,1,0:T(8,128)S(1)} %shard_map.171), channel_id=1, replica_groups=mesh['row'=16,'col'=8] {'row','col'}, dimensions={0} | all-to-all | bytes 4194304 | tf_op jit(solution)/shard_map/all_to_all | solution.py:467
  136.9 3.7 %shard_map.172 = f32[8,64,1024]{2,1,0:T(8,128)S(1)} custom-call(f32[128,32,128]{2,1,0:T(8,128)S(1)} %all_to_all.26.x_ref, bf16[1024,512]{1,0:T(8,128)(2,1)S(1)} %copy-done.15, f32[33,256]{1,0:T(8,128)S(1)} %copy-done.12, bf16[256,512]{1,0:T(8,128)(2,1)S(1)} %copy-done.7, bf16[256,256]{1,0:T(8,128)(2,1)S(1)} %copy-done.9), custom_call_target="tpu_custom_call" | custom-call | flops 2000000000 | bytes 6000000 | tf_op jit(solution)/shard_map/pallas_call | solution.py:469
  140.6 0.0 copy-start.1
  140.6 30.3 %all_to_all.27.field_ref = f32[8,64,1024]{2,1,0:T(8,128)S(1)} all-to-all(f32[8,64,1024]{2,1,0:T(8,128)S(1)} %shard_map.172), channel_id=1, replica_groups=mesh['row'=16,'col'=8] {'col'}, dimensions={0} | all-to-all | bytes 4194304 | tf_op jit(solution)/shard_map/all_to_all | solution.py:472
  170.9 2.1 %shard_map.174 = f32[128,128]{1,0:T(8,128)} custom-call(s32[32]{0:T(128)S(1)} %select_reduce_fusion.slot_ref, f32[8,64,1024]{2,1,0:T(8,128)S(1)} %all_to_all.27.field_ref, f32[8,64,1024]{2,1,0:T(8,128)S(1)} %bitcast.19), custom_call_target="tpu_custom_call" | custom-call | flops 5000000 | bytes 4000000 | tf_op jit(solution)/shard_map/pallas_call | solution.py:474
  173.0 4.4 %all-to-all-start.4 = ((f32[128,1,128]{2,1,0:T(1,128)}), f32[128,1,128]{2,1,0:T(1,128)S(1)}, u32[]{:S(2)}, u32[]{:S(2)}) async-start(f32[128,1,128]{2,1,0:T(1,128)} %bitcast.11), calls=%async_computation.4 | async-start | bytes 131072 | tf_op jit(solution)/shard_map/all_to_all | solution.py:483
  177.4 0.1 slice.26
  177.5 1.6 copy-done.2
  179.1 1.6 shard_map.173
  180.7 6.2 %all-to-all-done.4 = f32[128,1,128]{2,1,0:T(1,128)S(1)} async-done(((f32[128,1,128]{2,1,0:T(1,128)}), f32[128,1,128]{2,1,0:T(1,128)S(1)}, u32[]{:S(2)}, u32[]{:S(2)}) %all-to-all-start.4) | async-done | bytes 65568 | tf_op jit(solution)/shard_map/all_to_all | solution.py:483
  186.9 0.2 reduce_sum.29
  187.0 0.7 multiply_add_fusion
  (36 shorter events, 0.1 us)
Async XLA Ops:
  0.6 7.0 %copy-start = (f32[64,8192]{1,0:T(8,128)S(1)}, f32[64,8192]{1,0:T(8,128)}, u32[]{:S(2)}) copy-start(f32[64,8192]{1,0:T(8,128)} %amp_ref.3) | copy-start | bytes 6291460
  0.6 47.7 %all-to-all-start = ((f32[8,64,1024]{2,1,0:T(8,128)}), f32[8,64,1024]{2,1,0:T(8,128)}, u32[]{:S(2)}, u32[]{:S(2)}) async-start(f32[8,64,1024]{2,1,0:T(8,128)} %bitcast.23), calls=%async_computation | async-start | bytes 4194304 | tf_op jit(solution)/shard_map/all_to_all | solution.py:414
  7.6 14.7 %copy-start.18 = (s32[2048,1]{0,1:T(1,128)S(1)}, s32[2048,1]{0,1:T(1,128)}, u32[]{:S(2)}) copy-start(s32[2048,1]{0,1:T(1,128)} %param.20) | copy-start | bytes 24580
  8.6 36.3 %collective-permute-start = (f32[24,8192]{1,0:T(8,128)}, f32[24,8192]{1,0:T(8,128)S(1)}, u32[]{:S(2)}, u32[]{:S(2)}) collective-permute-start(f32[24,8192]{1,0:T(8,128)} %slice.21), channel_id=1, source_target_pairs={{0,127},{1,126},{2,125},{3,124},{4,123},{5,122},{6,121},{7,120},{8... | collective-permute-start | bytes 2359304 | tf_op jit(solution)/shard_map/ppermute | solution.py:416
  16.1 28.8 %collective-permute-start.1 = (f32[8,8192]{1,0:T(8,128)S(1)}, f32[8,8192]{1,0:T(8,128)}, u32[]{:S(2)}, u32[]{:S(2)}) collective-permute-start(f32[8,8192]{1,0:T(8,128)S(1)} %slice.22), channel_id=1, source_target_pairs={{0,120},{8,112},{16,104},{24,96},{32,88},{40,80},{48,72},{56,64},{... | collective-permute-start | bytes 786440 | tf_op jit(solution)/shard_map/ppermute | solution.py:417
  16.2 28.6 %collective-permute-start.2 = (f32[1,8192]{1,0:T(1,128)S(1)}, f32[1,8192]{1,0:T(1,128)S(1)}, u32[]{:S(2)}, u32[]{:S(2)}) collective-permute-start(f32[1,8192]{1,0:T(1,128)S(1)} %slice.23), channel_id=1, source_target_pairs={{0,64},{1,127},{2,126},{3,125},{4,124},{5,123},{6,122},{7,121},{8,... | collective-permute-start | bytes 98312 | tf_op jit(solution)/shard_map/ppermute | solution.py:418
  24.5 2.6 %copy-start.21 = (s32[4,8]{1,0:T(4,128)S(1)}, s32[4,8]{1,0:T(4,128)}, u32[]{:S(2)}) copy-start(s32[4,8]{1,0:T(4,128)} %param.19) | copy-start | bytes 388
  25.8 3.5 %copy-start.13 = (bf16[2,64,128]{2,1,0:T(8,128)(2,1)S(1)}, bf16[2,64,128]{2,1,0:T(8,128)(2,1)}, u32[]{:S(2)}) copy-start(bf16[2,64,128]{2,1,0:T(8,128)(2,1)} %constant.43.clone.small_ref) | copy-start | bytes 98308
  25.8 19.9 %copy-start.5 = (bf16[128,384]{1,0:T(8,128)(2,1)S(1)}, bf16[128,384]{1,0:T(8,128)(2,1)}, u32[]{:S(2)}) copy-start(bf16[128,384]{1,0:T(8,128)(2,1)} %constant.44.clone.flip_ref) | copy-start | bytes 294916
  29.3 19.1 %copy-start.11 = (bf16[512,128]{1,0:T(8,128)(2,1)S(1)}, bf16[512,128]{1,0:T(8,128)(2,1)}, u32[]{:S(2)}) copy-start(bf16[512,128]{1,0:T(8,128)(2,1)} %constant.47.clone.last_ref) | copy-start | bytes 393220
  29.3 19.1 %copy-start.12 = (f32[33,256]{1,0:T(8,128)S(1)}, f32[33,256]{1,0:T(8,128)}, u32[]{:S(2)}) copy-start(f32[33,256]{1,0:T(8,128)} %constant.45.clone.tw_ref) | copy-start | bytes 101380
  30.5 1.0 copy-start.14
  31.5 1.0 copy-start.16
  44.8 0.9 copy-start.3
  45.7 10.6 %collective-permute-start.3 = (f32[8,8192]{1,0:T(8,128)}, f32[8,8192]{1,0:T(8,128)S(1)}, u32[]{:S(2)}, u32[]{:S(2)}) collective-permute-start(f32[8,8192]{1,0:T(8,128)} %collective-permute-done.1), channel_id=1, source_target_pairs={{0,7},{1,6},{2,5},{3,4},{4,3},{5,2},{6,1},{7,0},{8,15},{9,14},{10,... | collective-permute-start | bytes 786440 | tf_op jit(solution)/shard_map/ppermute | solution.py:442
  45.7 1.1 copy-start.4
  48.4 1.0 copy-start.8
  49.3 1.2 copy-start.17
  56.9 39.7 %copy-start.6 = (bf16[2048,256]{1,0:T(8,128)(2,1)S(1)}, bf16[2048,256]{1,0:T(8,128)(2,1)}, u32[]{:S(2)}) copy-start(bf16[2048,256]{1,0:T(8,128)(2,1)} %constant.49.clone.table_ref) | copy-start | bytes 3145732
  57.0 39.7 %copy-start.10 = (f32[128,256]{1,0:T(8,128)S(1)}, f32[128,256]{1,0:T(8,128)}, u32[]{:S(2)}) copy-start(f32[128,256]{1,0:T(8,128)} %constant.48.clone.tw_ref) | copy-start | bytes 393220
  102.2 34.6 %copy-start.7 = (bf16[256,512]{1,0:T(8,128)(2,1)S(1)}, bf16[256,512]{1,0:T(8,128)(2,1)}, u32[]{:S(2)}) copy-start(bf16[256,512]{1,0:T(8,128)(2,1)} %constant.50.clone.whole_ref) | copy-start | bytes 786436
  102.3 34.6 %copy-start.9 = (bf16[256,256]{1,0:T(8,128)(2,1)S(1)}, bf16[256,256]{1,0:T(8,128)(2,1)}, u32[]{:S(2)}) copy-start(bf16[256,256]{1,0:T(8,128)(2,1)} %constant.51.clone.last_ref) | copy-start | bytes 393220
  102.3 34.6 %copy-start.15 = (bf16[1024,512]{1,0:T(8,128)(2,1)S(1)}, bf16[1024,512]{1,0:T(8,128)(2,1)}, u32[]{:S(2)}) copy-start(bf16[1024,512]{1,0:T(8,128)(2,1)} %copy-done.14) | copy-start | bytes 3145732
  140.6 30.3 %copy-start.1 = (f32[512,1024]{1,0:T(8,128)S(1)}, f32[512,1024]{1,0:T(8,128)}, u32[]{:S(2)}) copy-start(f32[512,1024]{1,0:T(8,128)} %param.18) | copy-start | bytes 6291460
  170.9 6.5 %copy-start.19 = (f32[288,32]{0,1:T(8,128)S(1)}, f32[288,32]{0,1:T(8,128)}, u32[]{:S(2)}) copy-start(f32[288,32]{0,1:T(8,128)} %param.22) | copy-start | bytes 110596
  173.0 13.9 %all-to-all-start.4 = ((f32[128,1,128]{2,1,0:T(1,128)}), f32[128,1,128]{2,1,0:T(1,128)S(1)}, u32[]{:S(2)}, u32[]{:S(2)}) async-start(f32[128,1,128]{2,1,0:T(1,128)} %bitcast.11), calls=%async_computation.4 | async-start | bytes 131072 | tf_op jit(solution)/shard_map/all_to_all | solution.py:483
  177.5 1.6 copy-start.2
  179.1 8.0 %copy-start.20 = (f32[288,32]{0,1:T(8,128)S(1)}, f32[288,32]{0,1:T(8,128)}, u32[]{:S(2)}) copy-start(f32[288,32]{0,1:T(8,128)} %param.21) | copy-start | bytes 110596

commit v5 on v4

--- a/solution.py
+++ b/solution.py
@@ -13,7 +13,7 @@
 CAP = 32
 N = 8192
 DEV = 128
-FAR = 8
+FAR = 16
 BOTH = ("row", "col")
 
 bump_height = 64.0
@@ -425,22 +425,23 @@
     device = d.astype(jnp.int32).reshape(1)
     scalar, vector = pl.BlockSpec(memory_space=pltpu.SMEM), pl.BlockSpec(memory_space=pltpu.VMEM)
 
-    def weigh(body, device, blocks, *args):
+    def weigh(body, device, blocks, rows, *args):
         return pl.pallas_call(
             body,
             out_shape=jax.ShapeDtypeStruct((blocks, 128, 128), F32),
-            in_specs=[scalar] + [vector] * len(args),
+            grid=(1,),
+            in_specs=[scalar, pl.BlockSpec((rows, N), lambda i: (0, 0))] + [vector] * (len(args) - 1),
             compiler_params=pltpu.CompilerParams(vmem_limit_bytes=24 << 20),
             cost_estimate=pl.CostEstimate(flops=300_000_000, bytes_accessed=3_000_000, transcendentals=0),
         )(device, *args)
 
     flip = reversal()
-    near, far, partner, tile_slot, forward_wide, inverse_wide = lax.optimization_barrier(
-        (near, far, partner, tile_slot, forward_wide, inverse_wide)
-    )
-    near_weight = weigh(near_weights, device, 17 - FAR // 2, amplitude, near, partner.reshape(64, 128), flip)
+    near, far = lax.optimization_barrier((near, far))
+    near_weight = weigh(near_weights, device, 17 - FAR // 2, 40, amplitude, near, partner.reshape(64, 128), flip)
     far = lax.ppermute(far, "col", [(i, 7 - i) for i in range(8)])
-    slab, near_weight = lax.optimization_barrier((slab, near_weight))
+    slab, near_weight, tile_slot, forward_wide, inverse_wide = lax.optimization_barrier(
+        (slab, near_weight, tile_slot, forward_wide, inverse_wide)
+    )
     tw_row = row_twiddle()
     whole, forward_last, inverse_last = row_tables()
     spec = pl.pallas_call(
@@ -457,7 +458,7 @@
         cost_estimate=pl.CostEstimate(flops=2_000_000_000, bytes_accessed=6_000_000, transcendentals=0),
     )(slab, forward_wide, tw_row, stacked(whole), stacked(forward_last))
     spec, device = lax.optimization_barrier((spec, device))
-    far_weight = weigh(far_weights, device, FAR // 2, amplitude, far, flip)
+    far_weight = weigh(far_weights, device, FAR // 2, FAR + 8, amplitude, far, flip)
     spec, far_weight = lax.optimization_barrier((spec, far_weight))
     spec = lax.all_to_all(spec, BOTH, 0, 0, tiled=True)
     long, short = col_tables(-1.0)

time: 188 us -> 188 us (level)
  waiting for transfers between devices: 19.4 us -> 24 us
  blocking collectives: 105 us -> 102 us
  local copies, waits for them, and re-layouts: 11.1 us -> 9.2 us
    ppermute x1, waiting for transfers between devices: 12.4 us -> 0.01 us  [shards(): lax.ppermute(amplitude[0:1], BOTH, [(0, 64)] + [(i, DEV - i) for i in ran...]
    ppermute x1, waiting for transfers between devices: 0.01 us -> 10.7 us  [shards(): lax.ppermute(amplitude[64 - FAR:64], 'row', [(i, 15 - i) for i in range(1...]
    ppermute x1, waiting for transfers between devices: 0.83 us -> 4.41 us  [shards(): far = lax.ppermute(far, 'col', [(i, 7 - i) for i in range(8)])]
    all_to_all x1, blocking collectives: 39.7 us -> 36.7 us  [shards(): spec = lax.all_to_all(spec, BOTH, 0, 0, tiled=True)]
    ppermute x1, waiting for transfers between devices: 0.01 us -> 2.67 us  [shards(): lax.ppermute(amplitude[32:64 - FAR], BOTH, [(i, DEV - 1 - i) for i in ran...]
    unnamed x44 -> x42, local copies, waits for them, and re-layouts: 7.82 us -> 6.75 us
  transfers between devices with their start and end apart: 6 -> 6, of which waited for: 3 -> 4; matrix products, arithmetic and copies ran while one was open for 4% -> 3% of each run, Pallas kernels for 5% -> 5%
where the time goes in v5:
time: 188 us; the launch traced here: 187 us
  blocking collectives  102 us (54%)
  starting transfers between devices  25 us (13%)
  waiting for transfers between devices  24 us (13%)
  Pallas kernels  22.2 us (12%)
  local copies, waits for them, and re-layouts  9.2 us (5%)
  other arithmetic  4.59 us (2%)
    all_to_all x1, blocking collectives, shards(): spec = lax.all_to_all(spec, BOTH, 0, 0, tiled=True)  36.7 us
    all_to_all x1, blocking collectives, shards(): shaped = lax.all_to_all(shaped, BOTH, 0, 0, tiled=True)  34.6 us
    all_to_all x1, blocking collectives, shards(): filtered = lax.all_to_all(field, 'col', 0, 0, tiled=True)  30.3 us
    ppermute x1, waiting for transfers between devices, shards(): lax.ppermute(amplitude[64 - FAR:64], 'row', [(i, 15 - i) for i in range(1...  10.7 us
    ppermute x1, starting transfers between devices, shards(): lax.ppermute(amplitude[32:64 - FAR], BOTH, [(i, DEV - 1 - i) for i in ran...  7.49 us
    all_to_all x1, starting transfers between devices, shards(): lax.all_to_all(white_noise.reshape(8, 64, 1024), 'col', 0, 0, tiled=True)  6.96 us
    unnamed x42, local copies, waits for them, and re-layouts  6.75 us
    all_to_all x1, waiting for transfers between devices, shards(): received = lax.all_to_all(sums.reshape(DEV, 1, 128), BOTH, 0, 0, tiled=True)  6.18 us
  transfers between devices with their start and end apart: 6, of which 4 were waited for; matrix products, arithmetic and copies ran while one was open for 3% of the time, Pallas kernels for 5%

profile of v5, /device:TPU:1, one launch (start us, length us, event | category | flops | bytes accessed | tf_op | source)
XLA Modules:
  0.0 187.4 jit_solution(16592788836384747685)
XLA Ops:
  0.6 7.0 %all-to-all-start = ((f32[8,64,1024]{2,1,0:T(8,128)}), f32[8,64,1024]{2,1,0:T(8,128)}, u32[]{:S(2)}, u32[]{:S(2)}) async-start(f32[8,64,1024]{2,1,0:T(8,128)} %bitcast.23), calls=%async_computation | async-start | bytes 4194304 | tf_op jit(solution)/shard_map/all_to_all | solution.py:414
  7.6 0.9 fusion.4
  8.5 7.5 %collective-permute-start = (f32[16,8192]{1,0:T(8,128)}, f32[16,8192]{1,0:T(8,128)S(1)}, u32[]{:S(2)}, u32[]{:S(2)}) collective-permute-start(f32[16,8192]{1,0:T(8,128)} %get-tuple-element.29), channel_id=1, source_target_pairs={{0,127},{1,126},{2,125},{3,124},{4,123},{5,122},{6,121},{7,120},{8... | collective-permute-start | bytes 1572872 | tf_op jit(solution)/shard_map/ppermute | solution.py:416
  16.0 0.0 collective-permute-start.1
  16.0 6.1 %collective-permute-start.2 = (f32[1,8192]{1,0:T(1,128)S(1)}, f32[1,8192]{1,0:T(1,128)S(1)}, u32[]{:S(2)}, u32[]{:S(2)}) collective-permute-start(f32[1,8192]{1,0:T(1,128)S(1)} %slice.23), channel_id=1, source_target_pairs={{0,64},{1,127},{2,126},{3,125},{4,124},{5,123},{6,122},{7,121},{8,... | collective-permute-start | bytes 98312 | tf_op jit(solution)/shard_map/ppermute | solution.py:418
  22.2 0.1 copy.24
  22.3 0.3 fusion.1
  22.6 0.0 copy-start.16
  22.6 1.0 copy-done.16
  23.6 1.3 add_add_fusion
  24.9 0.0 copy-start.11
  25.0 0.0 copy-start.3
  25.0 1.3 copy.25
  26.3 0.1 eq.38
  26.3 1.9 fusion
  28.2 0.0 copy-start.9
  28.2 0.0 copy-start.10
  28.2 2.7 %collective-permute-done.near_ref = f32[16,8192]{1,0:T(8,128)S(1)} collective-permute-done((f32[16,8192]{1,0:T(8,128)}, f32[16,8192]{1,0:T(8,128)S(1)}, u32[]{:S(2)}, u32[]{:S(2)}) %collective-permute-start) | collective-permute-done | bytes 524320 | tf_op jit(solution)/shard_map/ppermute | solution.py:416
  30.9 10.7 %collective-permute-done.1 = f32[16,8192]{1,0:T(8,128)} collective-permute-done((f32[16,8192]{1,0:T(8,128)S(1)}, f32[16,8192]{1,0:T(8,128)}, u32[]{:S(2)}, u32[]{:S(2)}) %collective-permute-start.1) | collective-permute-done | bytes 524320 | tf_op jit(solution)/shard_map/ppermute | solution.py:417
  41.6 0.2 select_reduce_fusion.slot_ref
  41.8 1.2 shard_map.168
  43.1 1.0 copy-done.12
  44.0 1.0 copy-done.14
  45.0 1.1 shard_map.167.near_ref
  46.1 0.0 copy-start.6
  46.1 0.9 copy-done.6
  47.1 1.2 copy-done.15
  48.3 4.9 %shard_map.169 = f32[128,32,128]{2,1,0:T(8,128)S(1)} custom-call(f32[8,64,1024]{2,1,0:T(8,128)} %all-to-all-done.x_hbm, bf16[1024,512]{1,0:T(8,128)(2,1)S(1)} %copy-done.15, f32[33,256]{1,0:T(8,128)S(1)} %copy-done.10, bf16[512,256]{1,0:T(8,128)(2,1)S(1)} %copy-done.6, bf16[512,128]{1,0:T(8,128)(2,1)S(1)} %copy-done.9), custom_call_target="tpu_custom_call" | custom-call | flops 2000000000 | bytes 6000000 | tf_op jit(solution)/shard_map/pallas_call | solution.py:447
  53.2 4.4 %collective-permute-done.3.far_ref = f32[16,8192]{1,0:T(8,128)} collective-permute-done((f32[16,8192]{1,0:T(8,128)}, f32[16,8192]{1,0:T(8,128)}, u32[]{:S(2)}, u32[]{:S(2)}) %collective-permute-start.3) | collective-permute-done | bytes 524320 | tf_op jit(solution)/shard_map/ppermute | solution.py:441
  57.6 2.1 %shard_map.170.far_ref = f32[8,128,128]{2,1,0:T(8,128)S(1)} custom-call(s32[1]{0:T(128)} %bitcast.1.d_ref, f32[64,8192]{1,0:T(8,128)S(1)} %copy-done, f32[16,8192]{1,0:T(8,128)} %collective-permute-done.3.far_ref, bf16[128,384]{1,0:T(8,128)(2,1)S(1)} %copy-done.3), custom_call_target="tpu_custom_call" | custom-call | flops 300000000 | bytes 3000000 | tf_op jit(solution)/shard_map/pallas_call | solution.py:429
  59.7 0.0 copy-start.4
  59.7 0.0 copy-start.8
  59.7 36.7 %all_to_all.25.x_ref = f32[128,32,128]{2,1,0:T(8,128)S(1)} all-to-all(f32[128,32,128]{2,1,0:T(8,128)S(1)} %shard_map.169), channel_id=1, replica_groups=mesh['row'=16,'col'=8] {'row','col'}, dimensions={0} | all-to-all | bytes 4194304 | tf_op jit(solution)/shard_map/all_to_all | solution.py:463
  96.4 5.6 %shard_map.171 = f32[128,32,128]{2,1,0:T(8,128)S(1)} custom-call(f32[128,32,128]{2,1,0:T(8,128)S(1)} %all_to_all.25.x_ref, f32[8,128,128]{2,1,0:T(8,128)S(1)} %shard_map.170.far_ref, f32[9,128,128]{2,1,0:T(8,128)S(1)} %shard_map.167.near_ref, f32[128,256]{1,0:T(8,128)S(1)} %copy-done.8, bf16[2048,256]{1,0:T(8,128)(2,1)S(1)} %copy-done.4), custom_call_target="tpu_custom_call" | custom-call | flops 2000000000 | bytes 6000000 | tf_op jit(solution)/shard_map/pallas_call | solution.py:467
  102.0 0.0 copy-start.5
  102.0 0.0 copy-start.7
  102.0 34.6 %all_to_all.26.x_ref = f32[128,32,128]{2,1,0:T(8,128)S(1)} all-to-all(f32[128,32,128]{2,1,0:T(8,128)S(1)} %shard_map.171), channel_id=1, replica_groups=mesh['row'=16,'col'=8] {'row','col'}, dimensions={0} | all-to-all | bytes 4194304 | tf_op jit(solution)/shard_map/all_to_all | solution.py:468
  136.6 3.7 %shard_map.172 = f32[8,64,1024]{2,1,0:T(8,128)S(1)} custom-call(f32[128,32,128]{2,1,0:T(8,128)S(1)} %all_to_all.26.x_ref, bf16[1024,512]{1,0:T(8,128)(2,1)S(1)} %copy-done.13, f32[33,256]{1,0:T(8,128)S(1)} %copy-done.10, bf16[256,512]{1,0:T(8,128)(2,1)S(1)} %copy-done.5, bf16[256,256]{1,0:T(8,128)(2,1)S(1)} %copy-done.7), custom_call_target="tpu_custom_call" | custom-call | flops 2000000000 | bytes 6000000 | tf_op jit(solution)/shard_map/pallas_call | solution.py:470
  140.2 0.0 copy-start.1
  140.3 30.3 %all_to_all.27.field_ref = f32[8,64,1024]{2,1,0:T(8,128)S(1)} all-to-all(f32[8,64,1024]{2,1,0:T(8,128)S(1)} %shard_map.172), channel_id=1, replica_groups=mesh['row'=16,'col'=8] {'col'}, dimensions={0} | all-to-all | bytes 4194304 | tf_op jit(solution)/shard_map/all_to_all | solution.py:473
  170.6 2.1 %shard_map.174 = f32[128,128]{1,0:T(8,128)} custom-call(s32[32]{0:T(128)S(1)} %select_reduce_fusion.slot_ref, f32[8,64,1024]{2,1,0:T(8,128)S(1)} %all_to_all.27.field_ref, f32[8,64,1024]{2,1,0:T(8,128)S(1)} %bitcast.19), custom_call_target="tpu_custom_call" | custom-call | flops 5000000 | bytes 4000000 | tf_op jit(solution)/shard_map/pallas_call | solution.py:475
  172.7 4.4 %all-to-all-start.4 = ((f32[128,1,128]{2,1,0:T(1,128)}), f32[128,1,128]{2,1,0:T(1,128)S(1)}, u32[]{:S(2)}, u32[]{:S(2)}) async-start(f32[128,1,128]{2,1,0:T(1,128)} %bitcast.11), calls=%async_computation.4 | async-start | bytes 131072 | tf_op jit(solution)/shard_map/all_to_all | solution.py:484
  177.1 0.1 slice.26
  177.2 1.6 copy-done.2
  178.8 1.6 shard_map.173
  180.4 6.2 %all-to-all-done.4 = f32[128,1,128]{2,1,0:T(1,128)S(1)} async-done(((f32[128,1,128]{2,1,0:T(1,128)}), f32[128,1,128]{2,1,0:T(1,128)S(1)}, u32[]{:S(2)}, u32[]{:S(2)}) %all-to-all-start.4) | async-done | bytes 65568 | tf_op jit(solution)/shard_map/all_to_all | solution.py:484
  186.6 0.2 reduce_sum.29
  186.7 0.7 multiply_add_fusion
  (33 shorter events, 0.1 us)
Async XLA Ops:
  0.6 7.0 %copy-start = (f32[64,8192]{1,0:T(8,128)S(1)}, f32[64,8192]{1,0:T(8,128)}, u32[]{:S(2)}) copy-start(f32[64,8192]{1,0:T(8,128)} %amp_ref.3) | copy-start | bytes 6291460
  0.6 45.4 %all-to-all-start = ((f32[8,64,1024]{2,1,0:T(8,128)}), f32[8,64,1024]{2,1,0:T(8,128)}, u32[]{:S(2)}, u32[]{:S(2)}) async-start(f32[8,64,1024]{2,1,0:T(8,128)} %bitcast.23), calls=%async_computation | async-start | bytes 4194304 | tf_op jit(solution)/shard_map/all_to_all | solution.py:414
  7.6 14.6 %copy-start.17 = (s32[2048,1]{0,1:T(1,128)S(1)}, s32[2048,1]{0,1:T(1,128)}, u32[]{:S(2)}) copy-start(s32[2048,1]{0,1:T(1,128)} %param.20) | copy-start | bytes 24580
  8.5 22.4 %collective-permute-start = (f32[16,8192]{1,0:T(8,128)}, f32[16,8192]{1,0:T(8,128)S(1)}, u32[]{:S(2)}, u32[]{:S(2)}) collective-permute-start(f32[16,8192]{1,0:T(8,128)} %get-tuple-element.29), channel_id=1, source_target_pairs={{0,127},{1,126},{2,125},{3,124},{4,123},{5,122},{6,121},{7,120},{8... | collective-permute-start | bytes 1572872 | tf_op jit(solution)/shard_map/ppermute | solution.py:416
  16.0 25.6 %collective-permute-start.1 = (f32[16,8192]{1,0:T(8,128)S(1)}, f32[16,8192]{1,0:T(8,128)}, u32[]{:S(2)}, u32[]{:S(2)}) collective-permute-start(f32[16,8192]{1,0:T(8,128)S(1)} %get-tuple-element.28), channel_id=1, source_target_pairs={{0,120},{8,112},{16,104},{24,96},{32,88},{40,80},{48,72},{56,64},{... | collective-permute-start | bytes 1572872 | tf_op jit(solution)/shard_map/ppermute | solution.py:417
  16.0 29.0 %collective-permute-start.2 = (f32[1,8192]{1,0:T(1,128)S(1)}, f32[1,8192]{1,0:T(1,128)S(1)}, u32[]{:S(2)}, u32[]{:S(2)}) collective-permute-start(f32[1,8192]{1,0:T(1,128)S(1)} %slice.23), channel_id=1, source_target_pairs={{0,64},{1,127},{2,126},{3,125},{4,124},{5,123},{6,122},{7,121},{8,... | collective-permute-start | bytes 98312 | tf_op jit(solution)/shard_map/ppermute | solution.py:418
  22.6 1.0 copy-start.16
  23.6 2.6 %copy-start.20 = (s32[4,8]{1,0:T(4,128)S(1)}, s32[4,8]{1,0:T(4,128)}, u32[]{:S(2)}) copy-start(s32[4,8]{1,0:T(4,128)} %param.19) | copy-start | bytes 388
  24.9 16.9 %copy-start.11 = (bf16[2,64,128]{2,1,0:T(8,128)(2,1)S(1)}, bf16[2,64,128]{2,1,0:T(8,128)(2,1)}, u32[]{:S(2)}) copy-start(bf16[2,64,128]{2,1,0:T(8,128)(2,1)} %constant.43.clone.small_ref) | copy-start | bytes 98308
  25.0 20.0 %copy-start.3 = (bf16[128,384]{1,0:T(8,128)(2,1)S(1)}, bf16[128,384]{1,0:T(8,128)(2,1)}, u32[]{:S(2)}) copy-start(bf16[128,384]{1,0:T(8,128)(2,1)} %constant.44.clone.flip_ref) | copy-start | bytes 294916
  28.2 17.9 %copy-start.9 = (bf16[512,128]{1,0:T(8,128)(2,1)S(1)}, bf16[512,128]{1,0:T(8,128)(2,1)}, u32[]{:S(2)}) copy-start(bf16[512,128]{1,0:T(8,128)(2,1)} %constant.47.clone.last_ref) | copy-start | bytes 393220
  28.2 17.9 %copy-start.10 = (f32[33,256]{1,0:T(8,128)S(1)}, f32[33,256]{1,0:T(8,128)}, u32[]{:S(2)}) copy-start(f32[33,256]{1,0:T(8,128)} %constant.45.clone.tw_ref) | copy-start | bytes 101380
  41.6 16.0 %collective-permute-start.3 = (f32[16,8192]{1,0:T(8,128)}, f32[16,8192]{1,0:T(8,128)}, u32[]{:S(2)}, u32[]{:S(2)}) collective-permute-start(f32[16,8192]{1,0:T(8,128)} %collective-permute-done.1), channel_id=1, source_target_pairs={{0,7},{1,6},{2,5},{3,4},{4,3},{5,2},{6,1},{7,0},{8,15},{9,14},{10,... | collective-permute-start | bytes 1572872 | tf_op jit(solution)/shard_map/ppermute | solution.py:441
  43.1 1.0 copy-start.12
  44.0 1.0 copy-start.14
  46.1 1.0 copy-start.6
  47.1 1.2 copy-start.15
  59.7 36.7 %copy-start.4 = (bf16[2048,256]{1,0:T(8,128)(2,1)S(1)}, bf16[2048,256]{1,0:T(8,128)(2,1)}, u32[]{:S(2)}) copy-start(bf16[2048,256]{1,0:T(8,128)(2,1)} %constant.49.clone.table_ref) | copy-start | bytes 3145732
  59.7 36.7 %copy-start.8 = (f32[128,256]{1,0:T(8,128)S(1)}, f32[128,256]{1,0:T(8,128)}, u32[]{:S(2)}) copy-start(f32[128,256]{1,0:T(8,128)} %constant.48.clone.tw_ref) | copy-start | bytes 393220
  102.0 34.6 %copy-start.5 = (bf16[256,512]{1,0:T(8,128)(2,1)S(1)}, bf16[256,512]{1,0:T(8,128)(2,1)}, u32[]{:S(2)}) copy-start(bf16[256,512]{1,0:T(8,128)(2,1)} %constant.50.clone.whole_ref) | copy-start | bytes 786436
  102.0 34.6 %copy-start.7 = (bf16[256,256]{1,0:T(8,128)(2,1)S(1)}, bf16[256,256]{1,0:T(8,128)(2,1)}, u32[]{:S(2)}) copy-start(bf16[256,256]{1,0:T(8,128)(2,1)} %constant.51.clone.last_ref) | copy-start | bytes 393220
  102.0 34.6 %copy-start.13 = (bf16[1024,512]{1,0:T(8,128)(2,1)S(1)}, bf16[1024,512]{1,0:T(8,128)(2,1)}, u32[]{:S(2)}) copy-start(bf16[1024,512]{1,0:T(8,128)(2,1)} %copy-done.12) | copy-start | bytes 3145732
  140.2 30.3 %copy-start.1 = (f32[512,1024]{1,0:T(8,128)S(1)}, f32[512,1024]{1,0:T(8,128)}, u32[]{:S(2)}) copy-start(f32[512,1024]{1,0:T(8,128)} %param.18) | copy-start | bytes 6291460
  170.6 6.5 %copy-start.18 = (f32[288,32]{0,1:T(8,128)S(1)}, f32[288,32]{0,1:T(8,128)}, u32[]{:S(2)}) copy-start(f32[288,32]{0,1:T(8,128)} %param.22) | copy-start | bytes 110596
  172.7 13.9 %all-to-all-start.4 = ((f32[128,1,128]{2,1,0:T(1,128)}), f32[128,1,128]{2,1,0:T(1,128)S(1)}, u32[]{:S(2)}, u32[]{:S(2)}) async-start(f32[128,1,128]{2,1,0:T(1,128)} %bitcast.11), calls=%async_computation.4 | async-start | bytes 131072 | tf_op jit(solution)/shard_map/all_to_all | solution.py:484
  177.2 1.6 copy-start.2
  178.8 8.0 %copy-start.19 = (f32[288,32]{0,1:T(8,128)S(1)}, f32[288,32]{0,1:T(8,128)}, u32[]{:S(2)}) copy-start(f32[288,32]{0,1:T(8,128)} %param.21) | copy-start | bytes 110596

commit v6 on v5

--- a/solution.py
+++ b/solution.py
@@ -13,7 +13,7 @@
 CAP = 32
 N = 8192
 DEV = 128
-FAR = 16
+FAR = 8
 BOTH = ("row", "col")
 
 bump_height = 64.0

time: 188 us -> 191 us (1.016)
  blocking collectives: 102 us -> 105 us
    ppermute x1, waiting for transfers between devices: 10.7 us -> 18.5 us  [shards(): lax.ppermute(amplitude[64 - FAR:64], 'row', [(i, 15 - i) for i in range(1...]
    ppermute x1, waiting for transfers between devices: 4.41 us -> 0.01 us  [shards(): far = lax.ppermute(far, 'col', [(i, 7 - i) for i in range(8)])]
    all_to_all x1, blocking collectives: 36.7 us -> 39.8 us  [shards(): spec = lax.all_to_all(spec, BOTH, 0, 0, tiled=True)]
    ppermute x1, waiting for transfers between devices: 2.67 us -> 0.01 us  [shards(): lax.ppermute(amplitude[32:64 - FAR], BOTH, [(i, DEV - 1 - i) for i in ran...]
    unnamed x42 -> x46, local copies, waits for them, and re-layouts: 6.75 us -> 8.78 us
  transfers between devices with their start and end apart: 6 -> 6, of which waited for: 4 -> 2; matrix products, arithmetic and copies ran while one was open for 3% -> 2% of each run, Pallas kernels for 5% -> 5%
where the time goes in v6:
time: 191 us; the launch traced here: 190 us
  blocking collectives  105 us (55%)
  starting transfers between devices  25 us (13%)
  waiting for transfers between devices  24.7 us (13%)
  Pallas kernels  21.2 us (11%)
  local copies, waits for them, and re-layouts  10.4 us (5%)
  other arithmetic  3.35 us (2%)
    all_to_all x1, blocking collectives, shards(): spec = lax.all_to_all(spec, BOTH, 0, 0, tiled=True)  39.8 us
    all_to_all x1, blocking collectives, shards(): shaped = lax.all_to_all(shaped, BOTH, 0, 0, tiled=True)  34.6 us
    all_to_all x1, blocking collectives, shards(): filtered = lax.all_to_all(field, 'col', 0, 0, tiled=True)  30.3 us
    ppermute x1, waiting for transfers between devices, shards(): lax.ppermute(amplitude[64 - FAR:64], 'row', [(i, 15 - i) for i in range(1...  18.5 us
    unnamed x46, local copies, waits for them, and re-layouts  8.78 us
    ppermute x1, starting transfers between devices, shards(): lax.ppermute(amplitude[32:64 - FAR], BOTH, [(i, DEV - 1 - i) for i in ran...  7.49 us
    all_to_all x1, starting transfers between devices, shards(): lax.all_to_all(white_noise.reshape(8, 64, 1024), 'col', 0, 0, tiled=True)  6.96 us
    all_to_all x1, waiting for transfers between devices, shards(): received = lax.all_to_all(sums.reshape(DEV, 1, 128), BOTH, 0, 0, tiled=True)  6.22 us
  transfers between devices with their start and end apart: 6, of which 2 were waited for; matrix products, arithmetic and copies ran while one was open for 2% of the time, Pallas kernels for 5%

profile of v6, /device:TPU:1, one launch (start us, length us, event | category | flops | bytes accessed | tf_op | source)
XLA Modules:
  0.0 190.3 jit_solution(13573478301048920053)
XLA Ops:
  0.6 7.0 %all-to-all-start = ((f32[8,64,1024]{2,1,0:T(8,128)}), f32[8,64,1024]{2,1,0:T(8,128)}, u32[]{:S(2)}, u32[]{:S(2)}) async-start(f32[8,64,1024]{2,1,0:T(8,128)} %bitcast.23), calls=%async_computation | async-start | bytes 4194304 | tf_op jit(solution)/shard_map/all_to_all | solution.py:414
  7.6 0.9 slice.21
  8.5 7.5 %collective-permute-start = (f32[24,8192]{1,0:T(8,128)}, f32[24,8192]{1,0:T(8,128)S(1)}, u32[]{:S(2)}, u32[]{:S(2)}) collective-permute-start(f32[24,8192]{1,0:T(8,128)} %slice.21), channel_id=1, source_target_pairs={{0,127},{1,126},{2,125},{3,124},{4,123},{5,122},{6,121},{7,120},{8... | collective-permute-start | bytes 2359304 | tf_op jit(solution)/shard_map/ppermute | solution.py:416
  16.1 0.1 collective-permute-start.1
  16.2 6.1 %collective-permute-start.2 = (f32[1,8192]{1,0:T(1,128)S(1)}, f32[1,8192]{1,0:T(1,128)S(1)}, u32[]{:S(2)}, u32[]{:S(2)}) collective-permute-start(f32[1,8192]{1,0:T(1,128)S(1)} %slice.23), channel_id=1, source_target_pairs={{0,64},{1,127},{2,126},{3,125},{4,124},{5,123},{6,122},{7,121},{8,... | collective-permute-start | bytes 98312 | tf_op jit(solution)/shard_map/ppermute | solution.py:418
  22.3 0.1 copy.24
  22.4 0.3 fusion.1
  22.8 0.0 copy-start.18
  22.8 1.0 copy-done.18
  23.8 1.3 add_add_fusion
  25.1 0.0 copy-start.22
  25.1 0.0 copy-start.13
  25.1 0.0 copy-start.5
  25.1 0.3 copy.25
  25.5 0.6 fusion
  26.1 0.1 eq.38
  26.2 18.5 %collective-permute-done.1 = f32[8,8192]{1,0:T(8,128)} collective-permute-done((f32[8,8192]{1,0:T(8,128)S(1)}, f32[8,8192]{1,0:T(8,128)}, u32[]{:S(2)}, u32[]{:S(2)}) %collective-permute-start.1) | collective-permute-done | bytes 262176 | tf_op jit(solution)/shard_map/ppermute | solution.py:417
  44.7 0.9 copy-done.3
  45.6 0.2 select_reduce_fusion.slot_ref
  45.8 0.0 copy-start.11
  45.8 0.0 copy-start.12
  45.9 1.2 shard_map.168
  47.1 1.0 copy-done.14
  48.0 1.0 copy-done.16
  49.0 1.1 copy-done.4
  50.2 1.4 shard_map.167.near_ref
  51.6 0.0 copy-start.8
  51.6 0.9 copy-done.8
  52.6 1.2 copy-done.17
  53.8 4.9 %shard_map.169 = f32[128,32,128]{2,1,0:T(8,128)S(1)} custom-call(f32[8,64,1024]{2,1,0:T(8,128)} %all-to-all-done.x_hbm, bf16[1024,512]{1,0:T(8,128)(2,1)S(1)} %copy-done.17, f32[33,256]{1,0:T(8,128)S(1)} %copy-done.12, bf16[512,256]{1,0:T(8,128)(2,1)S(1)} %copy-done.8, bf16[512,128]{1,0:T(8,128)(2,1)S(1)} %copy-done.11), custom_call_target="tpu_custom_call" | custom-call | flops 2000000000 | bytes 6000000 | tf_op jit(solution)/shard_map/pallas_call | solution.py:447
  58.7 0.6 shard_map.170.far_ref
  59.3 0.0 copy-start.6
  59.3 0.0 copy-start.10
  59.4 39.8 %all_to_all.25.x_ref = f32[128,32,128]{2,1,0:T(8,128)S(1)} all-to-all(f32[128,32,128]{2,1,0:T(8,128)S(1)} %shard_map.169), channel_id=1, replica_groups=mesh['row'=16,'col'=8] {'row','col'}, dimensions={0} | all-to-all | bytes 4194304 | tf_op jit(solution)/shard_map/all_to_all | solution.py:463
  99.1 5.6 %shard_map.171 = f32[128,32,128]{2,1,0:T(8,128)S(1)} custom-call(f32[128,32,128]{2,1,0:T(8,128)S(1)} %all_to_all.25.x_ref, f32[4,128,128]{2,1,0:T(8,128)S(1)} %shard_map.170.far_ref, f32[13,128,128]{2,1,0:T(8,128)S(1)} %shard_map.167.near_ref, f32[128,256]{1,0:T(8,128)S(1)} %copy-done.10, bf16[2048,256]{1,0:T(8,128)(2,1)S(1)} %copy-done.6), custom_call_target="tpu_custom_call" | custom-call | flops 2000000000 | bytes 6000000 | tf_op jit(solution)/shard_map/pallas_call | solution.py:467
  104.7 0.0 copy-start.7
  104.7 0.0 copy-start.9
  104.8 34.6 %all_to_all.26.x_ref = f32[128,32,128]{2,1,0:T(8,128)S(1)} all-to-all(f32[128,32,128]{2,1,0:T(8,128)S(1)} %shard_map.171), channel_id=1, replica_groups=mesh['row'=16,'col'=8] {'row','col'}, dimensions={0} | all-to-all | bytes 4194304 | tf_op jit(solution)/shard_map/all_to_all | solution.py:468
  139.3 3.8 %shard_map.172 = f32[8,64,1024]{2,1,0:T(8,128)S(1)} custom-call(f32[128,32,128]{2,1,0:T(8,128)S(1)} %all_to_all.26.x_ref, bf16[1024,512]{1,0:T(8,128)(2,1)S(1)} %copy-done.15, f32[33,256]{1,0:T(8,128)S(1)} %copy-done.12, bf16[256,512]{1,0:T(8,128)(2,1)S(1)} %copy-done.7, bf16[256,256]{1,0:T(8,128)(2,1)S(1)} %copy-done.9), custom_call_target="tpu_custom_call" | custom-call | flops 2000000000 | bytes 6000000 | tf_op jit(solution)/shard_map/pallas_call | solution.py:470
  143.1 30.3 %all_to_all.27.field_ref = f32[8,64,1024]{2,1,0:T(8,128)S(1)} all-to-all(f32[8,64,1024]{2,1,0:T(8,128)S(1)} %shard_map.172), channel_id=1, replica_groups=mesh['row'=16,'col'=8] {'col'}, dimensions={0} | all-to-all | bytes 4194304 | tf_op jit(solution)/shard_map/all_to_all | solution.py:473
  173.4 2.1 %shard_map.174 = f32[128,128]{1,0:T(8,128)} custom-call(s32[32]{0:T(128)S(1)} %select_reduce_fusion.slot_ref, f32[8,64,1024]{2,1,0:T(8,128)S(1)} %all_to_all.27.field_ref, f32[8,64,1024]{2,1,0:T(8,128)S(1)} %bitcast.19), custom_call_target="tpu_custom_call" | custom-call | flops 5000000 | bytes 4000000 | tf_op jit(solution)/shard_map/pallas_call | solution.py:475
  175.5 4.3 %all-to-all-start.4 = ((f32[128,1,128]{2,1,0:T(1,128)}), f32[128,1,128]{2,1,0:T(1,128)S(1)}, u32[]{:S(2)}, u32[]{:S(2)}) async-start(f32[128,1,128]{2,1,0:T(1,128)} %bitcast.11), calls=%async_computation.4 | async-start | bytes 131072 | tf_op jit(solution)/shard_map/all_to_all | solution.py:484
  179.9 0.1 slice.26
  180.0 1.6 copy-done.2
  181.6 1.6 shard_map.173
  183.2 6.2 %all-to-all-done.4 = f32[128,1,128]{2,1,0:T(1,128)S(1)} async-done(((f32[128,1,128]{2,1,0:T(1,128)}), f32[128,1,128]{2,1,0:T(1,128)S(1)}, u32[]{:S(2)}, u32[]{:S(2)}) %all-to-all-start.4) | async-done | bytes 65568 | tf_op jit(solution)/shard_map/all_to_all | solution.py:484
  189.4 0.2 reduce_sum.29
  189.6 0.7 multiply_add_fusion
  (38 shorter events, 0.2 us)
Async XLA Ops:
  0.6 7.0 %copy-start = (f32[64,8192]{1,0:T(8,128)S(1)}, f32[64,8192]{1,0:T(8,128)}, u32[]{:S(2)}) copy-start(f32[64,8192]{1,0:T(8,128)} %amp_ref.3) | copy-start | bytes 6291460
  0.6 51.0 %all-to-all-start = ((f32[8,64,1024]{2,1,0:T(8,128)}), f32[8,64,1024]{2,1,0:T(8,128)}, u32[]{:S(2)}, u32[]{:S(2)}) async-start(f32[8,64,1024]{2,1,0:T(8,128)} %bitcast.23), calls=%async_computation | async-start | bytes 4194304 | tf_op jit(solution)/shard_map/all_to_all | solution.py:414
  7.6 14.7 %copy-start.19 = (s32[2048,1]{0,1:T(1,128)S(1)}, s32[2048,1]{0,1:T(1,128)}, u32[]{:S(2)}) copy-start(s32[2048,1]{0,1:T(1,128)} %param.20) | copy-start | bytes 24580
  8.5 36.2 %collective-permute-start = (f32[24,8192]{1,0:T(8,128)}, f32[24,8192]{1,0:T(8,128)S(1)}, u32[]{:S(2)}, u32[]{:S(2)}) collective-permute-start(f32[24,8192]{1,0:T(8,128)} %slice.21), channel_id=1, source_target_pairs={{0,127},{1,126},{2,125},{3,124},{4,123},{5,122},{6,121},{7,120},{8... | collective-permute-start | bytes 2359304 | tf_op jit(solution)/shard_map/ppermute | solution.py:416
  16.1 28.7 %collective-permute-start.1 = (f32[8,8192]{1,0:T(8,128)S(1)}, f32[8,8192]{1,0:T(8,128)}, u32[]{:S(2)}, u32[]{:S(2)}) collective-permute-start(f32[8,8192]{1,0:T(8,128)S(1)} %slice.22), channel_id=1, source_target_pairs={{0,120},{8,112},{16,104},{24,96},{32,88},{40,80},{48,72},{56,64},{... | collective-permute-start | bytes 786440 | tf_op jit(solution)/shard_map/ppermute | solution.py:417
  16.2 32.8 %collective-permute-start.2 = (f32[1,8192]{1,0:T(1,128)S(1)}, f32[1,8192]{1,0:T(1,128)S(1)}, u32[]{:S(2)}, u32[]{:S(2)}) collective-permute-start(f32[1,8192]{1,0:T(1,128)S(1)} %slice.23), channel_id=1, source_target_pairs={{0,64},{1,127},{2,126},{3,125},{4,124},{5,123},{6,122},{7,121},{8,... | collective-permute-start | bytes 98312 | tf_op jit(solution)/shard_map/ppermute | solution.py:418
  22.8 1.0 copy-start.18
  25.1 1.0 copy-start.22
  25.1 20.7 %copy-start.13 = (bf16[2,64,128]{2,1,0:T(8,128)(2,1)S(1)}, bf16[2,64,128]{2,1,0:T(8,128)(2,1)}, u32[]{:S(2)}) copy-start(bf16[2,64,128]{2,1,0:T(8,128)(2,1)} %constant.43.clone.small_ref) | copy-start | bytes 98308
  25.1 23.9 %copy-start.5 = (bf16[128,384]{1,0:T(8,128)(2,1)S(1)}, bf16[128,384]{1,0:T(8,128)(2,1)}, u32[]{:S(2)}) copy-start(bf16[128,384]{1,0:T(8,128)(2,1)} %constant.44.clone.flip_ref) | copy-start | bytes 294916
  44.7 0.9 copy-start.3
  45.6 13.1 %collective-permute-start.3 = (f32[8,8192]{1,0:T(8,128)}, f32[8,8192]{1,0:T(8,128)S(1)}, u32[]{:S(2)}, u32[]{:S(2)}) collective-permute-start(f32[8,8192]{1,0:T(8,128)} %collective-permute-done.1), channel_id=1, source_target_pairs={{0,7},{1,6},{2,5},{3,4},{4,3},{5,2},{6,1},{7,0},{8,15},{9,14},{10,... | collective-permute-start | bytes 786440 | tf_op jit(solution)/shard_map/ppermute | solution.py:441
  45.8 5.8 %copy-start.11 = (bf16[512,128]{1,0:T(8,128)(2,1)S(1)}, bf16[512,128]{1,0:T(8,128)(2,1)}, u32[]{:S(2)}) copy-start(bf16[512,128]{1,0:T(8,128)(2,1)} %constant.47.clone.last_ref) | copy-start | bytes 393220
  45.8 5.8 %copy-start.12 = (f32[33,256]{1,0:T(8,128)S(1)}, f32[33,256]{1,0:T(8,128)}, u32[]{:S(2)}) copy-start(f32[33,256]{1,0:T(8,128)} %constant.45.clone.tw_ref) | copy-start | bytes 101380
  47.1 1.0 copy-start.14
  48.0 1.0 copy-start.16
  49.0 1.1 copy-start.4
  51.6 1.0 copy-start.8
  52.6 1.2 copy-start.17
  59.3 39.8 %copy-start.6 = (bf16[2048,256]{1,0:T(8,128)(2,1)S(1)}, bf16[2048,256]{1,0:T(8,128)(2,1)}, u32[]{:S(2)}) copy-start(bf16[2048,256]{1,0:T(8,128)(2,1)} %constant.49.clone.table_ref) | copy-start | bytes 3145732
  59.3 39.8 %copy-start.10 = (f32[128,256]{1,0:T(8,128)S(1)}, f32[128,256]{1,0:T(8,128)}, u32[]{:S(2)}) copy-start(f32[128,256]{1,0:T(8,128)} %constant.48.clone.tw_ref) | copy-start | bytes 393220
  104.7 34.6 %copy-start.7 = (bf16[256,512]{1,0:T(8,128)(2,1)S(1)}, bf16[256,512]{1,0:T(8,128)(2,1)}, u32[]{:S(2)}) copy-start(bf16[256,512]{1,0:T(8,128)(2,1)} %constant.50.clone.whole_ref) | copy-start | bytes 786436
  104.7 34.6 %copy-start.9 = (bf16[256,256]{1,0:T(8,128)(2,1)S(1)}, bf16[256,256]{1,0:T(8,128)(2,1)}, u32[]{:S(2)}) copy-start(bf16[256,256]{1,0:T(8,128)(2,1)} %constant.51.clone.last_ref) | copy-start | bytes 393220
  104.7 34.6 %copy-start.15 = (bf16[1024,512]{1,0:T(8,128)(2,1)S(1)}, bf16[1024,512]{1,0:T(8,128)(2,1)}, u32[]{:S(2)}) copy-start(bf16[1024,512]{1,0:T(8,128)(2,1)} %copy-done.14) | copy-start | bytes 3145732
  143.1 30.3 %copy-start.1 = (f32[512,1024]{1,0:T(8,128)S(1)}, f32[512,1024]{1,0:T(8,128)}, u32[]{:S(2)}) copy-start(f32[512,1024]{1,0:T(8,128)} %param.18) | copy-start | bytes 6291460
  173.4 6.5 %copy-start.20 = (f32[288,32]{0,1:T(8,128)S(1)}, f32[288,32]{0,1:T(8,128)}, u32[]{:S(2)}) copy-start(f32[288,32]{0,1:T(8,128)} %param.22) | copy-start | bytes 110596
  175.5 13.9 %all-to-all-start.4 = ((f32[128,1,128]{2,1,0:T(1,128)}), f32[128,1,128]{2,1,0:T(1,128)S(1)}, u32[]{:S(2)}, u32[]{:S(2)}) async-start(f32[128,1,128]{2,1,0:T(1,128)} %bitcast.11), calls=%async_computation.4 | async-start | bytes 131072 | tf_op jit(solution)/shard_map/all_to_all | solution.py:484
  180.0 1.6 copy-start.2
  181.6 8.0 %copy-start.21 = (f32[288,32]{0,1:T(8,128)S(1)}, f32[288,32]{0,1:T(8,128)}, u32[]{:S(2)}) copy-start(f32[288,32]{0,1:T(8,128)} %param.21) | copy-start | bytes 110596
